TPU v7x, 32 devices: a whole 2x2x4 slice. The times are simulated.
32 devices in a mesh: atoms: 8 (over z, y), space: 4 (over x, core).
Axes of the slice: x: 2, y: 2, z: 4, core: 2. Of those that a mesh axis runs over, the one named last changes fastest.
Arguments:
- block_store: bfloat16 [4, 32, 128, 128], P('space', 'atoms'), may hold values from -0.21875 to 0.21875
- block_source: int32 [8, 4, 36], P('atoms', 'space'), may hold values from 0 to 31, as said below
- chem_pot: float32 [1], replicated, may hold values from -0.6 to 0.6
- basis_values: bfloat16 [8, 4, 8, 128, 1024], P('atoms', 'space'), may hold values from -1.5 to 1.5
- core_density: float32 [8, 4, 1024], P('atoms', 'space'), may hold values from 0.5 to 4
- point_weights: float32 [8, 4, 1024], P('atoms', 'space'), may hold values from 0.2 to 0.8
- pair_dest: int32 [8, 4, 12], P('atoms', 'space'), may hold values from 0 to 3, as said below
- tile_pairs: int32 [8, 4, 2, 12], P('atoms', 'space'), may hold values from -1 to 7, as said below
Outputs:
- density: bfloat16 [8, 4, 768, 128], P('atoms', 'space')
- potential: float32 [8, 4, 1024], P('atoms', 'space')
- kohn_sham: float32 [8, 4, 768, 128], P('atoms', 'space')
Inputs may be any that keep to these rules, and one draw needn't show every extreme that they name: `block_source`: each device names at most 5 blocks whose number // 4 is the same; blocks may repeat. `pair_dest`: the two pairs of one density block go to different tiles; a device sends at most 3 pairs to one tile. `tile_pairs`: slots that receive no pair hold -1 in both entries; the others follow the pairs as stated.
All inputs are finite; a program needn't handle non-finite values.
Results may differ from a plain program's by a relative error of at most 0.0065.
Values may be sent and summed in bfloat16 or wider, within the bound.
No kernel may reach another device: no remote copies, remote signals or barrier semaphores. Data moves between devices by JAX's collectives and lax.ppermute only.
A program may use at most 64 MiB of HBM per device.

v0:
```python
import math

import jax
import jax.numpy as jnp
from jax import lax
from jax.sharding import PartitionSpec as P

KB = 6


slater_factor = math.pow(3.0 / math.pi, 1.0 / 3.0)
density_floor = 0.05


def earlier_count(labels):
    order = jnp.arange(labels.shape[0])
    earlier = (labels[None, :] == labels[:, None]) & (order[None, :] < order[:, None])
    return jnp.sum(earlier.astype(jnp.int32), axis=1)


def sign_density(blocks, chem):
    block_width = blocks.shape[-1]
    order_full = KB * block_width
    matrix = (
        blocks.reshape(KB, KB, block_width, block_width)
        .transpose(0, 2, 1, 3)
        .reshape(order_full, order_full)
    )
    widened = matrix.astype(jnp.float32)
    identity = jnp.eye(order_full, dtype=jnp.float32)
    shifted = 0.5 * (widened + widened.T) - chem * identity
    scaling = 2.0 * jnp.sqrt(jnp.sum(shifted * shifted) / order_full + 1e-06)
    start_x = (shifted / scaling).astype(jnp.bfloat16)
    square_one = jnp.dot(start_x, start_x, preferred_element_type=jnp.float32)
    factor_one = (1.5 * identity - 0.5 * square_one).astype(jnp.bfloat16)
    next_x = jnp.dot(start_x, factor_one, preferred_element_type=jnp.float32).astype(jnp.bfloat16)
    square_two = jnp.dot(next_x, next_x[:, :block_width], preferred_element_type=jnp.float32)
    factor_two = (1.5 * identity[:, :block_width] - 0.5 * square_two).astype(jnp.bfloat16)
    final_x = jnp.dot(next_x, factor_two, preferred_element_type=jnp.float32)
    return (0.5 * (identity[:, :block_width] - final_x)).astype(jnp.bfloat16)


def per_device(
    block_store,
    block_source,
    chem_pot,
    basis_values,
    core_density,
    point_weights,
    pair_dest,
    tile_pairs,
):
    stored = block_store[0]
    held_count = stored.shape[0]
    block_width = stored.shape[-1]
    source = block_source[0, 0]
    slot_count = source.shape[0]
    atom_devices = lax.axis_size("atoms")
    space_devices = lax.axis_size("space")
    capacity = (slot_count + atom_devices - 1) // atom_devices
    peer_index = source // held_count
    local_index = source % held_count
    arrival_rank = earlier_count(peer_index)
    slot_index = peer_index * capacity + arrival_rank
    wanted = jnp.full((atom_devices * capacity,), -1, jnp.int32).at[slot_index].set(local_index)
    requested = lax.all_to_all(
        wanted.reshape(atom_devices, capacity), "atoms", split_axis=0, concat_axis=0, tiled=True
    )
    flat_request = requested.reshape(-1)
    chosen = jnp.take(stored, jnp.clip(flat_request, 0, held_count - 1), axis=0)
    chosen = chosen * (flat_request >= 0).astype(jnp.bfloat16)[:, None, None]
    arrived = lax.all_to_all(
        chosen.reshape(atom_devices, capacity, block_width, block_width),
        "atoms",
        split_axis=0,
        concat_axis=0,
        tiled=True,
    )
    blocks = jnp.take(
        arrived.reshape(atom_devices * capacity, block_width, block_width), slot_index, axis=0
    )
    density = sign_density(blocks, chem_pot[0])
    destinations = pair_dest[0, 0]
    send_count = destinations.shape[0]
    tile_capacity = (send_count + space_devices - 1) // space_devices
    slot_total = space_devices * tile_capacity
    send_slot = destinations * tile_capacity + earlier_count(destinations)
    placed = (send_slot[None, :] == jnp.arange(slot_total)[:, None]).astype(jnp.bfloat16)
    owner_block = (jnp.arange(send_count)[:, None] // 2 == jnp.arange(KB)[None, :]).astype(
        jnp.bfloat16
    )
    routing = jnp.dot(placed, owner_block, preferred_element_type=jnp.float32).astype(jnp.bfloat16)
    column_blocks = density.reshape(KB, block_width, block_width)
    outgoing = jnp.einsum(
        "rk,kab->rab", routing, column_blocks, preferred_element_type=jnp.float32
    ).astype(jnp.bfloat16)
    incoming = lax.all_to_all(
        outgoing.reshape(space_devices, tile_capacity, block_width, block_width),
        "space",
        split_axis=0,
        concat_axis=0,
        tiled=True,
    )
    incoming = incoming.reshape(slot_total, block_width, block_width)
    row_pick = tile_pairs[0, 0, 0]
    col_pick = tile_pairs[0, 0, 1]
    tables = basis_values[0, 0]
    table_count = tables.shape[0]
    points = tables.shape[-1]

    def accumulate(total, items):
        pair_block, row_at, col_at = items
        left_basis = jnp.take(tables, jnp.clip(row_at, 0, table_count - 1), axis=0)
        right_basis = jnp.take(tables, jnp.clip(col_at, 0, table_count - 1), axis=0)
        product = jnp.dot(pair_block, right_basis, preferred_element_type=jnp.float32)
        term = jnp.sum(left_basis.astype(jnp.float32) * product, axis=0)
        return (total + (row_at >= 0).astype(jnp.float32) * term, None)

    valence, _ = lax.scan(
        accumulate, jnp.zeros((points,), jnp.float32), (incoming, row_pick, col_pick)
    )
    potential = -slater_factor * jnp.cbrt(jnp.maximum(core_density[0, 0] + valence, density_floor))
    scaled = point_weights[0, 0] * potential

    def project(unused, items):
        row_at, col_at = items
        left_basis = jnp.take(tables, jnp.clip(row_at, 0, table_count - 1), axis=0)
        right_basis = jnp.take(tables, jnp.clip(col_at, 0, table_count - 1), axis=0)
        weighted = (left_basis.astype(jnp.float32) * scaled[None, :]).astype(jnp.bfloat16)
        partial_value = lax.dot_general(
            weighted, right_basis, (((1,), (1,)), ((), ())), preferred_element_type=jnp.float32
        )
        return (unused, partial_value.astype(jnp.bfloat16))

    _, partials = lax.scan(project, jnp.zeros((), jnp.float32), (row_pick, col_pick))
    returned = lax.all_to_all(
        partials.reshape(space_devices, tile_capacity, block_width, block_width),
        "space",
        split_axis=0,
        concat_axis=0,
        tiled=True,
    )
    returned = returned.reshape(slot_total, block_width, block_width)
    kohn = jnp.einsum("rk,rab->kab", routing, returned, preferred_element_type=jnp.float32)
    kohn = kohn.reshape(KB * block_width, block_width)
    return (density[None, None], potential[None, None], kohn[None, None])


def solution(mesh):
    placed = (
        P("space", "atoms", None, None),
        P("atoms", "space", None),
        P(),
        P("atoms", "space", None, None, None),
        P("atoms", "space", None),
        P("atoms", "space", None),
        P("atoms", "space", None),
        P("atoms", "space", None, None),
    )
    return jax.shard_map(
        per_device,
        mesh=mesh,
        in_specs=placed,
        out_specs=(
            P("atoms", "space", None, None),
            P("atoms", "space", None),
            P("atoms", "space", None, None),
        ),
        check_vma=False,
    )
```

profile of v0, /device:TPU:0, one launch (start us, length us, event | category | flops | bytes accessed | tf_op | source)
XLA Modules:
  0.0 173.8 jit_solution(1931458254013255488)
XLA Ops:
  0.6 0.7 and_select_fusion.1
  1.5 0.7 fusion.52
  2.2 0.7 scatter_custom_fusion
  3.0 13.6 %all_to_all.24 = s32[8,1,5]{2,1,0:T(1,128)S(1)} all-to-all(s32[8,1,5]{2,1,0:T(1,128)S(1)} %bitcast.161), channel_id=1, replica_groups=mesh['atoms'=8,'space'=4] {'atoms'}, dimensions={0} | all-to-all | bytes 320 | tf_op jit(solution)/shard_map/all_to_all | solution.py:66
  16.7 0.8 gather_fusion
  17.5 1.3 select_multiply_fusion
  18.8 3.6 %all-to-all-start.1 = ((bf16[8,5,128,128]{3,2,1,0:T(8,128)(2,1)}), bf16[8,5,128,128]{3,2,1,0:T(8,128)(2,1)S(1)}, u32[]{:S(2)}, u32[]{:S(2)}) async-start(bf16[8,5,128,128]{3,2,1,0:T(8,128)(2,1)} %select_multiply_fusion), calls=%async_computation.1 | async-start | bytes 2621440 | tf_op jit(solution)/shard_map/all_to_all | solution.py:72
  23.0 0.7 reduce.3
  24.8 1.0 iota_compare_fusion
  25.8 26.9 %all-to-all-done.1 = bf16[8,5,128,128]{3,2,1,0:T(8,128)(2,1)S(1)} async-done(((bf16[8,5,128,128]{3,2,1,0:T(8,128)(2,1)}), bf16[8,5,128,128]{3,2,1,0:T(8,128)(2,1)S(1)}, u32[]{:S(2)}, u32[]{:S(2)}) %all-to-all-start.1) | async-done | bytes 1310752 | tf_op jit(solution)/shard_map/all_to_all | solution.py:72
  52.7 0.8 gather_fusion.1
  53.7 1.4 copy.34
  55.1 2.0 %copy.48 = f32[96,8,6,128]{3,1,2,0:T(8,128)} copy(f32[96,8,6,128]{3,2,1,0:T(8,128)S(1)} %bitcast.145) | data formatting | bytes 4718592
  57.1 3.0 %copy.35 = f32[768,768]{0,1:T(8,128)} copy(f32[768,768]{1,0:T(8,128)} %bitcast.147) | data formatting | bytes 4718592 | tf_op jit(solution)/shard_map/convert_element_type | solution.py:29
  60.1 3.0 %multiply_reduce_fusion = f32[]{:T(128)} fusion(f32[]{:T(128)} %bitcast.142, f32[768,768]{0,1:T(8,128)} %copy.35, f32[96,8,6,128]{3,2,1,0:T(8,128)S(1)} %bitcast.146), kind=kLoop, calls=%fused_computation.38 | loop fusion | flops 4128767 | bytes 4718600 | tf_op jit(solution)/shard_map/reduce_sum | solution.py:32
  63.8 8.3 %convolution_convert_fusion.1 = bf16[768,768]{1,0:T(8,128)(2,1)} fusion(f32[]{:T(128)S(6)} %mul_shard_map.3, f32[768,768]{1,0:T(8,128)} %bitcast.148, f32[768,768]{0,1:T(8,128)} %copy.35, f32[]{:T(128)} %bitcast.143), kind=kOutput, calls=%fused_computation.40 | convolution fusion | flops 1823735808 | bytes 5898248 | tf_op jit(solution)/shard_map/dot_general | solution.py:36
  72.1 3.2 %fusion.28 = bf16[768,128]{1,0:T(8,128)(2,1)S(1)} fusion(bf16[768,768]{1,0:T(8,128)(2,1)} %convolution_convert_fusion.1, pred[768,768]{1,0:T(32,128)(4,1)} %iota_compare_fusion), kind=kOutput, calls=%fused_computation.47 | convolution fusion | flops 302776320 | bytes 2949120 | tf_op jit(solution)/shard_map/dot_general | solution.py:39
  75.7 0.8 copy.37
  76.5 3.5 %all-to-all-start.2 = ((bf16[4,3,128,128]{3,2,1,0:T(8,128)(2,1)}), bf16[4,3,128,128]{3,2,1,0:T(8,128)(2,1)S(1)}, u32[]{:S(2)}, u32[]{:S(2)}) async-start(bf16[4,3,128,128]{3,2,1,0:T(8,128)(2,1)} %bitcast.29), calls=%async_computation.2 | async-start | bytes 786432 | tf_op jit(solution)/shard_map/all_to_all | solution.py:97
  80.1 7.3 %all-to-all-done.2 = bf16[4,3,128,128]{3,2,1,0:T(8,128)(2,1)S(1)} async-done(((bf16[4,3,128,128]{3,2,1,0:T(8,128)(2,1)}), bf16[4,3,128,128]{3,2,1,0:T(8,128)(2,1)S(1)}, u32[]{:S(2)}, u32[]{:S(2)}) %all-to-all-start.2) | async-done | bytes 393248 | tf_op jit(solution)/shard_map/all_to_all | solution.py:97
  87.4 41.5 %while.23 = (s32[]{:T(128)}, f32[1024]{0:T(1024)S(1)}, s32[12]{0:T(128)S(1)}, bf16[8,128,1024]{2,1,0:T(8,128)(2,1)S(1)}, bf16[12,128,128]{2,1,0:T(8,128)(2,1)S(1...) while((s32[]{:T(128)}, f32[1024]{0:T(1024)S(1)}, ...), condition=%wide.region_6.8_spmd.clone, body=%wide.region_4.7_spmd.clone.sunk | while | flops 34211856 | bytes 573781 | solution.py:119
  87.4 0.7 dynamic_slice.33
  90.9 0.7 dynamic_slice.33
  94.3 0.7 dynamic_slice.33
  97.8 0.7 dynamic_slice.33
  101.2 0.7 dynamic_slice.33
  104.7 0.7 dynamic_slice.33
  108.2 0.7 dynamic_slice.33
  111.6 0.7 dynamic_slice.33
  129.6 33.3 %while.22 = (s32[]{:T(128)}, bf16[12,128,128]{2,1,0:T(8,128)(2,1)S(1)}, s32[12]{0:T(128)S(1)}, bf16[8,128,1024]{2,1,0:T(8,128)(2,1)S(1)}, f32[1024]{0:T(1024)S(1...) while((s32[]{:T(128)}, ...), condition=%wide.region_8.10_spmd, body=%wide.region_7.9_spmd.sunk | while | flops 34226192 | bytes 561465 | solution.py:135
  162.9 9.8 %all_to_all.25 = bf16[4,3,128,128]{3,2,1,0:T(8,128)(2,1)S(1)} all-to-all(bf16[4,3,128,128]{3,2,1,0:T(8,128)(2,1)S(1)} %bitcast.154), channel_id=1, replica_groups=mesh['atoms'=8,'space'=4] {'space'}, dimensions={0} | all-to-all | bytes 786432 | tf_op jit(solution)/shard_map/all_to_all | solution.py:136
  173.0 0.8 copy.39
  (115 shorter events, 32.9 us)
Async XLA Ops:
  0.6 16.1 %copy-start = (bf16[1,4,128,128]{3,2,1,0:T(8,128)(2,1)S(1)}, bf16[1,4,128,128]{3,2,1,0:T(8,128)(2,1)}, u32[]{:S(2)}) copy-start(bf16[1,4,128,128]{3,2,1,0:T(8,128)(2,1)} %param.14) | copy-start | bytes 393220
  17.5 5.5 %copy-start.7 = (s32[1,1,36]{2,1,0:T(1,128)S(1)}, s32[1,1,36]{2,1,0:T(1,128)}, u32[]{:S(2)}) copy-start(s32[1,1,36]{2,1,0:T(1,128)} %param.15) | copy-start | bytes 436
  17.5 6.9 %copy-start.5 = (s32[1,1,12]{2,1,0:T(1,128)S(1)}, s32[1,1,12]{2,1,0:T(1,128)}, u32[]{:S(2)}) copy-start(s32[1,1,12]{2,1,0:T(1,128)} %param.20) | copy-start | bytes 148
  18.8 33.9 %all-to-all-start.1 = ((bf16[8,5,128,128]{3,2,1,0:T(8,128)(2,1)}), bf16[8,5,128,128]{3,2,1,0:T(8,128)(2,1)S(1)}, u32[]{:S(2)}, u32[]{:S(2)}) async-start(bf16[8,5,128,128]{3,2,1,0:T(8,128)(2,1)} %select_multiply_fusion), calls=%async_computation.1 | async-start | bytes 2621440 | tf_op jit(solution)/shard_map/all_to_all | solution.py:72
  72.1 8.0 %copy-start.4 = (s32[1,1,2,12]{3,2,1,0:T(2,128)S(1)}, s32[1,1,2,12]{3,2,1,0:T(2,128)}, u32[]{:S(2)}) copy-start(s32[1,1,2,12]{3,2,1,0:T(2,128)} %param.21) | copy-start | bytes 292
  72.1 15.3 %copy-start.6 = (bf16[1,1,8,128,1024]{4,3,2,1,0:T(8,128)(2,1)S(1)}, bf16[1,1,8,128,1024]{4,3,2,1,0:T(8,128)(2,1)}, u32[]{:S(2)}) copy-start(bf16[1,1,8,128,1024]{4,3,2,1,0:T(8,128)(2,1)} %param.17) | copy-start | bytes 6291460
  75.3 12.1 %copy-start.1 = (bf16[768,128]{1,0:T(8,128)(2,1)}, bf16[768,128]{1,0:T(8,128)(2,1)S(1)}, u32[]{:S(2)}) copy-start(bf16[768,128]{1,0:T(8,128)(2,1)S(1)} %fusion.28) | copy-start | bytes 589828
  76.5 10.8 %all-to-all-start.2 = ((bf16[4,3,128,128]{3,2,1,0:T(8,128)(2,1)}), bf16[4,3,128,128]{3,2,1,0:T(8,128)(2,1)S(1)}, u32[]{:S(2)}, u32[]{:S(2)}) async-start(bf16[4,3,128,128]{3,2,1,0:T(8,128)(2,1)} %bitcast.29), calls=%async_computation.2 | async-start | bytes 786432 | tf_op jit(solution)/shard_map/all_to_all | solution.py:97
  87.4 41.5 %copy-start.2 = (f32[1,1,1024]{2,1,0:T(1,128)S(1)}, f32[1,1,1024]{2,1,0:T(1,128)}, u32[]{:S(2)}) copy-start(f32[1,1,1024]{2,1,0:T(1,128)} %param.19) | copy-start | bytes 12292
  87.4 41.5 %copy-start.3 = (f32[1,1,1024]{2,1,0:T(1,128)S(1)}, f32[1,1,1024]{2,1,0:T(1,128)}, u32[]{:S(2)}) copy-start(f32[1,1,1024]{2,1,0:T(1,128)} %param.18) | copy-start | bytes 12292
where the time goes:
time: 175 us; the launch traced here: 174 us
  local copies, waits for them, and re-layouts  40.2 us (23%)
  loops' own time  39.8 us (23%)
  waiting for transfers between devices  34.2 us (20%)
  blocking collectives  23.4 us (13%)
  matrix products  18.3 us (10%)
  other arithmetic  8.64 us (5%)
  starting transfers between devices  7.03 us (4%)
  between operations  2.2 us (1%)
    dynamic_slice x48, local copies, waits for them, and re-layouts, per_device(): lax.scan(accumulate, jnp.zeros((points,), jnp.float32), (incoming, row_pi...  29 us
    all_to_all x1, waiting for transfers between devices, per_device(): lax.all_to_all(chosen.reshape(atom_devices, capacity, block_width, block_...  26.9 us
    another operation x1, loops' own time, per_device(): lax.scan(accumulate, jnp.zeros((points,), jnp.float32), (incoming, row_pi...  23.7 us
    another operation x1, loops' own time, per_device(): lax.scan(project, jnp.zeros((), jnp.float32), (row_pick, col_pick))  16.1 us
    all_to_all x1, blocking collectives, per_device(): lax.all_to_all(wanted.reshape(atom_devices, capacity), 'atoms', split_axi...  13.6 us
    all_to_all x1, blocking collectives, per_device(): lax.all_to_all(partials.reshape(space_devices, tile_capacity, block_width...  9.8 us
    dot_general x1, matrix products, sign_density(): jnp.dot(start_x, factor_one, preferred_element_type=jnp.float32)  8.25 us
    all_to_all x1, waiting for transfers between devices, per_device(): lax.all_to_all(outgoing.reshape(space_devices, tile_capacity, block_width...  7.33 us
  transfers between devices with their start and end apart: 2, of which 2 were waited for; matrix products, arithmetic and copies ran while one was open for 2% of the time, Pallas kernels for 0%

commit v1 on v0

v1 whole, which is shorter than its diff:
```python
import functools
import math

import jax
import jax.numpy as jnp
from jax import lax
from jax.experimental import pallas as pl
from jax.experimental.pallas import tpu as pltpu
from jax.sharding import PartitionSpec as P

KB = 6


slater_factor = math.pow(3.0 / math.pi, 1.0 / 3.0)
density_floor = 0.05

VMEM = pl.BlockSpec(memory_space=pltpu.VMEM)
SMEM = pl.BlockSpec(memory_space=pltpu.SMEM)


def earlier_count(labels):
    order = jnp.arange(labels.shape[0])
    earlier = (labels[None, :] == labels[:, None]) & (order[None, :] < order[:, None])
    return jnp.sum(earlier.astype(jnp.int32), axis=1)


def requested_blocks(stored, source):
    held_count, block_width, _ = stored.shape
    atom_devices = lax.axis_size("atoms")
    capacity = pl.cdiv(source.shape[0], atom_devices)
    peer_index = source // held_count
    local_index = source % held_count
    slot_index = peer_index * capacity + earlier_count(peer_index)
    wanted = jnp.full((atom_devices * capacity,), -1, jnp.int32).at[slot_index].set(local_index)
    requested = lax.all_to_all(
        wanted.reshape(atom_devices, capacity), "atoms", split_axis=0, concat_axis=0, tiled=True
    )
    flat_request = requested.reshape(-1)
    chosen = jnp.take(stored, jnp.clip(flat_request, 0, held_count - 1), axis=0)
    arrived = lax.all_to_all(
        chosen.reshape(atom_devices, capacity, block_width, block_width),
        "atoms",
        split_axis=0,
        concat_axis=0,
        tiled=True,
    )
    return arrived.reshape(atom_devices * capacity, block_width, block_width), slot_index


def gathered_blocks(stored, source):
    held_count, block_width, _ = stored.shape
    atom_devices = lax.axis_size("atoms")
    inner = 2 if atom_devices % 2 == 0 else 1
    outer = atom_devices // inner
    me = lax.axis_index("atoms")
    columns = [stored]
    for step in range(1, outer):
        pairs = [(i, (i + step * inner) % atom_devices) for i in range(atom_devices)]
        columns.append(lax.ppermute(stored, "atoms", pairs))
    parts = list(columns)
    if inner == 2:
        flip = [(i, i ^ 1) for i in range(atom_devices)]
        parts += [lax.ppermute(part, "atoms", flip) for part in columns]
    peer = source // held_count
    step = (me // inner - peer // inner) % outer
    other = (me % inner) ^ (peer % inner)
    place = (other * outer + step) * held_count + source % held_count
    return jnp.concatenate(parts, axis=0), place


def partner(me, step, devices):
    if devices & (devices - 1) == 0:
        return me ^ abs(step)
    return (me + step) % devices


def step_to(me, other, devices):
    if devices & (devices - 1) == 0:
        return me ^ other
    return lax.rem(other - me + devices, devices)


def step_from(me, other, devices):
    if devices & (devices - 1) == 0:
        return me ^ other
    return lax.rem(me - other + devices, devices)


def exchange(groups, sign):
    devices = lax.axis_size("space")
    got = [groups[0]] + [None] * (devices - 1)
    for step in reversed(range(1, devices)):
        pairs = [(i, partner(i, sign * step, devices)) for i in range(devices)]
        got[step] = lax.ppermute(groups[step], "space", pairs)
    return got


def pair_places(dest_ref, me, devices, capacity):
    sends = dest_ref.shape[0]
    dests = [dest_ref[j] for j in range(sends)]
    places = []
    for j in range(sends):
        rank = jnp.int32(0)
        for earlier in range(j):
            rank += jnp.where(dests[earlier] == dests[j], 1, 0)
        places.append(step_to(me, dests[j], devices) * capacity + rank)
    return places


def sign_kernel(
    devices, capacity, place_ref, chem_ref, dest_ref, me_ref, block_ref, density_ref, *rest
):
    out_refs = rest[:devices]
    shifted, x_zero, t_one, x_one, pairs = rest[devices:]
    width = block_ref.shape[-1]
    order = KB * width
    rows = lax.broadcasted_iota(jnp.int32, (width, width), 0)
    cols = lax.broadcasted_iota(jnp.int32, (width, width), 1)
    diagonal = rows == cols
    unit = jnp.where(diagonal, 1.0, 0.0)
    chem = chem_ref[0]

    def at(i):
        return pl.ds(i * width, width)

    total = jnp.zeros((8, width), jnp.float32)
    tiles = [(i, j) for i in range(KB) for j in range(i, KB)]
    for i, j in tiles:
        upper = block_ref[place_ref[i * KB + j]].astype(jnp.float32)
        lower = block_ref[place_ref[j * KB + i]].astype(jnp.float32)
        value = 0.5 * (upper + lower.T)
        if i == j:
            value = value - chem * unit
        shifted[at(i), at(j)] = value
        squares = (value * value).reshape(width // 8, 8, width).sum(axis=0)
        total = total + (squares if i == j else 2.0 * squares)
    mean = jnp.sum(total, keepdims=True) / order
    inverse = 1.0 / (2.0 * jnp.sqrt(mean + 1e-06))
    for i, j in tiles:
        value = (shifted[at(i), at(j)] * inverse).astype(jnp.bfloat16)
        x_zero[at(i), at(j)] = value
        if i != j:
            x_zero[at(j), at(i)] = value.T
    for i in range(KB):
        square = jnp.dot(x_zero[at(i), :], x_zero[...], preferred_element_type=jnp.float32)
        for j in range(KB):
            part = -0.5 * square[:, j * width : (j + 1) * width]
            t_one[at(i), at(j)] = (1.5 * unit + part if i == j else part).astype(jnp.bfloat16)
    for i in range(KB):
        x_one[at(i), :] = jnp.dot(
            x_zero[at(i), :], t_one[...], preferred_element_type=jnp.float32
        ).astype(jnp.bfloat16)
    square = jnp.dot(x_one[...], x_one[:, at(0)], preferred_element_type=jnp.float32)
    parts = []
    for i in range(KB):
        part = -0.5 * square[i * width : (i + 1) * width]
        parts.append((1.5 * unit + part if i == 0 else part).astype(jnp.bfloat16))
    t_two = jnp.concatenate(parts, axis=0)
    final = jnp.dot(x_one[...], t_two, preferred_element_type=jnp.float32)
    for i in range(KB):
        part = final[i * width : (i + 1) * width]
        density_ref[at(i), :] = (0.5 * (unit - part if i == 0 else -part)).astype(jnp.bfloat16)
    places = pair_places(dest_ref, me_ref[0], devices, capacity)
    for j, place in enumerate(places):
        pairs[place] = density_ref[at(j // 2), :]
    for k in range(devices):
        out_refs[k][...] = pairs[k * capacity : (k + 1) * capacity]


def grid_kernel(devices, capacity, full, me_ref, pick_ref, table_ref, core_ref, weight_ref, *rest):
    in_refs = rest[:devices]
    potential_ref = rest[devices]
    out_refs = rest[devices + 1 :]
    points = table_ref.shape[-1]
    width = table_ref.shape[1]
    me = me_ref[0]
    slots = []
    for k in range(devices):
        owner = step_from(me, k, devices)
        for c in range(capacity):
            slot = owner * capacity + c
            slots.append((k, c, pick_ref[0, slot], pick_ref[1, slot]))
    total = jnp.zeros((8, points), jnp.float32)
    for k, c, u, v in slots:
        left = table_ref[jnp.maximum(u, 0)].astype(jnp.float32)
        right = table_ref[jnp.maximum(v, 0)]
        product = jnp.dot(in_refs[k][c], right, preferred_element_type=jnp.float32)
        term = (left * product).reshape(width // 8, 8, points).sum(axis=0)
        total = total + term if full else jnp.where(u >= 0, total + term, total)
    valence = jnp.sum(total, axis=0, keepdims=True)
    value = jnp.maximum(core_ref[...] + valence, density_floor)
    root = jnp.exp(jnp.log(value) * (1.0 / 3.0))
    root = root - (root * root * root - value) / (3.0 * root * root)
    potential = -slater_factor * root
    potential_ref[...] = potential
    scaled = weight_ref[...] * potential
    for k, c, u, v in slots:
        left = table_ref[jnp.maximum(u, 0)].astype(jnp.float32)
        right = table_ref[jnp.maximum(v, 0)]
        weighted = (left * scaled).astype(jnp.bfloat16)
        out_refs[k][c] = lax.dot_general(
            weighted, right, (((1,), (1,)), ((), ())), preferred_element_type=jnp.float32
        ).astype(jnp.bfloat16)


def sum_kernel(devices, capacity, dest_ref, me_ref, *rest):
    in_refs = rest[:devices]
    kohn_ref, pairs = rest[devices:]
    width = kohn_ref.shape[-1]
    for k in range(devices):
        pairs[k * capacity : (k + 1) * capacity] = in_refs[k][...]
    places = pair_places(dest_ref, me_ref[0], devices, capacity)
    for i in range(KB):
        kohn_ref[pl.ds(i * width, width), :] = pairs[places[2 * i]].astype(jnp.float32) + pairs[
            places[2 * i + 1]
        ].astype(jnp.float32)


def per_device(
    block_store,
    block_source,
    chem_pot,
    basis_values,
    core_density,
    point_weights,
    pair_dest,
    tile_pairs,
):
    stored = block_store[0]
    held_count, block_width, _ = stored.shape
    source = block_source[0, 0]
    atom_devices = lax.axis_size("atoms")
    devices = lax.axis_size("space")
    if pl.cdiv(source.shape[0], atom_devices) < held_count:
        blocks, place = requested_blocks(stored, source)
    else:
        blocks, place = gathered_blocks(stored, source)
    destinations = pair_dest[0, 0]
    send_count = destinations.shape[0]
    capacity = pl.cdiv(send_count, devices)
    order = KB * block_width
    me = lax.axis_index("space").reshape(1)
    group = jax.ShapeDtypeStruct((capacity, block_width, block_width), jnp.bfloat16)
    out = pl.pallas_call(
        functools.partial(sign_kernel, devices, capacity),
        name="sign",
        in_specs=[SMEM] * 4 + [VMEM],
        out_shape=[jax.ShapeDtypeStruct((order, block_width), jnp.bfloat16)] + [group] * devices,
        out_specs=[VMEM] * (1 + devices),
        scratch_shapes=[
            pltpu.VMEM((order, order), jnp.float32),
            pltpu.VMEM((order, order), jnp.bfloat16),
            pltpu.VMEM((order, order), jnp.bfloat16),
            pltpu.VMEM((order, order), jnp.bfloat16),
            pltpu.VMEM((devices * capacity, block_width, block_width), jnp.bfloat16),
        ],
        compiler_params=pltpu.CompilerParams(vmem_limit_bytes=16 << 20),
        cost_estimate=pl.CostEstimate(
            flops=4 * order**3, bytes_accessed=4 * order * order, transcendentals=0
        ),
    )(place, chem_pot, destinations, me, blocks)
    density, outgoing = out[0], out[1:]
    incoming = exchange(outgoing, 1)
    tables = basis_values[0, 0]
    points = tables.shape[-1]
    out = pl.pallas_call(
        functools.partial(grid_kernel, devices, capacity, devices * capacity == send_count),
        name="grid",
        in_specs=[SMEM] * 2 + [VMEM] * (3 + devices),
        out_shape=[jax.ShapeDtypeStruct((1, points), jnp.float32)] + [group] * devices,
        out_specs=[VMEM] * (1 + devices),
        compiler_params=pltpu.CompilerParams(vmem_limit_bytes=24 << 20),
        cost_estimate=pl.CostEstimate(
            flops=4 * devices * capacity * block_width**2 * points,
            bytes_accessed=2 * tables.size,
            transcendentals=2 * points,
        ),
    )(me, tile_pairs[0, 0], tables, core_density[0], point_weights[0], *incoming)
    potential, partials = out[0], out[1:]
    returned = exchange(partials, -1)
    kohn = pl.pallas_call(
        functools.partial(sum_kernel, devices, capacity),
        name="sum",
        in_specs=[SMEM] * 2 + [VMEM] * devices,
        out_shape=jax.ShapeDtypeStruct((order, block_width), jnp.float32),
        out_specs=VMEM,
        scratch_shapes=[
            pltpu.VMEM((devices * capacity, block_width, block_width), jnp.bfloat16),
        ],
        compiler_params=pltpu.CompilerParams(vmem_limit_bytes=8 << 20),
    )(destinations, me, *returned)
    return (density[None, None], potential[None], kohn[None, None])


def solution(mesh):
    placed = (
        P("space", "atoms", None, None),
        P("atoms", "space", None),
        P(),
        P("atoms", "space", None, None, None),
        P("atoms", "space", None),
        P("atoms", "space", None),
        P("atoms", "space", None),
        P("atoms", "space", None, None),
    )
    return jax.shard_map(
        per_device,
        mesh=mesh,
        in_specs=placed,
        out_specs=(
            P("atoms", "space", None, None),
            P("atoms", "space", None),
            P("atoms", "space", None, None),
        ),
        check_vma=False,
    )
```

time: 175 us -> 46.9 us (0.27)
  loops' own time: 39.8 us -> 0 us
  local copies, waits for them, and re-layouts: 40.2 us -> 1.11 us
  blocking collectives: 23.4 us -> 0 us
  matrix products: 18.3 us -> 0 us
  waiting for transfers between devices: 34.2 us -> 18.9 us
  Pallas kernels: 0 us -> 9.62 us
  starting transfers between devices: 7.03 us -> 15 us
  other arithmetic: 8.64 us -> 0.69 us
    another operation x2 -> x0, loops' own time: 39.8 us -> none  [the longest x1 23.7 us: per_device(): lax.scan(accumulate, jnp.zeros((points,), jnp.float32), (incoming, row_pi...]
    all_to_all x2 -> x0, waiting for transfers between devices: 34.2 us -> none  [the longest x1 26.9 us: per_device(): lax.all_to_all(chosen.reshape(atom_devices, capacity, block_width, block_...]
    dynamic_slice x48 -> x0, local copies, waits for them, and re-layouts: 29 us -> none  [per_device(): lax.scan(accumulate, jnp.zeros((points,), jnp.float32), (incoming, row_pi...]
    all_to_all x2 -> x0, blocking collectives: 23.4 us -> none  [the longest x1 13.6 us: per_device(): lax.all_to_all(wanted.reshape(atom_devices, capacity), 'atoms', split_axi...]
    ppermute x0 -> x13, waiting for transfers between devices: none -> 18.9 us  [the longest x6 9.99 us: exchange(): got[step] = lax.ppermute(groups[step], 'space', pairs)]
    dot_general x29 -> x0, matrix products: 18.3 us -> none  [the longest x1 8.25 us: sign_density(): jnp.dot(start_x, factor_one, preferred_element_type=jnp.float32)]
    ppermute x0 -> x13, starting transfers between devices: none -> 15 us  [the longest x3 7.04 us: gathered_blocks(): columns.append(lax.ppermute(stored, 'atoms', pairs))]
    pallas_call x0 -> x3, Pallas kernels: none -> 9.62 us  [the longest x1 5.21 us: per_device(): pl.pallas_call(functools.partial(sign_kernel, devices, capacity), name='s...]
  transfers between devices with their start and end apart: 2 -> 13, of which waited for: 2 -> 7; matrix products, arithmetic and copies ran while one was open for 2% -> 4% of each run, Pallas kernels for 0% -> 0%
where the time goes in v1:
time: 46.9 us; the launch traced here: 46.8 us
  waiting for transfers between devices  18.9 us (40%)
  starting transfers between devices  15 us (32%)
  Pallas kernels  9.62 us (21%)
  between operations  1.44 us (3%)
  local copies, waits for them, and re-layouts  1.11 us (2%)
  other arithmetic  0.69 us (1%)
    ppermute x6, waiting for transfers between devices, exchange(): got[step] = lax.ppermute(groups[step], 'space', pairs)  9.99 us
    ppermute x3, starting transfers between devices, gathered_blocks(): columns.append(lax.ppermute(stored, 'atoms', pairs))  7.04 us
    ppermute x4, waiting for transfers between devices, gathered_blocks(): parts += [lax.ppermute(part, 'atoms', flip) for part in columns]  5.9 us
    pallas_call x1, Pallas kernels, per_device(): pl.pallas_call(functools.partial(sign_kernel, devices, capacity), name='s...  5.21 us
    ppermute x4, starting transfers between devices, gathered_blocks(): parts += [lax.ppermute(part, 'atoms', flip) for part in columns]  4.25 us
    ppermute x6, starting transfers between devices, exchange(): got[step] = lax.ppermute(groups[step], 'space', pairs)  3.72 us
    pallas_call x1, Pallas kernels, per_device(): pl.pallas_call(functools.partial(grid_kernel, devices, capacity, devices...  3.01 us
    ppermute x3, waiting for transfers between devices, gathered_blocks(): columns.append(lax.ppermute(stored, 'atoms', pairs))  3.01 us
  transfers between devices with their start and end apart: 13, of which 7 were waited for; matrix products, arithmetic and copies ran while one was open for 4% of the time, Pallas kernels for 0%

profile of v1, /device:TPU:0, one launch (start us, length us, event | category | flops | bytes accessed | tf_op | source)
XLA Modules:
  0.0 46.8 jit_solution(8883009249425282885)
XLA Ops:
  0.6 3.1 %collective-permute-start = (bf16[4,128,128]{2,1,0:T(8,128)(2,1)}, bf16[4,128,128]{2,1,0:T(8,128)(2,1)S(1)}, u32[]{:S(2)}, u32[]{:S(2)}) collective-permute-start(bf16[4,128,128]{2,1,0:T(8,128)(2,1)} %bitcast.31), channel_id=1, source_target_pairs={{0,8},{4,12},{8,16},{12,20},{16,24},{20,28},{24,0},{28,4},{1,9},{5... | collective-permute-start | bytes 393224 | tf_op jit(solution)/shard_map/ppermute | solution.py:59
  3.7 2.6 %collective-permute-start.1 = (bf16[4,128,128]{2,1,0:T(8,128)(2,1)}, bf16[4,128,128]{2,1,0:T(8,128)(2,1)S(1)}, u32[]{:S(2)}, u32[]{:S(2)}) collective-permute-start(bf16[4,128,128]{2,1,0:T(8,128)(2,1)} %bitcast.32), channel_id=1, source_target_pairs={{0,16},{4,20},{8,24},{12,28},{16,0},{20,4},{24,8},{28,12},{1,17},{... | collective-permute-start | bytes 393224 | tf_op jit(solution)/shard_map/ppermute | solution.py:59
  6.3 1.3 %collective-permute-start.2 = (bf16[4,128,128]{2,1,0:T(8,128)(2,1)}, bf16[4,128,128]{2,1,0:T(8,128)(2,1)S(1)}, u32[]{:S(2)}, u32[]{:S(2)}) collective-permute-start(bf16[4,128,128]{2,1,0:T(8,128)(2,1)} %bitcast.33), channel_id=1, source_target_pairs={{0,24},{4,28},{8,0},{12,4},{16,8},{20,12},{24,16},{28,20},{1,25},{... | collective-permute-start | bytes 393224 | tf_op jit(solution)/shard_map/ppermute | solution.py:59
  7.7 1.5 %collective-permute-start.3 = (bf16[4,128,128]{2,1,0:T(8,128)(2,1)}, bf16[4,128,128]{2,1,0:T(8,128)(2,1)S(1)}, u32[]{:S(2)}, u32[]{:S(2)}) collective-permute-start(bf16[4,128,128]{2,1,0:T(8,128)(2,1)} %bitcast.34), channel_id=1, source_target_pairs={{0,4},{4,0},{8,12},{12,8},{16,20},{20,16},{24,28},{28,24},{1,5},{5... | collective-permute-start | bytes 393224 | tf_op jit(solution)/shard_map/ppermute | solution.py:63
  9.2 0.9 %constant_dynamic-update-slice_fusion.7 = bf16[32,128,128]{2,1,0:T(8,128)(2,1)S(1)} fusion(bf16[1,4,128,128]{3,2,1,0:T(8,128)(2,1)} %param.8), kind=kLoop, calls=%fused_computation.7 | loop fusion | bytes 262144
  10.2 0.7 %fusion.1.place_ref = s32[36]{0:T(128)S(1)} fusion(s32[1,1,36]{2,1,0:T(1,128)} %param.9, s32[]{:T(128)S(6)} %select_n.36, s32[]{:T(128)S(6)} %select_n.33), kind=kLoop, calls=%fused_computation.22 | loop fusion | flops 1980 | bytes 296 | tf_op jit(solution)/shard_map/add | solution.py:67
  11.5 0.6 %collective-permute-start.4 = (bf16[4,128,128]{2,1,0:T(8,128)(2,1)S(1)}, bf16[4,128,128]{2,1,0:T(8,128)(2,1)S(1)}, u32[]{:S(2)}, u32[]{:S(2)}) collective-permute-start(bf16[4,128,128]{2,1,0:T(8,128)(2,1)S(1)} %collective-permute-done), channel_id=1, source_target_pairs={{0,4},{4,0},{8,12},{12,8},{16,20},{20,16},{24,28},{28,24},{1,5},{5... | collective-permute-start | bytes 393224 | tf_op jit(solution)/shard_map/ppermute | solution.py:63
  12.2 3.0 %collective-permute-done.1 = bf16[4,128,128]{2,1,0:T(8,128)(2,1)S(1)} collective-permute-done((bf16[4,128,128]{2,1,0:T(8,128)(2,1)}, bf16[4,128,128]{2,1,0:T(8,128)(2,1)S(1)}, u32[]{:S(2)}, u32[]{:S(2)}) %collective-permute-start.1) | collective-permute-done | bytes 131104 | tf_op jit(solution)/shard_map/ppermute | solution.py:59
  15.2 1.5 %collective-permute-start.5 = (bf16[4,128,128]{2,1,0:T(8,128)(2,1)S(1)}, bf16[4,128,128]{2,1,0:T(8,128)(2,1)S(1)}, u32[]{:S(2)}, u32[]{:S(2)}) collective-permute-start(bf16[4,128,128]{2,1,0:T(8,128)(2,1)S(1)} %collective-permute-done.1), channel_id=1, source_target_pairs={{0,4},{4,0},{8,12},{12,8},{16,20},{20,16},{24,28},{28,24},{1,5},{5... | collective-permute-start | bytes 393224 | tf_op jit(solution)/shard_map/ppermute | solution.py:63
  16.7 0.0 collective-permute-done.2
  16.7 0.6 %collective-permute-start.6 = (bf16[4,128,128]{2,1,0:T(8,128)(2,1)S(1)}, bf16[4,128,128]{2,1,0:T(8,128)(2,1)S(1)}, u32[]{:S(2)}, u32[]{:S(2)}) collective-permute-start(bf16[4,128,128]{2,1,0:T(8,128)(2,1)S(1)} %collective-permute-done.2), channel_id=1, source_target_pairs={{0,4},{4,0},{8,12},{12,8},{16,20},{20,16},{24,28},{28,24},{1,5},{5... | collective-permute-start | bytes 393224 | tf_op jit(solution)/shard_map/ppermute | solution.py:63
  17.3 0.0 collective-permute-done.3
  17.4 0.0 collective-permute-done.4
  17.4 4.1 %collective-permute-done.5 = bf16[4,128,128]{2,1,0:T(8,128)(2,1)S(1)} collective-permute-done((bf16[4,128,128]{2,1,0:T(8,128)(2,1)S(1)}, bf16[4,128,128]{2,1,0:T(8,128)(2,1)S(1)}, u32[]{:S(2)}, u32[]{:S(2)}) %collective-permute-start.5) | collective-permute-done | bytes 131104 | tf_op jit(solution)/shard_map/ppermute | solution.py:63
  21.6 1.7 %collective-permute-done.6 = bf16[4,128,128]{2,1,0:T(8,128)(2,1)S(1)} collective-permute-done((bf16[4,128,128]{2,1,0:T(8,128)(2,1)S(1)}, bf16[4,128,128]{2,1,0:T(8,128)(2,1)S(1)}, u32[]{:S(2)}, u32[]{:S(2)}) %collective-permute-start.6) | collective-permute-done | bytes 131104 | tf_op jit(solution)/shard_map/ppermute | solution.py:63
  23.4 0.0 copy-start.1
  23.4 0.0 copy-start.2
  23.4 0.0 copy-start.3
  23.4 0.0 copy-start.4
  23.4 5.2 %sign.26 = (bf16[768,128]{1,0:T(8,128)(2,1)}, bf16[3,128,128]{2,1,0:T(8,128)(2,1)S(1)}, bf16[3,128,128]{2,1,0:T(8,128)(2,1)S(1)}, bf16[3,128,128]{2,1,0:T(8,128)(2,1)S(1)}, bf16[3,128,128]{2,1,0:T(8,128)(2,1)S(1)}) custom-call(s32[36]{0:T(128)S(1)} %fusion.1.place_ref, f32[1]{0:T(128)S(6)} %copy.18.chem_ref, s32[12]{0:T(128)S(1)} %bitcast.24, ...), custom_call_target="tpu_custom_call" | custom-call | flops 1811939328 | bytes 2359296 | tf_op jit(solution)/shard_map/sign/pallas_call | solution.py:244
  28.6 0.0 collective-permute-start.7
  28.6 1.5 %collective-permute-start.8 = (bf16[3,128,128]{2,1,0:T(8,128)(2,1)S(1)}, bf16[3,128,128]{2,1,0:T(8,128)(2,1)S(1)}, u32[]{:S(2)}, u32[]{:S(2)}) collective-permute-start(bf16[3,128,128]{2,1,0:T(8,128)(2,1)S(1)} %get-tuple-element.16), channel_id=1, source_target_pairs={{0,2},{1,3},{2,0},{3,1},{4,6},{5,7},{6,4},{7,5},{8,10},{9,11},{10,... | collective-permute-start | bytes 294920 | tf_op jit(solution)/shard_map/ppermute | solution.py:94
  30.1 0.4 collective-permute-start.9
  30.5 3.8 %collective-permute-done.8.rest_2_ = bf16[3,128,128]{2,1,0:T(8,128)(2,1)S(1)} collective-permute-done((bf16[3,128,128]{2,1,0:T(8,128)(2,1)S(1)}, bf16[3,128,128]{2,1,0:T(8,128)(2,1)S(1)}, u32[]{:S(2)}, u32[]{:S(2)}) %collective-permute-start.8) | collective-permute-done | bytes 98336 | tf_op jit(solution)/shard_map/ppermute | solution.py:94
  34.3 1.2 %collective-permute-done.9.rest_3_ = bf16[3,128,128]{2,1,0:T(8,128)(2,1)S(1)} collective-permute-done((bf16[3,128,128]{2,1,0:T(8,128)(2,1)S(1)}, bf16[3,128,128]{2,1,0:T(8,128)(2,1)S(1)}, u32[]{:S(2)}, u32[]{:S(2)}) %collective-permute-start.9) | collective-permute-done | bytes 98336 | tf_op jit(solution)/shard_map/ppermute | solution.py:94
  35.5 3.0 %grid.1 = (f32[1,1024]{1,0:T(1,128)}, bf16[3,128,128]{2,1,0:T(8,128)(2,1)S(1)}, bf16[3,128,128]{2,1,0:T(8,128)(2,1)S(1)}, bf16[3,128,128]{2,1,0:T(8,128)(2,1)S(1)}, bf16[3,128,128]{2,1,0:T(8,128)(2,1)S(1)}) custom-call(s32[1]{0:T(128)} %bitcast.2.me_ref, s32[2,12]{1,0:T(2,128)S(1)} %bitcast.29, bf16[8,128,1024]{2,1,0:T(8,128)(2,1)S(1)} %bitcast.26, ...), custom_call_target="tpu_custom_call" | custom-call | flops 805306368 | bytes 2097152 | tf_op jit(solution)/shard_map/grid/pallas_call | solution.py:266
  38.5 0.3 collective-permute-start.10
  38.8 1.5 %collective-permute-start.11 = (bf16[3,128,128]{2,1,0:T(8,128)(2,1)S(1)}, bf16[3,128,128]{2,1,0:T(8,128)(2,1)S(1)}, u32[]{:S(2)}, u32[]{:S(2)}) collective-permute-start(bf16[3,128,128]{2,1,0:T(8,128)(2,1)S(1)} %get-tuple-element.21), channel_id=1, source_target_pairs={{0,2},{1,3},{2,0},{3,1},{4,6},{5,7},{6,4},{7,5},{8,10},{9,11},{10,... | collective-permute-start | bytes 294920 | tf_op jit(solution)/shard_map/ppermute | solution.py:94
  40.3 0.1 collective-permute-start.12
  40.4 3.8 %collective-permute-done.11.rest_2_ = bf16[3,128,128]{2,1,0:T(8,128)(2,1)S(1)} collective-permute-done((bf16[3,128,128]{2,1,0:T(8,128)(2,1)S(1)}, bf16[3,128,128]{2,1,0:T(8,128)(2,1)S(1)}, u32[]{:S(2)}, u32[]{:S(2)}) %collective-permute-start.11) | collective-permute-done | bytes 98336 | tf_op jit(solution)/shard_map/ppermute | solution.py:94
  44.1 1.2 %collective-permute-done.12.rest_3_ = bf16[3,128,128]{2,1,0:T(8,128)(2,1)S(1)} collective-permute-done((bf16[3,128,128]{2,1,0:T(8,128)(2,1)S(1)}, bf16[3,128,128]{2,1,0:T(8,128)(2,1)S(1)}, u32[]{:S(2)}, u32[]{:S(2)}) %collective-permute-start.12) | collective-permute-done | bytes 98336 | tf_op jit(solution)/shard_map/ppermute | solution.py:94
  45.4 1.4 %sum.1 = f32[768,128]{1,0:T(8,128)} custom-call(s32[12]{0:T(128)S(1)} %bitcast.25, s32[1]{0:T(128)} %bitcast.2.me_ref, bf16[3,128,128]{2,1,0:T(8,128)(2,1)S(1)} %get-tuple-element.19.rest_0_, bf16[3,128,128]{2,1,0:T(8,128)(2,1)S(1)} %collective-permute-done.10.rest_1_, bf16[3,128,128]{2,1,0:T(8,128)(2,1)S(1)} %collective-permute-done.11.rest_2_, ...), custom_call_target="tpu_custom_call" | custom-call | tf_op jit(solution)/shard_map/sum/pallas_call | solution.py:281
  (16 shorter events, 0.2 us)
Async XLA Ops:
  0.6 22.7 %copy-start = (s32[1,1,12]{2,1,0:T(1,128)S(1)}, s32[1,1,12]{2,1,0:T(1,128)}, u32[]{:S(2)}) copy-start(s32[1,1,12]{2,1,0:T(1,128)} %param.14) | copy-start | bytes 148
  0.6 10.9 %collective-permute-start = (bf16[4,128,128]{2,1,0:T(8,128)(2,1)}, bf16[4,128,128]{2,1,0:T(8,128)(2,1)S(1)}, u32[]{:S(2)}, u32[]{:S(2)}) collective-permute-start(bf16[4,128,128]{2,1,0:T(8,128)(2,1)} %bitcast.31), channel_id=1, source_target_pairs={{0,8},{4,12},{8,16},{12,20},{16,24},{20,28},{24,0},{28,4},{1,9},{5... | collective-permute-start | bytes 393224 | tf_op jit(solution)/shard_map/ppermute | solution.py:59
  3.7 11.4 %collective-permute-start.1 = (bf16[4,128,128]{2,1,0:T(8,128)(2,1)}, bf16[4,128,128]{2,1,0:T(8,128)(2,1)S(1)}, u32[]{:S(2)}, u32[]{:S(2)}) collective-permute-start(bf16[4,128,128]{2,1,0:T(8,128)(2,1)} %bitcast.32), channel_id=1, source_target_pairs={{0,16},{4,20},{8,24},{12,28},{16,0},{20,4},{24,8},{28,12},{1,17},{... | collective-permute-start | bytes 393224 | tf_op jit(solution)/shard_map/ppermute | solution.py:59
  6.3 10.4 %collective-permute-start.2 = (bf16[4,128,128]{2,1,0:T(8,128)(2,1)}, bf16[4,128,128]{2,1,0:T(8,128)(2,1)S(1)}, u32[]{:S(2)}, u32[]{:S(2)}) collective-permute-start(bf16[4,128,128]{2,1,0:T(8,128)(2,1)} %bitcast.33), channel_id=1, source_target_pairs={{0,24},{4,28},{8,0},{12,4},{16,8},{20,12},{24,16},{28,20},{1,25},{... | collective-permute-start | bytes 393224 | tf_op jit(solution)/shard_map/ppermute | solution.py:59
  7.7 9.7 %collective-permute-start.3 = (bf16[4,128,128]{2,1,0:T(8,128)(2,1)}, bf16[4,128,128]{2,1,0:T(8,128)(2,1)S(1)}, u32[]{:S(2)}, u32[]{:S(2)}) collective-permute-start(bf16[4,128,128]{2,1,0:T(8,128)(2,1)} %bitcast.34), channel_id=1, source_target_pairs={{0,4},{4,0},{8,12},{12,8},{16,20},{20,16},{24,28},{28,24},{1,5},{5... | collective-permute-start | bytes 393224 | tf_op jit(solution)/shard_map/ppermute | solution.py:63
  11.5 5.8 %collective-permute-start.4 = (bf16[4,128,128]{2,1,0:T(8,128)(2,1)S(1)}, bf16[4,128,128]{2,1,0:T(8,128)(2,1)S(1)}, u32[]{:S(2)}, u32[]{:S(2)}) collective-permute-start(bf16[4,128,128]{2,1,0:T(8,128)(2,1)S(1)} %collective-permute-done), channel_id=1, source_target_pairs={{0,4},{4,0},{8,12},{12,8},{16,20},{20,16},{24,28},{28,24},{1,5},{5... | collective-permute-start | bytes 393224 | tf_op jit(solution)/shard_map/ppermute | solution.py:63
  15.2 6.4 %collective-permute-start.5 = (bf16[4,128,128]{2,1,0:T(8,128)(2,1)S(1)}, bf16[4,128,128]{2,1,0:T(8,128)(2,1)S(1)}, u32[]{:S(2)}, u32[]{:S(2)}) collective-permute-start(bf16[4,128,128]{2,1,0:T(8,128)(2,1)S(1)} %collective-permute-done.1), channel_id=1, source_target_pairs={{0,4},{4,0},{8,12},{12,8},{16,20},{20,16},{24,28},{28,24},{1,5},{5... | collective-permute-start | bytes 393224 | tf_op jit(solution)/shard_map/ppermute | solution.py:63
  16.7 6.6 %collective-permute-start.6 = (bf16[4,128,128]{2,1,0:T(8,128)(2,1)S(1)}, bf16[4,128,128]{2,1,0:T(8,128)(2,1)S(1)}, u32[]{:S(2)}, u32[]{:S(2)}) collective-permute-start(bf16[4,128,128]{2,1,0:T(8,128)(2,1)S(1)} %collective-permute-done.2), channel_id=1, source_target_pairs={{0,4},{4,0},{8,12},{12,8},{16,20},{20,16},{24,28},{28,24},{1,5},{5... | collective-permute-start | bytes 393224 | tf_op jit(solution)/shard_map/ppermute | solution.py:63
  23.4 12.1 %copy-start.1 = (bf16[1,1,8,128,1024]{4,3,2,1,0:T(8,128)(2,1)S(1)}, bf16[1,1,8,128,1024]{4,3,2,1,0:T(8,128)(2,1)}, u32[]{:S(2)}) copy-start(bf16[1,1,8,128,1024]{4,3,2,1,0:T(8,128)(2,1)} %param.11) | copy-start | bytes 6291460
  23.4 12.1 %copy-start.2 = (f32[1,1,1024]{2,1,0:T(1,128)S(1)}, f32[1,1,1024]{2,1,0:T(1,128)}, u32[]{:S(2)}) copy-start(f32[1,1,1024]{2,1,0:T(1,128)} %param.12) | copy-start | bytes 12292
  23.4 12.1 %copy-start.3 = (f32[1,1,1024]{2,1,0:T(1,128)S(1)}, f32[1,1,1024]{2,1,0:T(1,128)}, u32[]{:S(2)}) copy-start(f32[1,1,1024]{2,1,0:T(1,128)} %param.13) | copy-start | bytes 12292
  23.4 12.1 %copy-start.4 = (s32[1,1,2,12]{3,2,1,0:T(2,128)S(1)}, s32[1,1,2,12]{3,2,1,0:T(2,128)}, u32[]{:S(2)}) copy-start(s32[1,1,2,12]{3,2,1,0:T(2,128)} %param.15) | copy-start | bytes 292
  28.6 1.9 %collective-permute-start.7 = (bf16[3,128,128]{2,1,0:T(8,128)(2,1)S(1)}, bf16[3,128,128]{2,1,0:T(8,128)(2,1)S(1)}, u32[]{:S(2)}, u32[]{:S(2)}) collective-permute-start(bf16[3,128,128]{2,1,0:T(8,128)(2,1)S(1)} %get-tuple-element.15), channel_id=1, source_target_pairs={{0,1},{1,0},{2,3},{3,2},{4,5},{5,4},{6,7},{7,6},{8,9},{9,8},{10,11... | collective-permute-start | bytes 294920 | tf_op jit(solution)/shard_map/ppermute | solution.py:94
  28.6 5.7 %collective-permute-start.8 = (bf16[3,128,128]{2,1,0:T(8,128)(2,1)S(1)}, bf16[3,128,128]{2,1,0:T(8,128)(2,1)S(1)}, u32[]{:S(2)}, u32[]{:S(2)}) collective-permute-start(bf16[3,128,128]{2,1,0:T(8,128)(2,1)S(1)} %get-tuple-element.16), channel_id=1, source_target_pairs={{0,2},{1,3},{2,0},{3,1},{4,6},{5,7},{6,4},{7,5},{8,10},{9,11},{10,... | collective-permute-start | bytes 294920 | tf_op jit(solution)/shard_map/ppermute | solution.py:94
  30.1 5.4 %collective-permute-start.9 = (bf16[3,128,128]{2,1,0:T(8,128)(2,1)S(1)}, bf16[3,128,128]{2,1,0:T(8,128)(2,1)S(1)}, u32[]{:S(2)}, u32[]{:S(2)}) collective-permute-start(bf16[3,128,128]{2,1,0:T(8,128)(2,1)S(1)} %get-tuple-element.17), channel_id=1, source_target_pairs={{0,3},{1,2},{2,1},{3,0},{4,7},{5,6},{6,5},{7,4},{8,11},{9,10},{10,... | collective-permute-start | bytes 294920 | tf_op jit(solution)/shard_map/ppermute | solution.py:94
  38.5 1.9 %collective-permute-start.10 = (bf16[3,128,128]{2,1,0:T(8,128)(2,1)S(1)}, bf16[3,128,128]{2,1,0:T(8,128)(2,1)S(1)}, u32[]{:S(2)}, u32[]{:S(2)}) collective-permute-start(bf16[3,128,128]{2,1,0:T(8,128)(2,1)S(1)} %get-tuple-element.20), channel_id=1, source_target_pairs={{0,1},{1,0},{2,3},{3,2},{4,5},{5,4},{6,7},{7,6},{8,9},{9,8},{10,11... | collective-permute-start | bytes 294920 | tf_op jit(solution)/shard_map/ppermute | solution.py:94
  38.8 5.4 %collective-permute-start.11 = (bf16[3,128,128]{2,1,0:T(8,128)(2,1)S(1)}, bf16[3,128,128]{2,1,0:T(8,128)(2,1)S(1)}, u32[]{:S(2)}, u32[]{:S(2)}) collective-permute-start(bf16[3,128,128]{2,1,0:T(8,128)(2,1)S(1)} %get-tuple-element.21), channel_id=1, source_target_pairs={{0,2},{1,3},{2,0},{3,1},{4,6},{5,7},{6,4},{7,5},{8,10},{9,11},{10,... | collective-permute-start | bytes 294920 | tf_op jit(solution)/shard_map/ppermute | solution.py:94
  40.3 5.1 %collective-permute-start.12 = (bf16[3,128,128]{2,1,0:T(8,128)(2,1)S(1)}, bf16[3,128,128]{2,1,0:T(8,128)(2,1)S(1)}, u32[]{:S(2)}, u32[]{:S(2)}) collective-permute-start(bf16[3,128,128]{2,1,0:T(8,128)(2,1)S(1)} %get-tuple-element.22), channel_id=1, source_target_pairs={{0,3},{1,2},{2,1},{3,0},{4,7},{5,6},{6,5},{7,4},{8,11},{9,10},{10,... | collective-permute-start | bytes 294920 | tf_op jit(solution)/shard_map/ppermute | solution.py:94

commit v2 on v1

--- a/solution.py
+++ b/solution.py
@@ -48,23 +48,17 @@
 
 
 def gathered_blocks(stored, source):
-    held_count, block_width, _ = stored.shape
+    held_count, _, _ = stored.shape
     atom_devices = lax.axis_size("atoms")
-    inner = 2 if atom_devices % 2 == 0 else 1
-    outer = atom_devices // inner
+    if atom_devices & (atom_devices - 1):
+        return lax.all_gather(stored, "atoms", axis=0, tiled=True), source
+    parts = [stored] + [None] * (atom_devices - 1)
+    for offset in sorted(range(1, atom_devices), key=lambda r: (r.bit_count(), -r)):
+        step = 2 if offset == 3 else offset & -offset
+        pairs = [(i, i ^ step) for i in range(atom_devices)]
+        parts[offset] = lax.ppermute(parts[offset ^ step], "atoms", pairs)
     me = lax.axis_index("atoms")
-    columns = [stored]
-    for step in range(1, outer):
-        pairs = [(i, (i + step * inner) % atom_devices) for i in range(atom_devices)]
-        columns.append(lax.ppermute(stored, "atoms", pairs))
-    parts = list(columns)
-    if inner == 2:
-        flip = [(i, i ^ 1) for i in range(atom_devices)]
-        parts += [lax.ppermute(part, "atoms", flip) for part in columns]
-    peer = source // held_count
-    step = (me // inner - peer // inner) % outer
-    other = (me % inner) ^ (peer % inner)
-    place = (other * outer + step) * held_count + source % held_count
+    place = (me ^ (source // held_count)) * held_count + source % held_count
     return jnp.concatenate(parts, axis=0), place
 
 
@@ -88,10 +82,10 @@
 
 def exchange(groups, sign):
     devices = lax.axis_size("space")
-    got = [groups[0]] + [None] * (devices - 1)
-    for step in reversed(range(1, devices)):
+    got = {}
+    for step in sorted(groups, reverse=True):
         pairs = [(i, partner(i, sign * step, devices)) for i in range(devices)]
-        got[step] = lax.ppermute(groups[step], "space", pairs)
+        got[step] = lax.ppermute(groups[step], "space", pairs) if step else groups[step]
     return got
 
 
@@ -167,40 +161,73 @@
         out_refs[k][...] = pairs[k * capacity : (k + 1) * capacity]
 
 
-def grid_kernel(devices, capacity, full, me_ref, pick_ref, table_ref, core_ref, weight_ref, *rest):
-    in_refs = rest[:devices]
-    potential_ref = rest[devices]
-    out_refs = rest[devices + 1 :]
-    points = table_ref.shape[-1]
-    width = table_ref.shape[1]
-    me = me_ref[0]
+def tile_slots(pick_ref, me, steps, devices, capacity):
     slots = []
-    for k in range(devices):
+    for k in steps:
         owner = step_from(me, k, devices)
         for c in range(capacity):
             slot = owner * capacity + c
             slots.append((k, c, pick_ref[0, slot], pick_ref[1, slot]))
-    total = jnp.zeros((8, points), jnp.float32)
+    return slots
+
+
+def pair_density(slots, total, full, table_ref, group_refs):
+    width, points = table_ref.shape[1:]
     for k, c, u, v in slots:
         left = table_ref[jnp.maximum(u, 0)].astype(jnp.float32)
         right = table_ref[jnp.maximum(v, 0)]
-        product = jnp.dot(in_refs[k][c], right, preferred_element_type=jnp.float32)
+        product = jnp.dot(group_refs[k][c], right, preferred_element_type=jnp.float32)
         term = (left * product).reshape(width // 8, 8, points).sum(axis=0)
         total = total + term if full else jnp.where(u >= 0, total + term, total)
+    return total
+
+
+def pair_partials(slots, scaled, table_ref, group_refs):
+    for k, c, u, v in slots:
+        left = table_ref[jnp.maximum(u, 0)].astype(jnp.float32)
+        right = table_ref[jnp.maximum(v, 0)]
+        weighted = (left * scaled).astype(jnp.bfloat16)
+        group_refs[k][c] = lax.dot_general(
+            weighted, right, (((1,), (1,)), ((), ())), preferred_element_type=jnp.float32
+        ).astype(jnp.bfloat16)
+
+
+def near_density_kernel(
+    devices, capacity, full, steps, me_ref, pick_ref, table_ref, column_ref, *rest
+):
+    groups = dict(zip(steps, rest[: len(steps)]))
+    total_ref, density_ref = rest[len(steps) :]
+    density_ref[...] = column_ref[...]
+    slots = tile_slots(pick_ref, me_ref[0], steps, devices, capacity)
+    total = jnp.zeros(total_ref.shape, jnp.float32)
+    total_ref[...] = pair_density(slots, total, full, table_ref, groups)
+
+
+def far_kernel(
+    devices, capacity, full, steps, me_ref, pick_ref, table_ref, core_ref, weight_ref, near_ref, *rest
+):
+    groups = dict(zip(steps, rest[: len(steps)]))
+    potential_ref = rest[len(steps)]
+    out_groups = dict(zip(steps, rest[len(steps) + 1 :]))
+    slots = tile_slots(pick_ref, me_ref[0], steps, devices, capacity)
+    total = pair_density(slots, near_ref[...], full, table_ref, groups)
     valence = jnp.sum(total, axis=0, keepdims=True)
     value = jnp.maximum(core_ref[...] + valence, density_floor)
     root = jnp.exp(jnp.log(value) * (1.0 / 3.0))
     root = root - (root * root * root - value) / (3.0 * root * root)
     potential = -slater_factor * root
     potential_ref[...] = potential
-    scaled = weight_ref[...] * potential
-    for k, c, u, v in slots:
-        left = table_ref[jnp.maximum(u, 0)].astype(jnp.float32)
-        right = table_ref[jnp.maximum(v, 0)]
-        weighted = (left * scaled).astype(jnp.bfloat16)
-        out_refs[k][c] = lax.dot_general(
-            weighted, right, (((1,), (1,)), ((), ())), preferred_element_type=jnp.float32
-        ).astype(jnp.bfloat16)
+    pair_partials(slots, weight_ref[...] * potential, table_ref, out_groups)
+
+
+def near_partials_kernel(
+    devices, capacity, steps, me_ref, pick_ref, table_ref, weight_ref, found_ref, *rest
+):
+    out_groups = dict(zip(steps, rest))
+    potential_ref = rest[len(steps)]
+    potential_ref[...] = found_ref[...]
+    slots = tile_slots(pick_ref, me_ref[0], steps, devices, capacity)
+    pair_partials(slots, weight_ref[...] * found_ref[...], table_ref, out_groups)
 
 
 def sum_kernel(devices, capacity, dest_ref, me_ref, *rest):
@@ -259,24 +286,61 @@
             flops=4 * order**3, bytes_accessed=4 * order * order, transcendentals=0
         ),
     )(place, chem_pot, destinations, me, blocks)
-    density, outgoing = out[0], out[1:]
+    column = out[0]
+    outgoing = dict(enumerate(out[1:]))
+    near, far = range(min(2, devices)), range(min(2, devices), devices)
     incoming = exchange(outgoing, 1)
     tables = basis_values[0, 0]
     points = tables.shape[-1]
-    out = pl.pallas_call(
-        functools.partial(grid_kernel, devices, capacity, devices * capacity == send_count),
-        name="grid",
-        in_specs=[SMEM] * 2 + [VMEM] * (3 + devices),
-        out_shape=[jax.ShapeDtypeStruct((1, points), jnp.float32)] + [group] * devices,
-        out_specs=[VMEM] * (1 + devices),
-        compiler_params=pltpu.CompilerParams(vmem_limit_bytes=24 << 20),
-        cost_estimate=pl.CostEstimate(
-            flops=4 * devices * capacity * block_width**2 * points,
-            bytes_accessed=2 * tables.size,
-            transcendentals=2 * points,
-        ),
-    )(me, tile_pairs[0, 0], tables, core_density[0], point_weights[0], *incoming)
-    potential, partials = out[0], out[1:]
+    full = devices * capacity == send_count
+    pick = tile_pairs[0, 0]
+    row = jax.ShapeDtypeStruct((1, points), jnp.float32)
+
+    def cost(pairs):
+        return pl.CostEstimate(
+            flops=2 * pairs * block_width**2 * points,
+            bytes_accessed=4 * pairs * block_width * points,
+            transcendentals=0,
+        )
+
+    limit = pltpu.CompilerParams(vmem_limit_bytes=16 << 20)
+    total, density = pl.pallas_call(
+        functools.partial(near_density_kernel, devices, capacity, full, near),
+        name="near_density",
+        in_specs=[SMEM] * 2 + [VMEM] * (2 + len(near)),
+        out_shape=[jax.ShapeDtypeStruct((8, points), jnp.float32), column],
+        out_specs=[VMEM] * 2,
+        compiler_params=limit,
+        cost_estimate=cost(len(near) * capacity),
+    )(me, pick, tables, column, *[incoming[k] for k in near])
+    found, *sent = pl.pallas_call(
+        functools.partial(far_kernel, devices, capacity, full, far),
+        name="far",
+        in_specs=[SMEM] * 2 + [VMEM] * (4 + len(far)),
+        out_shape=[row] + [group] * len(far),
+        out_specs=[VMEM] * (1 + len(far)),
+        compiler_params=limit,
+        cost_estimate=cost(2 * len(far) * capacity),
+    )(
+        me,
+        pick,
+        tables,
+        core_density[0],
+        point_weights[0],
+        total,
+        *[incoming[k] for k in far],
+    )
+    partials = dict(zip(far, sent))
+    *sent, potential = pl.pallas_call(
+        functools.partial(near_partials_kernel, devices, capacity, near),
+        name="near_partials",
+        in_specs=[SMEM] * 2 + [VMEM] * 3,
+        out_shape=[group] * len(near) + [row],
+        out_specs=[VMEM] * (len(near) + 1),
+        compiler_params=limit,
+        cost_estimate=cost(len(near) * capacity),
+    )(me, pick, tables, point_weights[0], found)
+    partials.update(zip(near, sent))
     returned = exchange(partials, -1)
     kohn = pl.pallas_call(
         functools.partial(sum_kernel, devices, capacity),
@@ -288,7 +352,7 @@
             pltpu.VMEM((devices * capacity, block_width, block_width), jnp.bfloat16),
         ],
         compiler_params=pltpu.CompilerParams(vmem_limit_bytes=8 << 20),
-    )(destinations, me, *returned)
+    )(destinations, me, *[returned[k] for k in range(devices)])
     return (density[None, None], potential[None], kohn[None, None])
 
 
@@ -303,6 +367,7 @@
         P("atoms", "space", None),
         P("atoms", "space", None, None),
     )
+
     return jax.shard_map(
         per_device,
         mesh=mesh,

time: 46.9 us -> 47.7 us (1.017)
  Pallas kernels: 9.62 us -> 11 us
  waiting for transfers between devices: 18.9 us -> 18.3 us
    pallas_call x1 -> x3, Pallas kernels: 3.01 us -> 5.08 us  [the longest x1 1.75 us: per_device(): pl.pallas_call(functools.partial(near_density_kernel, devices, capacity,...]
    pallas_call x1, Pallas kernels: 5.21 us -> 4.56 us  [per_device(): pl.pallas_call(functools.partial(sign_kernel, devices, capacity), name='s...]
    ppermute x13, waiting for transfers between devices: 18.9 us -> 18.3 us  [the longest x7 10 us: gathered_blocks(): parts[offset] = lax.ppermute(parts[offset ^ step], 'atoms', pairs)]
  transfers between devices with their start and end apart: 13 -> 13, of which waited for: 7 -> 7; matrix products, arithmetic and copies ran while one was open for 4% -> 4% of each run, Pallas kernels for 0% -> 4%
where the time goes in v2:
time: 47.7 us; the launch traced here: 47.6 us
  waiting for transfers between devices  18.3 us (38%)
  starting transfers between devices  15.1 us (32%)
  Pallas kernels  11 us (23%)
  between operations  1.44 us (3%)
  local copies, waits for them, and re-layouts  1.11 us (2%)
  other arithmetic  0.67 us (1%)
    ppermute x7, starting transfers between devices, gathered_blocks(): parts[offset] = lax.ppermute(parts[offset ^ step], 'atoms', pairs)  11.3 us
    ppermute x7, waiting for transfers between devices, gathered_blocks(): parts[offset] = lax.ppermute(parts[offset ^ step], 'atoms', pairs)  10 us
    ppermute x6, waiting for transfers between devices, exchange(): lax.ppermute(groups[step], 'space', pairs)  8.24 us
    pallas_call x1, Pallas kernels, per_device(): pl.pallas_call(functools.partial(sign_kernel, devices, capacity), name='s...  4.56 us
    ppermute x6, starting transfers between devices, exchange(): lax.ppermute(groups[step], 'space', pairs)  3.78 us
    pallas_call x1, Pallas kernels, per_device(): pl.pallas_call(functools.partial(near_density_kernel, devices, capacity,...  1.75 us
    pallas_call x1, Pallas kernels, per_device(): pl.pallas_call(functools.partial(far_kernel, devices, capacity, full, far...  1.72 us
    pallas_call x1, Pallas kernels, per_device(): pl.pallas_call(functools.partial(near_partials_kernel, devices, capacity,...  1.61 us
  transfers between devices with their start and end apart: 13, of which 7 were waited for; matrix products, arithmetic and copies ran while one was open for 4% of the time, Pallas kernels for 4%

profile of v2, /device:TPU:0, one launch (start us, length us, event | category | flops | bytes accessed | tf_op | source)
XLA Modules:
  0.0 47.6 jit_solution(14765029983701389116)
XLA Ops:
  0.6 3.1 %collective-permute-start = (bf16[4,128,128]{2,1,0:T(8,128)(2,1)}, bf16[4,128,128]{2,1,0:T(8,128)(2,1)S(1)}, u32[]{:S(2)}, u32[]{:S(2)}) collective-permute-start(bf16[4,128,128]{2,1,0:T(8,128)(2,1)} %bitcast.36), channel_id=1, source_target_pairs={{0,4},{4,0},{8,12},{12,8},{16,20},{20,16},{24,28},{28,24},{1,5},{5... | collective-permute-start | bytes 393224 | tf_op jit(solution)/shard_map/ppermute | solution.py:59
  3.7 1.6 %collective-permute-start.1 = (bf16[4,128,128]{2,1,0:T(8,128)(2,1)}, bf16[4,128,128]{2,1,0:T(8,128)(2,1)S(1)}, u32[]{:S(2)}, u32[]{:S(2)}) collective-permute-start(bf16[4,128,128]{2,1,0:T(8,128)(2,1)} %bitcast.37), channel_id=1, source_target_pairs={{0,8},{4,12},{8,0},{12,4},{16,24},{20,28},{24,16},{28,20},{1,9},{5... | collective-permute-start | bytes 393224 | tf_op jit(solution)/shard_map/ppermute | solution.py:59
  5.3 2.6 %collective-permute-start.3 = (bf16[4,128,128]{2,1,0:T(8,128)(2,1)}, bf16[4,128,128]{2,1,0:T(8,128)(2,1)S(1)}, u32[]{:S(2)}, u32[]{:S(2)}) collective-permute-start(bf16[4,128,128]{2,1,0:T(8,128)(2,1)} %bitcast.38), channel_id=1, source_target_pairs={{0,16},{4,20},{8,24},{12,28},{16,0},{20,4},{24,8},{28,12},{1,17},{... | collective-permute-start | bytes 393224 | tf_op jit(solution)/shard_map/ppermute | solution.py:59
  7.9 0.9 %constant_dynamic-update-slice_fusion.7 = bf16[32,128,128]{2,1,0:T(8,128)(2,1)S(1)} fusion(bf16[1,4,128,128]{3,2,1,0:T(8,128)(2,1)} %param.8), kind=kLoop, calls=%fused_computation.7 | loop fusion | bytes 262144
  8.8 0.7 %fusion.place_ref = s32[36]{0:T(128)S(1)} fusion(s32[1,1,36]{2,1,0:T(1,128)} %param.9, s32[]{:T(128)S(6)} %axis_index.25), kind=kLoop, calls=%fused_computation.13 | loop fusion | flops 792 | bytes 292 | tf_op jit(solution)/shard_map/add | solution.py:61
  10.1 3.8 %collective-permute-done.3 = bf16[4,128,128]{2,1,0:T(8,128)(2,1)S(1)} collective-permute-done((bf16[4,128,128]{2,1,0:T(8,128)(2,1)}, bf16[4,128,128]{2,1,0:T(8,128)(2,1)S(1)}, u32[]{:S(2)}, u32[]{:S(2)}) %collective-permute-start.3) | collective-permute-done | bytes 131104 | tf_op jit(solution)/shard_map/ppermute | solution.py:59
  14.0 0.5 %collective-permute-start.4 = (bf16[4,128,128]{2,1,0:T(8,128)(2,1)S(1)}, bf16[4,128,128]{2,1,0:T(8,128)(2,1)S(1)}, u32[]{:S(2)}, u32[]{:S(2)}) collective-permute-start(bf16[4,128,128]{2,1,0:T(8,128)(2,1)S(1)} %collective-permute-done.3), channel_id=1, source_target_pairs={{0,4},{4,0},{8,12},{12,8},{16,20},{20,16},{24,28},{28,24},{1,5},{5... | collective-permute-start | bytes 393224 | tf_op jit(solution)/shard_map/ppermute | solution.py:59
  14.4 0.3 collective-permute-start.5
  14.8 0.0 collective-permute-done
  14.8 1.7 %collective-permute-start.2 = (bf16[4,128,128]{2,1,0:T(8,128)(2,1)S(1)}, bf16[4,128,128]{2,1,0:T(8,128)(2,1)S(1)}, u32[]{:S(2)}, u32[]{:S(2)}) collective-permute-start(bf16[4,128,128]{2,1,0:T(8,128)(2,1)S(1)} %collective-permute-done), channel_id=1, source_target_pairs={{0,8},{4,12},{8,0},{12,4},{16,24},{20,28},{24,16},{28,20},{1,9},{5... | collective-permute-start | bytes 393224 | tf_op jit(solution)/shard_map/ppermute | solution.py:59
  16.5 2.9 %collective-permute-done.5 = bf16[4,128,128]{2,1,0:T(8,128)(2,1)S(1)} collective-permute-done((bf16[4,128,128]{2,1,0:T(8,128)(2,1)S(1)}, bf16[4,128,128]{2,1,0:T(8,128)(2,1)S(1)}, u32[]{:S(2)}, u32[]{:S(2)}) %collective-permute-start.5) | collective-permute-done | bytes 131104 | tf_op jit(solution)/shard_map/ppermute | solution.py:59
  19.4 1.5 %collective-permute-start.6 = (bf16[4,128,128]{2,1,0:T(8,128)(2,1)S(1)}, bf16[4,128,128]{2,1,0:T(8,128)(2,1)S(1)}, u32[]{:S(2)}, u32[]{:S(2)}) collective-permute-start(bf16[4,128,128]{2,1,0:T(8,128)(2,1)S(1)} %collective-permute-done.5), channel_id=1, source_target_pairs={{0,4},{4,0},{8,12},{12,8},{16,20},{20,16},{24,28},{28,24},{1,5},{5... | collective-permute-start | bytes 393224 | tf_op jit(solution)/shard_map/ppermute | solution.py:59
  20.9 0.0 collective-permute-done.2
  21.1 3.3 %collective-permute-done.6 = bf16[4,128,128]{2,1,0:T(8,128)(2,1)S(1)} collective-permute-done((bf16[4,128,128]{2,1,0:T(8,128)(2,1)S(1)}, bf16[4,128,128]{2,1,0:T(8,128)(2,1)S(1)}, u32[]{:S(2)}, u32[]{:S(2)}) %collective-permute-start.6) | collective-permute-done | bytes 131104 | tf_op jit(solution)/shard_map/ppermute | solution.py:59
  24.4 0.0 copy-start
  24.4 0.0 copy-start.2
  24.4 4.6 %sign.13 = (bf16[768,128]{1,0:T(8,128)(2,1)S(1)}, bf16[3,128,128]{2,1,0:T(8,128)(2,1)S(1)}, bf16[3,128,128]{2,1,0:T(8,128)(2,1)S(1)}, bf16[3,128,128]{2,1,0:T(8,128)(2,1)S(1)}, bf16[3,128,128]{2,1,0:T(8,128)(2,1)S(1)}) custom-call(s32[36]{0:T(128)S(1)} %fusion.place_ref, f32[1]{0:T(128)S(6)} %copy.18.chem_ref, s32[12]{0:T(128)S(1)} %bitcast.33, ...), custom_call_target="tpu_custom_call" | custom-call | flops 1811939328 | bytes 2359296 | tf_op jit(solution)/shard_map/sign/pallas_call | solution.py:271
  29.0 0.0 copy-start.1
  29.0 0.0 copy-start.3
  29.0 0.1 collective-permute-start.7
  29.1 1.6 %collective-permute-start.8 = (bf16[3,128,128]{2,1,0:T(8,128)(2,1)S(1)}, bf16[3,128,128]{2,1,0:T(8,128)(2,1)S(1)}, u32[]{:S(2)}, u32[]{:S(2)}) collective-permute-start(bf16[3,128,128]{2,1,0:T(8,128)(2,1)S(1)} %get-tuple-element.21), channel_id=1, source_target_pairs={{0,2},{1,3},{2,0},{3,1},{4,6},{5,7},{6,4},{7,5},{8,10},{9,11},{10,... | collective-permute-start | bytes 294920 | tf_op jit(solution)/shard_map/ppermute | solution.py:88
  30.7 0.3 collective-permute-start.9
  31.0 1.7 %near_density.1 = (f32[8,1024]{1,0:T(8,128)S(1)}, bf16[768,128]{1,0:T(8,128)(2,1)}) custom-call(s32[1]{0:T(128)} %bitcast.me_ref, s32[2,12]{1,0:T(2,128)S(1)} %bitcast.29, bf16[8,128,1024]{2,1,0:T(8,128)(2,1)S(1)} %bitcast.24, bf16[768,128]{1,0:T(8,128)(2,1)S(1)} %get-tuple-element.16.column_ref, bf16[3,128,128]{2,1,0:T(8,128)(2,1)S(1)} %get-tuple-element.17.rest_0_, ...), custom_call_target="tpu_custom_call" | custom-call | flops 201326592 | bytes 3145728 | tf_op jit(solution)/shard_map/near_density/pallas_call | solution.py:307
  32.7 2.1 %collective-permute-done.8.rest_0_ = bf16[3,128,128]{2,1,0:T(8,128)(2,1)S(1)} collective-permute-done((bf16[3,128,128]{2,1,0:T(8,128)(2,1)S(1)}, bf16[3,128,128]{2,1,0:T(8,128)(2,1)S(1)}, u32[]{:S(2)}, u32[]{:S(2)}) %collective-permute-start.8) | collective-permute-done | bytes 98336 | tf_op jit(solution)/shard_map/ppermute | solution.py:88
  34.8 1.0 %collective-permute-done.9.rest_1_ = bf16[3,128,128]{2,1,0:T(8,128)(2,1)S(1)} collective-permute-done((bf16[3,128,128]{2,1,0:T(8,128)(2,1)S(1)}, bf16[3,128,128]{2,1,0:T(8,128)(2,1)S(1)}, u32[]{:S(2)}, u32[]{:S(2)}) %collective-permute-start.9) | collective-permute-done | bytes 98336 | tf_op jit(solution)/shard_map/ppermute | solution.py:88
  35.9 1.7 %far.1 = (f32[1,1024]{1,0:T(1,128)S(1)}, bf16[3,128,128]{2,1,0:T(8,128)(2,1)S(1)}, bf16[3,128,128]{2,1,0:T(8,128)(2,1)S(1)}) custom-call(s32[1]{0:T(128)} %bitcast.me_ref, s32[2,12]{1,0:T(2,128)S(1)} %bitcast.30, bf16[8,128,1024]{2,1,0:T(8,128)(2,1)S(1)} %bitcast.25, f32[1,1024]{1,0:T(1,128)S(1)} %bitcast.32, f32[1,1024]{1,0:T(1,128)S(1)} %bitcast.27, ...), custom_call_target="tpu_custom_call" | custom-call | flops 402653184 | bytes 6291456 | tf_op jit(solution)/shard_map/far/pallas_call | solution.py:316
  37.6 1.6 %near_partials.1 = (bf16[3,128,128]{2,1,0:T(8,128)(2,1)S(1)}, bf16[3,128,128]{2,1,0:T(8,128)(2,1)S(1)}, f32[1,1024]{1,0:T(1,128)}) custom-call(s32[1]{0:T(128)} %bitcast.me_ref, s32[2,12]{1,0:T(2,128)S(1)} %bitcast.31, bf16[8,128,1024]{2,1,0:T(8,128)(2,1)S(1)} %bitcast.26, f32[1,1024]{1,0:T(1,128)S(1)} %bitcast.28, f32[1,1024]{1,0:T(1,128)S(1)} %get-tuple-element.23.found_ref), custom_call_target="tpu_custom_call" | custom-call | flops 201326592 | bytes 3145728 | tf_op jit(solution)/shard_map/near_partials/pallas_call | solution.py:334
  39.2 0.4 collective-permute-start.10
  39.6 1.5 %collective-permute-start.11 = (bf16[3,128,128]{2,1,0:T(8,128)(2,1)S(1)}, bf16[3,128,128]{2,1,0:T(8,128)(2,1)S(1)}, u32[]{:S(2)}, u32[]{:S(2)}) collective-permute-start(bf16[3,128,128]{2,1,0:T(8,128)(2,1)S(1)} %get-tuple-element.27), channel_id=1, source_target_pairs={{0,2},{1,3},{2,0},{3,1},{4,6},{5,7},{6,4},{7,5},{8,10},{9,11},{10,... | collective-permute-start | bytes 294920 | tf_op jit(solution)/shard_map/ppermute | solution.py:88
  41.1 3.7 %collective-permute-done.11.rest_2_ = bf16[3,128,128]{2,1,0:T(8,128)(2,1)S(1)} collective-permute-done((bf16[3,128,128]{2,1,0:T(8,128)(2,1)S(1)}, bf16[3,128,128]{2,1,0:T(8,128)(2,1)S(1)}, u32[]{:S(2)}, u32[]{:S(2)}) %collective-permute-start.11) | collective-permute-done | bytes 98336 | tf_op jit(solution)/shard_map/ppermute | solution.py:88
  44.8 1.4 %collective-permute-done.12.rest_3_ = bf16[3,128,128]{2,1,0:T(8,128)(2,1)S(1)} collective-permute-done((bf16[3,128,128]{2,1,0:T(8,128)(2,1)S(1)}, bf16[3,128,128]{2,1,0:T(8,128)(2,1)S(1)}, u32[]{:S(2)}, u32[]{:S(2)}) %collective-permute-start.12) | collective-permute-done | bytes 98336 | tf_op jit(solution)/shard_map/ppermute | solution.py:88
  46.2 1.4 %sum.1 = f32[768,128]{1,0:T(8,128)} custom-call(s32[12]{0:T(128)S(1)} %bitcast.34, s32[1]{0:T(128)} %bitcast.me_ref, bf16[3,128,128]{2,1,0:T(8,128)(2,1)S(1)} %get-tuple-element.25.rest_0_, bf16[3,128,128]{2,1,0:T(8,128)(2,1)S(1)} %collective-permute-done.10.rest_1_, bf16[3,128,128]{2,1,0:T(8,128)(2,1)S(1)} %collective-permute-done.11.rest_2_, ...), custom_call_target="tpu_custom_call" | custom-call | tf_op jit(solution)/shard_map/sum/pallas_call | solution.py:345
  (18 shorter events, 0.2 us)
Async XLA Ops:
  0.6 23.8 %copy-start.4 = (s32[1,1,12]{2,1,0:T(1,128)S(1)}, s32[1,1,12]{2,1,0:T(1,128)}, u32[]{:S(2)}) copy-start(s32[1,1,12]{2,1,0:T(1,128)} %param.14) | copy-start | bytes 148
  0.6 14.1 %collective-permute-start = (bf16[4,128,128]{2,1,0:T(8,128)(2,1)}, bf16[4,128,128]{2,1,0:T(8,128)(2,1)S(1)}, u32[]{:S(2)}, u32[]{:S(2)}) collective-permute-start(bf16[4,128,128]{2,1,0:T(8,128)(2,1)} %bitcast.36), channel_id=1, source_target_pairs={{0,4},{4,0},{8,12},{12,8},{16,20},{20,16},{24,28},{28,24},{1,5},{5... | collective-permute-start | bytes 393224 | tf_op jit(solution)/shard_map/ppermute | solution.py:59
  3.7 12.8 %collective-permute-start.1 = (bf16[4,128,128]{2,1,0:T(8,128)(2,1)}, bf16[4,128,128]{2,1,0:T(8,128)(2,1)S(1)}, u32[]{:S(2)}, u32[]{:S(2)}) collective-permute-start(bf16[4,128,128]{2,1,0:T(8,128)(2,1)} %bitcast.37), channel_id=1, source_target_pairs={{0,8},{4,12},{8,0},{12,4},{16,24},{20,28},{24,16},{28,20},{1,9},{5... | collective-permute-start | bytes 393224 | tf_op jit(solution)/shard_map/ppermute | solution.py:59
  5.3 8.7 %collective-permute-start.3 = (bf16[4,128,128]{2,1,0:T(8,128)(2,1)}, bf16[4,128,128]{2,1,0:T(8,128)(2,1)S(1)}, u32[]{:S(2)}, u32[]{:S(2)}) collective-permute-start(bf16[4,128,128]{2,1,0:T(8,128)(2,1)} %bitcast.38), channel_id=1, source_target_pairs={{0,16},{4,20},{8,24},{12,28},{16,0},{20,4},{24,8},{28,12},{1,17},{... | collective-permute-start | bytes 393224 | tf_op jit(solution)/shard_map/ppermute | solution.py:59
  14.0 7.1 %collective-permute-start.4 = (bf16[4,128,128]{2,1,0:T(8,128)(2,1)S(1)}, bf16[4,128,128]{2,1,0:T(8,128)(2,1)S(1)}, u32[]{:S(2)}, u32[]{:S(2)}) collective-permute-start(bf16[4,128,128]{2,1,0:T(8,128)(2,1)S(1)} %collective-permute-done.3), channel_id=1, source_target_pairs={{0,4},{4,0},{8,12},{12,8},{16,20},{20,16},{24,28},{28,24},{1,5},{5... | collective-permute-start | bytes 393224 | tf_op jit(solution)/shard_map/ppermute | solution.py:59
  14.4 5.0 %collective-permute-start.5 = (bf16[4,128,128]{2,1,0:T(8,128)(2,1)S(1)}, bf16[4,128,128]{2,1,0:T(8,128)(2,1)S(1)}, u32[]{:S(2)}, u32[]{:S(2)}) collective-permute-start(bf16[4,128,128]{2,1,0:T(8,128)(2,1)S(1)} %collective-permute-done.3), channel_id=1, source_target_pairs={{0,8},{4,12},{8,0},{12,4},{16,24},{20,28},{24,16},{28,20},{1,9},{5... | collective-permute-start | bytes 393224 | tf_op jit(solution)/shard_map/ppermute | solution.py:59
  14.8 6.2 %collective-permute-start.2 = (bf16[4,128,128]{2,1,0:T(8,128)(2,1)S(1)}, bf16[4,128,128]{2,1,0:T(8,128)(2,1)S(1)}, u32[]{:S(2)}, u32[]{:S(2)}) collective-permute-start(bf16[4,128,128]{2,1,0:T(8,128)(2,1)S(1)} %collective-permute-done), channel_id=1, source_target_pairs={{0,8},{4,12},{8,0},{12,4},{16,24},{20,28},{24,16},{28,20},{1,9},{5... | collective-permute-start | bytes 393224 | tf_op jit(solution)/shard_map/ppermute | solution.py:59
  19.4 5.0 %collective-permute-start.6 = (bf16[4,128,128]{2,1,0:T(8,128)(2,1)S(1)}, bf16[4,128,128]{2,1,0:T(8,128)(2,1)S(1)}, u32[]{:S(2)}, u32[]{:S(2)}) collective-permute-start(bf16[4,128,128]{2,1,0:T(8,128)(2,1)S(1)} %collective-permute-done.5), channel_id=1, source_target_pairs={{0,4},{4,0},{8,12},{12,8},{16,20},{20,16},{24,28},{28,24},{1,5},{5... | collective-permute-start | bytes 393224 | tf_op jit(solution)/shard_map/ppermute | solution.py:59
  24.4 6.5 %copy-start = (bf16[1,1,8,128,1024]{4,3,2,1,0:T(8,128)(2,1)S(1)}, bf16[1,1,8,128,1024]{4,3,2,1,0:T(8,128)(2,1)}, u32[]{:S(2)}) copy-start(bf16[1,1,8,128,1024]{4,3,2,1,0:T(8,128)(2,1)} %param.11) | copy-start | bytes 6291460
  24.4 6.5 %copy-start.2 = (s32[1,1,2,12]{3,2,1,0:T(2,128)S(1)}, s32[1,1,2,12]{3,2,1,0:T(2,128)}, u32[]{:S(2)}) copy-start(s32[1,1,2,12]{3,2,1,0:T(2,128)} %param.15) | copy-start | bytes 292
  29.0 6.9 %copy-start.1 = (f32[1,1,1024]{2,1,0:T(1,128)S(1)}, f32[1,1,1024]{2,1,0:T(1,128)}, u32[]{:S(2)}) copy-start(f32[1,1,1024]{2,1,0:T(1,128)} %param.13) | copy-start | bytes 12292
  29.0 6.9 %copy-start.3 = (f32[1,1,1024]{2,1,0:T(1,128)S(1)}, f32[1,1,1024]{2,1,0:T(1,128)}, u32[]{:S(2)}) copy-start(f32[1,1,1024]{2,1,0:T(1,128)} %param.12) | copy-start | bytes 12292
  29.0 1.9 %collective-permute-start.7 = (bf16[3,128,128]{2,1,0:T(8,128)(2,1)S(1)}, bf16[3,128,128]{2,1,0:T(8,128)(2,1)S(1)}, u32[]{:S(2)}, u32[]{:S(2)}) collective-permute-start(bf16[3,128,128]{2,1,0:T(8,128)(2,1)S(1)} %get-tuple-element.18), channel_id=1, source_target_pairs={{0,1},{1,0},{2,3},{3,2},{4,5},{5,4},{6,7},{7,6},{8,9},{9,8},{10,11... | collective-permute-start | bytes 294920 | tf_op jit(solution)/shard_map/ppermute | solution.py:88
  29.1 5.7 %collective-permute-start.8 = (bf16[3,128,128]{2,1,0:T(8,128)(2,1)S(1)}, bf16[3,128,128]{2,1,0:T(8,128)(2,1)S(1)}, u32[]{:S(2)}, u32[]{:S(2)}) collective-permute-start(bf16[3,128,128]{2,1,0:T(8,128)(2,1)S(1)} %get-tuple-element.21), channel_id=1, source_target_pairs={{0,2},{1,3},{2,0},{3,1},{4,6},{5,7},{6,4},{7,5},{8,10},{9,11},{10,... | collective-permute-start | bytes 294920 | tf_op jit(solution)/shard_map/ppermute | solution.py:88
  30.7 5.2 %collective-permute-start.9 = (bf16[3,128,128]{2,1,0:T(8,128)(2,1)S(1)}, bf16[3,128,128]{2,1,0:T(8,128)(2,1)S(1)}, u32[]{:S(2)}, u32[]{:S(2)}) collective-permute-start(bf16[3,128,128]{2,1,0:T(8,128)(2,1)S(1)} %get-tuple-element.22), channel_id=1, source_target_pairs={{0,3},{1,2},{2,1},{3,0},{4,7},{5,6},{6,5},{7,4},{8,11},{9,10},{10,... | collective-permute-start | bytes 294920 | tf_op jit(solution)/shard_map/ppermute | solution.py:88
  39.2 1.9 %collective-permute-start.10 = (bf16[3,128,128]{2,1,0:T(8,128)(2,1)S(1)}, bf16[3,128,128]{2,1,0:T(8,128)(2,1)S(1)}, u32[]{:S(2)}, u32[]{:S(2)}) collective-permute-start(bf16[3,128,128]{2,1,0:T(8,128)(2,1)S(1)} %get-tuple-element.26), channel_id=1, source_target_pairs={{0,1},{1,0},{2,3},{3,2},{4,5},{5,4},{6,7},{7,6},{8,9},{9,8},{10,11... | collective-permute-start | bytes 294920 | tf_op jit(solution)/shard_map/ppermute | solution.py:88
  39.6 5.2 %collective-permute-start.11 = (bf16[3,128,128]{2,1,0:T(8,128)(2,1)S(1)}, bf16[3,128,128]{2,1,0:T(8,128)(2,1)S(1)}, u32[]{:S(2)}, u32[]{:S(2)}) collective-permute-start(bf16[3,128,128]{2,1,0:T(8,128)(2,1)S(1)} %get-tuple-element.27), channel_id=1, source_target_pairs={{0,2},{1,3},{2,0},{3,1},{4,6},{5,7},{6,4},{7,5},{8,10},{9,11},{10,... | collective-permute-start | bytes 294920 | tf_op jit(solution)/shard_map/ppermute | solution.py:88
  41.1 5.1 %collective-permute-start.12 = (bf16[3,128,128]{2,1,0:T(8,128)(2,1)S(1)}, bf16[3,128,128]{2,1,0:T(8,128)(2,1)S(1)}, u32[]{:S(2)}, u32[]{:S(2)}) collective-permute-start(bf16[3,128,128]{2,1,0:T(8,128)(2,1)S(1)} %get-tuple-element.28), channel_id=1, source_target_pairs={{0,3},{1,2},{2,1},{3,0},{4,7},{5,6},{6,5},{7,4},{8,11},{9,10},{10,... | collective-permute-start | bytes 294920 | tf_op jit(solution)/shard_map/ppermute | solution.py:88

commit v3 on v2

--- a/solution.py
+++ b/solution.py
@@ -47,19 +47,18 @@
     return arrived.reshape(atom_devices * capacity, block_width, block_width), slot_index
 
 
-def gathered_blocks(stored, source):
-    held_count, _, _ = stored.shape
-    atom_devices = lax.axis_size("atoms")
-    if atom_devices & (atom_devices - 1):
-        return lax.all_gather(stored, "atoms", axis=0, tiled=True), source
-    parts = [stored] + [None] * (atom_devices - 1)
-    for offset in sorted(range(1, atom_devices), key=lambda r: (r.bit_count(), -r)):
+def gather_order(devices):
+    return sorted(range(1, devices), key=lambda r: (r.bit_count(), -r))
+
+
+def gathered_blocks(stored):
+    devices = lax.axis_size("atoms")
+    parts = [stored] + [None] * (devices - 1)
+    for offset in gather_order(devices):
         step = 2 if offset == 3 else offset & -offset
-        pairs = [(i, i ^ step) for i in range(atom_devices)]
+        pairs = [(i, i ^ step) for i in range(devices)]
         parts[offset] = lax.ppermute(parts[offset ^ step], "atoms", pairs)
-    me = lax.axis_index("atoms")
-    place = (me ^ (source // held_count)) * held_count + source % held_count
-    return jnp.concatenate(parts, axis=0), place
+    return jnp.concatenate(parts, axis=0)
 
 
 def partner(me, step, devices):
@@ -89,20 +88,46 @@
     return got
 
 
-def pair_places(dest_ref, me, devices, capacity):
-    sends = dest_ref.shape[0]
-    dests = [dest_ref[j] for j in range(sends)]
-    places = []
-    for j in range(sends):
+def index_kernel(
+    devices, capacity, held, slots, sends, table_ref, atom_ref, me_ref, chem_ref, row_ref, level_ref
+):
+    me = me_ref[0]
+    table = table_ref[...]
+    values = []
+    for j in range(slots):
+        place = table[0, j]
+        if held:
+            place = (atom_ref[0] ^ lax.div(place, held)) * held + lax.rem(place, held)
+        values.append(place)
+    dests = [table[0, slots + j] for j in range(sends)]
+    for j, dest in enumerate(dests):
         rank = jnp.int32(0)
-        for earlier in range(j):
-            rank += jnp.where(dests[earlier] == dests[j], 1, 0)
-        places.append(step_to(me, dests[j], devices) * capacity + rank)
-    return places
+        for earlier in dests[:j]:
+            rank += jnp.where(earlier == dest, 1, 0)
+        values.append(step_to(me, dest, devices) * capacity + rank)
+    for k in range(devices):
+        owner = step_from(me, k, devices)
+        for c in range(capacity):
+            for side in range(2):
+                at = slots + sends + side * devices * capacity
+                value = table[0, at]
+                for slot in range(1, devices * capacity):
+                    value = jnp.where(owner * capacity + c == slot, table[0, at + slot], value)
+                values.append(value)
+    lanes = lax.broadcasted_iota(jnp.int32, row_ref.shape, 1)
+    row = jnp.zeros(row_ref.shape, jnp.int32)
+    for j, value in enumerate(values):
+        row = jnp.where(lanes == j, value, row)
+    row_ref[...] = row
+    level_ref[...] = jnp.full(level_ref.shape, chem_ref[0], jnp.float32)
+
+
+def pair_places(row, sends):
+    return [row[0, KB * KB + j] for j in range(sends)]
 
 
 def sign_kernel(
-    devices, capacity, place_ref, chem_ref, dest_ref, me_ref, block_ref, density_ref, *rest
+    devices, capacity, row_ref, level_ref, block_ref, density_ref, *rest
 ):
     out_refs = rest[:devices]
     shifted, x_zero, t_one, x_one, pairs = rest[devices:]
@@ -112,7 +137,8 @@
     cols = lax.broadcasted_iota(jnp.int32, (width, width), 1)
     diagonal = rows == cols
     unit = jnp.where(diagonal, 1.0, 0.0)
-    chem = chem_ref[0]
+    level = level_ref[...] * unit
+    row = row_ref[...]
 
     def at(i):
         return pl.ds(i * width, width)
@@ -120,11 +146,11 @@
     total = jnp.zeros((8, width), jnp.float32)
     tiles = [(i, j) for i in range(KB) for j in range(i, KB)]
     for i, j in tiles:
-        upper = block_ref[place_ref[i * KB + j]].astype(jnp.float32)
-        lower = block_ref[place_ref[j * KB + i]].astype(jnp.float32)
+        upper = block_ref[row[0, i * KB + j]].astype(jnp.float32)
+        lower = block_ref[row[0, j * KB + i]].astype(jnp.float32)
         value = 0.5 * (upper + lower.T)
         if i == j:
-            value = value - chem * unit
+            value = value - level
         shifted[at(i), at(j)] = value
         squares = (value * value).reshape(width // 8, 8, width).sum(axis=0)
         total = total + (squares if i == j else 2.0 * squares)
@@ -154,20 +180,19 @@
     for i in range(KB):
         part = final[i * width : (i + 1) * width]
         density_ref[at(i), :] = (0.5 * (unit - part if i == 0 else -part)).astype(jnp.bfloat16)
-    places = pair_places(dest_ref, me_ref[0], devices, capacity)
+    places = pair_places(row, 2 * KB)
     for j, place in enumerate(places):
         pairs[place] = density_ref[at(j // 2), :]
     for k in range(devices):
         out_refs[k][...] = pairs[k * capacity : (k + 1) * capacity]
 
 
-def tile_slots(pick_ref, me, steps, devices, capacity):
+def tile_slots(row, steps, capacity):
     slots = []
     for k in steps:
-        owner = step_from(me, k, devices)
         for c in range(capacity):
-            slot = owner * capacity + c
-            slots.append((k, c, pick_ref[0, slot], pick_ref[1, slot]))
+            at = KB * KB + 2 * KB + 2 * (k * capacity + c)
+            slots.append((k, c, row[0, at], row[0, at + 1]))
     return slots
 
 
@@ -193,23 +218,23 @@
 
 
 def near_density_kernel(
-    devices, capacity, full, steps, me_ref, pick_ref, table_ref, column_ref, *rest
+    capacity, full, steps, row_ref, table_ref, column_ref, *rest
 ):
     groups = dict(zip(steps, rest[: len(steps)]))
     total_ref, density_ref = rest[len(steps) :]
     density_ref[...] = column_ref[...]
-    slots = tile_slots(pick_ref, me_ref[0], steps, devices, capacity)
+    slots = tile_slots(row_ref[...], steps, capacity)
     total = jnp.zeros(total_ref.shape, jnp.float32)
     total_ref[...] = pair_density(slots, total, full, table_ref, groups)
 
 
 def far_kernel(
-    devices, capacity, full, steps, me_ref, pick_ref, table_ref, core_ref, weight_ref, near_ref, *rest
+    capacity, full, steps, row_ref, table_ref, core_ref, weight_ref, near_ref, *rest
 ):
     groups = dict(zip(steps, rest[: len(steps)]))
     potential_ref = rest[len(steps)]
     out_groups = dict(zip(steps, rest[len(steps) + 1 :]))
-    slots = tile_slots(pick_ref, me_ref[0], steps, devices, capacity)
+    slots = tile_slots(row_ref[...], steps, capacity)
     total = pair_density(slots, near_ref[...], full, table_ref, groups)
     valence = jnp.sum(total, axis=0, keepdims=True)
     value = jnp.maximum(core_ref[...] + valence, density_floor)
@@ -221,26 +246,30 @@
 
 
 def near_partials_kernel(
-    devices, capacity, steps, me_ref, pick_ref, table_ref, weight_ref, found_ref, *rest
+    capacity, steps, row_ref, table_ref, weight_ref, found_ref, *rest
 ):
     out_groups = dict(zip(steps, rest))
     potential_ref = rest[len(steps)]
     potential_ref[...] = found_ref[...]
-    slots = tile_slots(pick_ref, me_ref[0], steps, devices, capacity)
+    slots = tile_slots(row_ref[...], steps, capacity)
     pair_partials(slots, weight_ref[...] * found_ref[...], table_ref, out_groups)
 
 
-def sum_kernel(devices, capacity, dest_ref, me_ref, *rest):
+def sum_kernel(devices, capacity, row_ref, *rest):
     in_refs = rest[:devices]
     kohn_ref, pairs = rest[devices:]
     width = kohn_ref.shape[-1]
     for k in range(devices):
         pairs[k * capacity : (k + 1) * capacity] = in_refs[k][...]
-    places = pair_places(dest_ref, me_ref[0], devices, capacity)
+    places = pair_places(row_ref[...], 2 * KB)
     for i in range(KB):
         kohn_ref[pl.ds(i * width, width), :] = pairs[places[2 * i]].astype(jnp.float32) + pairs[
             places[2 * i + 1]
         ].astype(jnp.float32)
+
+
+def gathers(slot_count, devices, held_count):
+    return devices & (devices - 1) == 0 and pl.cdiv(slot_count, devices) >= held_count
 
 
 def per_device(
@@ -258,20 +287,48 @@
     source = block_source[0, 0]
     atom_devices = lax.axis_size("atoms")
     devices = lax.axis_size("space")
-    if pl.cdiv(source.shape[0], atom_devices) < held_count:
-        blocks, place = requested_blocks(stored, source)
-    else:
-        blocks, place = gathered_blocks(stored, source)
     destinations = pair_dest[0, 0]
     send_count = destinations.shape[0]
     capacity = pl.cdiv(send_count, devices)
     order = KB * block_width
-    me = lax.axis_index("space").reshape(1)
+    direct = gathers(source.shape[0], atom_devices, held_count)
+    if direct:
+        blocks = gathered_blocks(stored)
+    else:
+        blocks, source = requested_blocks(stored, source)
+    length = source.shape[0] + send_count + 2 * devices * capacity
+    length = pl.cdiv(length, 128) * 128
+    table = jnp.concatenate([source, destinations, tile_pairs[0, 0].reshape(-1)])
+    table = jnp.pad(table, (0, length - table.shape[0])).reshape(1, length)
+    row, level = pl.pallas_call(
+        functools.partial(
+            index_kernel,
+            devices,
+            capacity,
+            held_count if direct else 0,
+            source.shape[0],
+            send_count,
+        ),
+        name="index",
+        in_specs=[VMEM] + [SMEM] * 3,
+        out_shape=[
+            jax.ShapeDtypeStruct((1, length), jnp.int32),
+            jax.ShapeDtypeStruct((1, block_width), jnp.float32),
+        ],
+        out_specs=[VMEM] * 2,
+        compiler_params=pltpu.CompilerParams(vmem_limit_bytes=1 << 20),
+        cost_estimate=pl.CostEstimate(flops=2000, bytes_accessed=2000, transcendentals=0),
+    )(
+        table,
+        lax.axis_index("atoms").reshape(1),
+        lax.axis_index("space").reshape(1),
+        chem_pot,
+    )
     group = jax.ShapeDtypeStruct((capacity, block_width, block_width), jnp.bfloat16)
     out = pl.pallas_call(
         functools.partial(sign_kernel, devices, capacity),
         name="sign",
-        in_specs=[SMEM] * 4 + [VMEM],
+        in_specs=[VMEM] * 3,
         out_shape=[jax.ShapeDtypeStruct((order, block_width), jnp.bfloat16)] + [group] * devices,
         out_specs=[VMEM] * (1 + devices),
         scratch_shapes=[
@@ -285,7 +342,7 @@
         cost_estimate=pl.CostEstimate(
             flops=4 * order**3, bytes_accessed=4 * order * order, transcendentals=0
         ),
-    )(place, chem_pot, destinations, me, blocks)
+    )(row, level, blocks)
     column = out[0]
     outgoing = dict(enumerate(out[1:]))
     near, far = range(min(2, devices)), range(min(2, devices), devices)
@@ -293,8 +350,7 @@
     tables = basis_values[0, 0]
     points = tables.shape[-1]
     full = devices * capacity == send_count
-    pick = tile_pairs[0, 0]
-    row = jax.ShapeDtypeStruct((1, points), jnp.float32)
+    line = jax.ShapeDtypeStruct((1, points), jnp.float32)
 
     def cost(pairs):
         return pl.CostEstimate(
@@ -305,25 +361,24 @@
 
     limit = pltpu.CompilerParams(vmem_limit_bytes=16 << 20)
     total, density = pl.pallas_call(
-        functools.partial(near_density_kernel, devices, capacity, full, near),
+        functools.partial(near_density_kernel, capacity, full, near),
         name="near_density",
-        in_specs=[SMEM] * 2 + [VMEM] * (2 + len(near)),
+        in_specs=[VMEM] * (3 + len(near)),
         out_shape=[jax.ShapeDtypeStruct((8, points), jnp.float32), column],
         out_specs=[VMEM] * 2,
         compiler_params=limit,
         cost_estimate=cost(len(near) * capacity),
-    )(me, pick, tables, column, *[incoming[k] for k in near])
+    )(row, tables, column, *[incoming[k] for k in near])
     found, *sent = pl.pallas_call(
-        functools.partial(far_kernel, devices, capacity, full, far),
+        functools.partial(far_kernel, capacity, full, far),
         name="far",
-        in_specs=[SMEM] * 2 + [VMEM] * (4 + len(far)),
-        out_shape=[row] + [group] * len(far),
+        in_specs=[VMEM] * (5 + len(far)),
+        out_shape=[line] + [group] * len(far),
         out_specs=[VMEM] * (1 + len(far)),
         compiler_params=limit,
         cost_estimate=cost(2 * len(far) * capacity),
     )(
-        me,
-        pick,
+        row,
         tables,
         core_density[0],
         point_weights[0],
@@ -332,27 +387,27 @@
     )
     partials = dict(zip(far, sent))
     *sent, potential = pl.pallas_call(
-        functools.partial(near_partials_kernel, devices, capacity, near),
+        functools.partial(near_partials_kernel, capacity, near),
         name="near_partials",
-        in_specs=[SMEM] * 2 + [VMEM] * 3,
-        out_shape=[group] * len(near) + [row],
+        in_specs=[VMEM] * 4,
+        out_shape=[group] * len(near) + [line],
         out_specs=[VMEM] * (len(near) + 1),
         compiler_params=limit,
         cost_estimate=cost(len(near) * capacity),
-    )(me, pick, tables, point_weights[0], found)
+    )(row, tables, point_weights[0], found)
     partials.update(zip(near, sent))
     returned = exchange(partials, -1)
     kohn = pl.pallas_call(
         functools.partial(sum_kernel, devices, capacity),
         name="sum",
-        in_specs=[SMEM] * 2 + [VMEM] * devices,
+        in_specs=[VMEM] * (1 + devices),
         out_shape=jax.ShapeDtypeStruct((order, block_width), jnp.float32),
         out_specs=VMEM,
         scratch_shapes=[
             pltpu.VMEM((devices * capacity, block_width, block_width), jnp.bfloat16),
         ],
         compiler_params=pltpu.CompilerParams(vmem_limit_bytes=8 << 20),
-    )(destinations, me, *[returned[k] for k in range(devices)])
+    )(row, *[returned[k] for k in range(devices)])
     return (density[None, None], potential[None], kohn[None, None])
 
 

time: 47.7 us -> 45.9 us (0.962)
  Pallas kernels: 11 us -> 9.43 us
  waiting for transfers between devices: 18.3 us -> 17.2 us
  local copies, waits for them, and re-layouts: 1.11 us -> 1.87 us
    ppermute x7, waiting for transfers between devices: 10 us -> 8.54 us  [gathered_blocks(): parts[offset] = lax.ppermute(parts[offset ^ step], 'atoms', pairs)]
    another operation x0 -> x1, local copies, waits for them, and re-layouts: none -> 0.76 us  [per_device(): tile_pairs[0, 0].reshape(-1)]
    concatenate x0 -> x1, other arithmetic: none -> 0.75 us  [per_device(): jnp.concatenate([source, destinations, tile_pairs[0, 0].reshape(-1)])]
    pallas_call x3 -> x4, Pallas kernels: 5.08 us -> 4.41 us  [the longest x1 1.32 us: per_device(): pl.pallas_call(functools.partial(near_density_kernel, capacity, full, nea...]
    add x1 -> x0, other arithmetic: 0.67 us -> none  [gathered_blocks(): place = (me ^ source // held_count) * held_count + source % held_count]
    pallas_call x1, Pallas kernels: 1.4 us -> 0.89 us  [per_device(): pl.pallas_call(functools.partial(sum_kernel, devices, capacity), name='su...]
    unnamed x17 -> x13, local copies, waits for them, and re-layouts: 1.09 us -> 1.08 us
  transfers between devices with their start and end apart: 13 -> 13, of which waited for: 7 -> 7; matrix products, arithmetic and copies ran while one was open for 4% -> 6% of each run, Pallas kernels for 4% -> 4%
where the time goes in v3:
time: 45.9 us; the launch traced here: 45.7 us
  waiting for transfers between devices  17.2 us (37%)
  starting transfers between devices  15.1 us (33%)
  Pallas kernels  9.43 us (21%)
  local copies, waits for them, and re-layouts  1.87 us (4%)
  between operations  1.41 us (3%)
  other arithmetic  0.75 us (2%)
    ppermute x7, starting transfers between devices, gathered_blocks(): parts[offset] = lax.ppermute(parts[offset ^ step], 'atoms', pairs)  11.3 us
    ppermute x6, waiting for transfers between devices, exchange(): lax.ppermute(groups[step], 'space', pairs)  8.67 us
    ppermute x7, waiting for transfers between devices, gathered_blocks(): parts[offset] = lax.ppermute(parts[offset ^ step], 'atoms', pairs)  8.54 us
    pallas_call x1, Pallas kernels, per_device(): pl.pallas_call(functools.partial(sign_kernel, devices, capacity), name='s...  4.13 us
    ppermute x6, starting transfers between devices, exchange(): lax.ppermute(groups[step], 'space', pairs)  3.78 us
    pallas_call x1, Pallas kernels, per_device(): pl.pallas_call(functools.partial(near_density_kernel, capacity, full, nea...  1.32 us
    pallas_call x1, Pallas kernels, per_device(): pl.pallas_call(functools.partial(far_kernel, capacity, full, far), name='...  1.29 us
    pallas_call x1, Pallas kernels, per_device(): pl.pallas_call(functools.partial(near_partials_kernel, capacity, near), n...  1.17 us
  transfers between devices with their start and end apart: 13, of which 7 were waited for; matrix products, arithmetic and copies ran while one was open for 6% of the time, Pallas kernels for 4%

profile of v3, /device:TPU:0, one launch (start us, length us, event | category | flops | bytes accessed | tf_op | source)
XLA Modules:
  0.0 45.7 jit_solution(9537597021857775346)
XLA Ops:
  0.6 3.1 %collective-permute-start = (bf16[4,128,128]{2,1,0:T(8,128)(2,1)}, bf16[4,128,128]{2,1,0:T(8,128)(2,1)S(1)}, u32[]{:S(2)}, u32[]{:S(2)}) collective-permute-start(bf16[4,128,128]{2,1,0:T(8,128)(2,1)} %bitcast.21), channel_id=1, source_target_pairs={{0,4},{4,0},{8,12},{12,8},{16,20},{20,16},{24,28},{28,24},{1,5},{5... | collective-permute-start | bytes 393224 | tf_op jit(solution)/shard_map/ppermute | solution.py:60
  3.7 1.6 %collective-permute-start.1 = (bf16[4,128,128]{2,1,0:T(8,128)(2,1)}, bf16[4,128,128]{2,1,0:T(8,128)(2,1)S(1)}, u32[]{:S(2)}, u32[]{:S(2)}) collective-permute-start(bf16[4,128,128]{2,1,0:T(8,128)(2,1)} %bitcast.22), channel_id=1, source_target_pairs={{0,8},{4,12},{8,0},{12,4},{16,24},{20,28},{24,16},{28,20},{1,9},{5... | collective-permute-start | bytes 393224 | tf_op jit(solution)/shard_map/ppermute | solution.py:60
  5.3 2.6 %collective-permute-start.3 = (bf16[4,128,128]{2,1,0:T(8,128)(2,1)}, bf16[4,128,128]{2,1,0:T(8,128)(2,1)S(1)}, u32[]{:S(2)}, u32[]{:S(2)}) collective-permute-start(bf16[4,128,128]{2,1,0:T(8,128)(2,1)} %bitcast.23), channel_id=1, source_target_pairs={{0,16},{4,20},{8,24},{12,28},{16,0},{20,4},{24,8},{28,12},{1,17},{... | collective-permute-start | bytes 393224 | tf_op jit(solution)/shard_map/ppermute | solution.py:60
  7.9 0.9 %constant_dynamic-update-slice_fusion.7 = bf16[32,128,128]{2,1,0:T(8,128)(2,1)S(1)} fusion(bf16[1,4,128,128]{3,2,1,0:T(8,128)(2,1)} %param.8), kind=kLoop, calls=%fused_computation.7 | loop fusion | bytes 262144
  8.8 0.8 %reshape_squeeze.3 = s32[24]{0:T(128)S(1)} reshape(s32[1,1,2,12]{3,2,1,0:T(2,128)} %param.15) | data formatting | bytes 192 | tf_op jit(solution)/shard_map/reshape;squeeze | solution.py:301
  9.6 0.7 %pad_add_fusion = s32[72]{0:T(128)S(1)} fusion(s32[24]{0:T(128)S(1)} %reshape_squeeze.3, s32[12]{0:T(128)} %bitcast.24, s32[36]{0:T(128)} %bitcast.25), kind=kLoop, calls=%fused_computation.8 | loop fusion | flops 144 | bytes 576 | tf_op jit(solution)/shard_map/concatenate | solution.py:301
  11.0 0.6 %index.1 = (s32[1,128]{1,0:T(1,128)S(1)}, f32[1,128]{1,0:T(1,128)S(1)}) custom-call(s32[1,128]{1,0:T(1,128)S(1)} %pad_bitcast_fusion.table_ref, s32[1]{0:T(128)} %bitcast.3.atom_ref, s32[1]{0:T(128)} %bitcast.4.me_ref, f32[1]{0:T(128)S(6)} %copy.18.chem_ref), custom_call_target="tpu_custom_call" | custom-call | flops 2000 | bytes 2000 | tf_op jit(solution)/shard_map/index/pallas_call | solution.py:303
  11.6 2.3 %collective-permute-done.3 = bf16[4,128,128]{2,1,0:T(8,128)(2,1)S(1)} collective-permute-done((bf16[4,128,128]{2,1,0:T(8,128)(2,1)}, bf16[4,128,128]{2,1,0:T(8,128)(2,1)S(1)}, u32[]{:S(2)}, u32[]{:S(2)}) %collective-permute-start.3) | collective-permute-done | bytes 131104 | tf_op jit(solution)/shard_map/ppermute | solution.py:60
  13.9 0.5 %collective-permute-start.4 = (bf16[4,128,128]{2,1,0:T(8,128)(2,1)S(1)}, bf16[4,128,128]{2,1,0:T(8,128)(2,1)S(1)}, u32[]{:S(2)}, u32[]{:S(2)}) collective-permute-start(bf16[4,128,128]{2,1,0:T(8,128)(2,1)S(1)} %collective-permute-done.3), channel_id=1, source_target_pairs={{0,4},{4,0},{8,12},{12,8},{16,20},{20,16},{24,28},{28,24},{1,5},{5... | collective-permute-start | bytes 393224 | tf_op jit(solution)/shard_map/ppermute | solution.py:60
  14.4 0.3 collective-permute-start.5
  14.8 1.7 %collective-permute-start.2 = (bf16[4,128,128]{2,1,0:T(8,128)(2,1)S(1)}, bf16[4,128,128]{2,1,0:T(8,128)(2,1)S(1)}, u32[]{:S(2)}, u32[]{:S(2)}) collective-permute-start(bf16[4,128,128]{2,1,0:T(8,128)(2,1)S(1)} %collective-permute-done), channel_id=1, source_target_pairs={{0,8},{4,12},{8,0},{12,4},{16,24},{20,28},{24,16},{28,20},{1,9},{5... | collective-permute-start | bytes 393224 | tf_op jit(solution)/shard_map/ppermute | solution.py:60
  16.5 2.9 %collective-permute-done.5 = bf16[4,128,128]{2,1,0:T(8,128)(2,1)S(1)} collective-permute-done((bf16[4,128,128]{2,1,0:T(8,128)(2,1)S(1)}, bf16[4,128,128]{2,1,0:T(8,128)(2,1)S(1)}, u32[]{:S(2)}, u32[]{:S(2)}) %collective-permute-start.5) | collective-permute-done | bytes 131104 | tf_op jit(solution)/shard_map/ppermute | solution.py:60
  19.4 1.5 %collective-permute-start.6 = (bf16[4,128,128]{2,1,0:T(8,128)(2,1)S(1)}, bf16[4,128,128]{2,1,0:T(8,128)(2,1)S(1)}, u32[]{:S(2)}, u32[]{:S(2)}) collective-permute-start(bf16[4,128,128]{2,1,0:T(8,128)(2,1)S(1)} %collective-permute-done.5), channel_id=1, source_target_pairs={{0,4},{4,0},{8,12},{12,8},{16,20},{20,16},{24,28},{28,24},{1,5},{5... | collective-permute-start | bytes 393224 | tf_op jit(solution)/shard_map/ppermute | solution.py:60
  21.1 3.3 %collective-permute-done.6 = bf16[4,128,128]{2,1,0:T(8,128)(2,1)S(1)} collective-permute-done((bf16[4,128,128]{2,1,0:T(8,128)(2,1)S(1)}, bf16[4,128,128]{2,1,0:T(8,128)(2,1)S(1)}, u32[]{:S(2)}, u32[]{:S(2)}) %collective-permute-start.6) | collective-permute-done | bytes 131104 | tf_op jit(solution)/shard_map/ppermute | solution.py:60
  24.4 0.0 copy-start
  24.4 4.1 %sign.1 = (bf16[768,128]{1,0:T(8,128)(2,1)S(1)}, bf16[3,128,128]{2,1,0:T(8,128)(2,1)S(1)}, bf16[3,128,128]{2,1,0:T(8,128)(2,1)S(1)}, bf16[3,128,128]{2,1,0:T(8,128)(2,1)S(1)}, bf16[3,128,128]{2,1,0:T(8,128)(2,1)S(1)}) custom-call(s32[1,128]{1,0:T(1,128)S(1)} %get-tuple-element.18.row_ref, f32[1,128]{1,0:T(1,128)S(1)} %get-tuple-element.19.level_ref, ...), custom_call_target="tpu_custom_call" | custom-call | flops 1811939328 | bytes 2359296 | tf_op jit(solution)/shard_map/sign/pallas_call | solution.py:328
  28.5 0.0 copy-start.1
  28.6 0.0 copy-start.2
  28.6 0.1 collective-permute-start.7
  28.6 1.6 %collective-permute-start.8 = (bf16[3,128,128]{2,1,0:T(8,128)(2,1)S(1)}, bf16[3,128,128]{2,1,0:T(8,128)(2,1)S(1)}, u32[]{:S(2)}, u32[]{:S(2)}) collective-permute-start(bf16[3,128,128]{2,1,0:T(8,128)(2,1)S(1)} %get-tuple-element.25), channel_id=1, source_target_pairs={{0,2},{1,3},{2,0},{3,1},{4,6},{5,7},{6,4},{7,5},{8,10},{9,11},{10,... | collective-permute-start | bytes 294920 | tf_op jit(solution)/shard_map/ppermute | solution.py:87
  30.2 0.3 collective-permute-start.9
  30.5 1.3 %near_density.1 = (f32[8,1024]{1,0:T(8,128)S(1)}, bf16[768,128]{1,0:T(8,128)(2,1)}) custom-call(s32[1,128]{1,0:T(1,128)S(1)} %get-tuple-element.18.row_ref, bf16[8,128,1024]{2,1,0:T(8,128)(2,1)S(1)} %bitcast.14, bf16[768,128]{1,0:T(8,128)(2,1)S(1)} %get-tuple-element.20.column_ref, bf16[3,128,128]{2,1,0:T(8,128)(2,1)S(1)} %get-tuple-element.21.rest_0_, ...), custom_call_target="tpu_custom_call" | custom-call | flops 201326592 | bytes 3145728 | tf_op jit(solution)/shard_map/near_density/pallas_call | solution.py:363
  31.8 2.6 %collective-permute-done.8.rest_0_ = bf16[3,128,128]{2,1,0:T(8,128)(2,1)S(1)} collective-permute-done((bf16[3,128,128]{2,1,0:T(8,128)(2,1)S(1)}, bf16[3,128,128]{2,1,0:T(8,128)(2,1)S(1)}, u32[]{:S(2)}, u32[]{:S(2)}) %collective-permute-start.8) | collective-permute-done | bytes 98336 | tf_op jit(solution)/shard_map/ppermute | solution.py:87
  34.4 1.0 %collective-permute-done.9.rest_1_ = bf16[3,128,128]{2,1,0:T(8,128)(2,1)S(1)} collective-permute-done((bf16[3,128,128]{2,1,0:T(8,128)(2,1)S(1)}, bf16[3,128,128]{2,1,0:T(8,128)(2,1)S(1)}, u32[]{:S(2)}, u32[]{:S(2)}) %collective-permute-start.9) | collective-permute-done | bytes 98336 | tf_op jit(solution)/shard_map/ppermute | solution.py:87
  35.4 1.3 %far.1 = (f32[1,1024]{1,0:T(1,128)S(1)}, bf16[3,128,128]{2,1,0:T(8,128)(2,1)S(1)}, bf16[3,128,128]{2,1,0:T(8,128)(2,1)S(1)}) custom-call(s32[1,128]{1,0:T(1,128)S(1)} %get-tuple-element.18.row_ref, bf16[8,128,1024]{2,1,0:T(8,128)(2,1)S(1)} %bitcast.15, f32[1,1024]{1,0:T(1,128)S(1)} %bitcast.19, f32[1,1024]{1,0:T(1,128)S(1)} %bitcast.17, ...), custom_call_target="tpu_custom_call" | custom-call | flops 402653184 | bytes 6291456 | tf_op jit(solution)/shard_map/far/pallas_call | solution.py:372
  36.7 1.2 %near_partials.1 = (bf16[3,128,128]{2,1,0:T(8,128)(2,1)S(1)}, bf16[3,128,128]{2,1,0:T(8,128)(2,1)S(1)}, f32[1,1024]{1,0:T(1,128)}) custom-call(s32[1,128]{1,0:T(1,128)S(1)} %get-tuple-element.18.row_ref, bf16[8,128,1024]{2,1,0:T(8,128)(2,1)S(1)} %bitcast.16, f32[1,1024]{1,0:T(1,128)S(1)} %bitcast.18, f32[1,1024]{1,0:T(1,128)S(1)} %get-tuple-element.27.found_ref), custom_call_target="tpu_custom_call" | custom-call | flops 201326592 | bytes 3145728 | tf_op jit(solution)/shard_map/near_partials/pallas_call | solution.py:389
  37.9 0.4 collective-permute-start.10
  38.2 1.5 %collective-permute-start.11 = (bf16[3,128,128]{2,1,0:T(8,128)(2,1)S(1)}, bf16[3,128,128]{2,1,0:T(8,128)(2,1)S(1)}, u32[]{:S(2)}, u32[]{:S(2)}) collective-permute-start(bf16[3,128,128]{2,1,0:T(8,128)(2,1)S(1)} %get-tuple-element.31), channel_id=1, source_target_pairs={{0,2},{1,3},{2,0},{3,1},{4,6},{5,7},{6,4},{7,5},{8,10},{9,11},{10,... | collective-permute-start | bytes 294920 | tf_op jit(solution)/shard_map/ppermute | solution.py:87
  39.7 0.0 collective-permute-start.12
  39.7 3.7 %collective-permute-done.11.rest_2_ = bf16[3,128,128]{2,1,0:T(8,128)(2,1)S(1)} collective-permute-done((bf16[3,128,128]{2,1,0:T(8,128)(2,1)S(1)}, bf16[3,128,128]{2,1,0:T(8,128)(2,1)S(1)}, u32[]{:S(2)}, u32[]{:S(2)}) %collective-permute-start.11) | collective-permute-done | bytes 98336 | tf_op jit(solution)/shard_map/ppermute | solution.py:87
  43.5 1.4 %collective-permute-done.12.rest_3_ = bf16[3,128,128]{2,1,0:T(8,128)(2,1)S(1)} collective-permute-done((bf16[3,128,128]{2,1,0:T(8,128)(2,1)S(1)}, bf16[3,128,128]{2,1,0:T(8,128)(2,1)S(1)}, u32[]{:S(2)}, u32[]{:S(2)}) %collective-permute-start.12) | collective-permute-done | bytes 98336 | tf_op jit(solution)/shard_map/ppermute | solution.py:87
  44.8 0.9 %sum.1 = f32[768,128]{1,0:T(8,128)} custom-call(s32[1,128]{1,0:T(1,128)S(1)} %get-tuple-element.18.row_ref, bf16[3,128,128]{2,1,0:T(8,128)(2,1)S(1)} %get-tuple-element.29.rest_0_, bf16[3,128,128]{2,1,0:T(8,128)(2,1)S(1)} %collective-permute-done.10.rest_1_, bf16[3,128,128]{2,1,0:T(8,128)(2,1)S(1)} %collective-permute-done.11.rest_2_, ...), custom_call_target="tpu_custom_call" | custom-call | tf_op jit(solution)/shard_map/sum/pallas_call | solution.py:400
  (17 shorter events, 0.2 us)
Async XLA Ops:
  0.6 14.1 %collective-permute-start = (bf16[4,128,128]{2,1,0:T(8,128)(2,1)}, bf16[4,128,128]{2,1,0:T(8,128)(2,1)S(1)}, u32[]{:S(2)}, u32[]{:S(2)}) collective-permute-start(bf16[4,128,128]{2,1,0:T(8,128)(2,1)} %bitcast.21), channel_id=1, source_target_pairs={{0,4},{4,0},{8,12},{12,8},{16,20},{20,16},{24,28},{28,24},{1,5},{5... | collective-permute-start | bytes 393224 | tf_op jit(solution)/shard_map/ppermute | solution.py:60
  3.7 12.8 %collective-permute-start.1 = (bf16[4,128,128]{2,1,0:T(8,128)(2,1)}, bf16[4,128,128]{2,1,0:T(8,128)(2,1)S(1)}, u32[]{:S(2)}, u32[]{:S(2)}) collective-permute-start(bf16[4,128,128]{2,1,0:T(8,128)(2,1)} %bitcast.22), channel_id=1, source_target_pairs={{0,8},{4,12},{8,0},{12,4},{16,24},{20,28},{24,16},{28,20},{1,9},{5... | collective-permute-start | bytes 393224 | tf_op jit(solution)/shard_map/ppermute | solution.py:60
  5.3 8.7 %collective-permute-start.3 = (bf16[4,128,128]{2,1,0:T(8,128)(2,1)}, bf16[4,128,128]{2,1,0:T(8,128)(2,1)S(1)}, u32[]{:S(2)}, u32[]{:S(2)}) collective-permute-start(bf16[4,128,128]{2,1,0:T(8,128)(2,1)} %bitcast.23), channel_id=1, source_target_pairs={{0,16},{4,20},{8,24},{12,28},{16,0},{20,4},{24,8},{28,12},{1,17},{... | collective-permute-start | bytes 393224 | tf_op jit(solution)/shard_map/ppermute | solution.py:60
  13.9 7.1 %collective-permute-start.4 = (bf16[4,128,128]{2,1,0:T(8,128)(2,1)S(1)}, bf16[4,128,128]{2,1,0:T(8,128)(2,1)S(1)}, u32[]{:S(2)}, u32[]{:S(2)}) collective-permute-start(bf16[4,128,128]{2,1,0:T(8,128)(2,1)S(1)} %collective-permute-done.3), channel_id=1, source_target_pairs={{0,4},{4,0},{8,12},{12,8},{16,20},{20,16},{24,28},{28,24},{1,5},{5... | collective-permute-start | bytes 393224 | tf_op jit(solution)/shard_map/ppermute | solution.py:60
  14.4 5.0 %collective-permute-start.5 = (bf16[4,128,128]{2,1,0:T(8,128)(2,1)S(1)}, bf16[4,128,128]{2,1,0:T(8,128)(2,1)S(1)}, u32[]{:S(2)}, u32[]{:S(2)}) collective-permute-start(bf16[4,128,128]{2,1,0:T(8,128)(2,1)S(1)} %collective-permute-done.3), channel_id=1, source_target_pairs={{0,8},{4,12},{8,0},{12,4},{16,24},{20,28},{24,16},{28,20},{1,9},{5... | collective-permute-start | bytes 393224 | tf_op jit(solution)/shard_map/ppermute | solution.py:60
  14.8 6.2 %collective-permute-start.2 = (bf16[4,128,128]{2,1,0:T(8,128)(2,1)S(1)}, bf16[4,128,128]{2,1,0:T(8,128)(2,1)S(1)}, u32[]{:S(2)}, u32[]{:S(2)}) collective-permute-start(bf16[4,128,128]{2,1,0:T(8,128)(2,1)S(1)} %collective-permute-done), channel_id=1, source_target_pairs={{0,8},{4,12},{8,0},{12,4},{16,24},{20,28},{24,16},{28,20},{1,9},{5... | collective-permute-start | bytes 393224 | tf_op jit(solution)/shard_map/ppermute | solution.py:60
  19.4 5.0 %collective-permute-start.6 = (bf16[4,128,128]{2,1,0:T(8,128)(2,1)S(1)}, bf16[4,128,128]{2,1,0:T(8,128)(2,1)S(1)}, u32[]{:S(2)}, u32[]{:S(2)}) collective-permute-start(bf16[4,128,128]{2,1,0:T(8,128)(2,1)S(1)} %collective-permute-done.5), channel_id=1, source_target_pairs={{0,4},{4,0},{8,12},{12,8},{16,20},{20,16},{24,28},{28,24},{1,5},{5... | collective-permute-start | bytes 393224 | tf_op jit(solution)/shard_map/ppermute | solution.py:60
  24.4 6.1 %copy-start = (bf16[1,1,8,128,1024]{4,3,2,1,0:T(8,128)(2,1)S(1)}, bf16[1,1,8,128,1024]{4,3,2,1,0:T(8,128)(2,1)}, u32[]{:S(2)}) copy-start(bf16[1,1,8,128,1024]{4,3,2,1,0:T(8,128)(2,1)} %param.11) | copy-start | bytes 6291460
  28.5 6.9 %copy-start.1 = (f32[1,1,1024]{2,1,0:T(1,128)S(1)}, f32[1,1,1024]{2,1,0:T(1,128)}, u32[]{:S(2)}) copy-start(f32[1,1,1024]{2,1,0:T(1,128)} %param.13) | copy-start | bytes 12292
  28.6 6.9 %copy-start.2 = (f32[1,1,1024]{2,1,0:T(1,128)S(1)}, f32[1,1,1024]{2,1,0:T(1,128)}, u32[]{:S(2)}) copy-start(f32[1,1,1024]{2,1,0:T(1,128)} %param.12) | copy-start | bytes 12292
  28.6 1.9 %collective-permute-start.7 = (bf16[3,128,128]{2,1,0:T(8,128)(2,1)S(1)}, bf16[3,128,128]{2,1,0:T(8,128)(2,1)S(1)}, u32[]{:S(2)}, u32[]{:S(2)}) collective-permute-start(bf16[3,128,128]{2,1,0:T(8,128)(2,1)S(1)} %get-tuple-element.22), channel_id=1, source_target_pairs={{0,1},{1,0},{2,3},{3,2},{4,5},{5,4},{6,7},{7,6},{8,9},{9,8},{10,11... | collective-permute-start | bytes 294920 | tf_op jit(solution)/shard_map/ppermute | solution.py:87
  28.6 5.7 %collective-permute-start.8 = (bf16[3,128,128]{2,1,0:T(8,128)(2,1)S(1)}, bf16[3,128,128]{2,1,0:T(8,128)(2,1)S(1)}, u32[]{:S(2)}, u32[]{:S(2)}) collective-permute-start(bf16[3,128,128]{2,1,0:T(8,128)(2,1)S(1)} %get-tuple-element.25), channel_id=1, source_target_pairs={{0,2},{1,3},{2,0},{3,1},{4,6},{5,7},{6,4},{7,5},{8,10},{9,11},{10,... | collective-permute-start | bytes 294920 | tf_op jit(solution)/shard_map/ppermute | solution.py:87
  30.2 5.2 %collective-permute-start.9 = (bf16[3,128,128]{2,1,0:T(8,128)(2,1)S(1)}, bf16[3,128,128]{2,1,0:T(8,128)(2,1)S(1)}, u32[]{:S(2)}, u32[]{:S(2)}) collective-permute-start(bf16[3,128,128]{2,1,0:T(8,128)(2,1)S(1)} %get-tuple-element.26), channel_id=1, source_target_pairs={{0,3},{1,2},{2,1},{3,0},{4,7},{5,6},{6,5},{7,4},{8,11},{9,10},{10,... | collective-permute-start | bytes 294920 | tf_op jit(solution)/shard_map/ppermute | solution.py:87
  37.9 1.9 %collective-permute-start.10 = (bf16[3,128,128]{2,1,0:T(8,128)(2,1)S(1)}, bf16[3,128,128]{2,1,0:T(8,128)(2,1)S(1)}, u32[]{:S(2)}, u32[]{:S(2)}) collective-permute-start(bf16[3,128,128]{2,1,0:T(8,128)(2,1)S(1)} %get-tuple-element.30), channel_id=1, source_target_pairs={{0,1},{1,0},{2,3},{3,2},{4,5},{5,4},{6,7},{7,6},{8,9},{9,8},{10,11... | collective-permute-start | bytes 294920 | tf_op jit(solution)/shard_map/ppermute | solution.py:87
  38.2 5.2 %collective-permute-start.11 = (bf16[3,128,128]{2,1,0:T(8,128)(2,1)S(1)}, bf16[3,128,128]{2,1,0:T(8,128)(2,1)S(1)}, u32[]{:S(2)}, u32[]{:S(2)}) collective-permute-start(bf16[3,128,128]{2,1,0:T(8,128)(2,1)S(1)} %get-tuple-element.31), channel_id=1, source_target_pairs={{0,2},{1,3},{2,0},{3,1},{4,6},{5,7},{6,4},{7,5},{8,10},{9,11},{10,... | collective-permute-start | bytes 294920 | tf_op jit(solution)/shard_map/ppermute | solution.py:87
  39.7 5.1 %collective-permute-start.12 = (bf16[3,128,128]{2,1,0:T(8,128)(2,1)S(1)}, bf16[3,128,128]{2,1,0:T(8,128)(2,1)S(1)}, u32[]{:S(2)}, u32[]{:S(2)}) collective-permute-start(bf16[3,128,128]{2,1,0:T(8,128)(2,1)S(1)} %get-tuple-element.32), channel_id=1, source_target_pairs={{0,3},{1,2},{2,1},{3,0},{4,7},{5,6},{6,5},{7,4},{8,11},{9,10},{10,... | collective-permute-start | bytes 294920 | tf_op jit(solution)/shard_map/ppermute | solution.py:87

commit v4 on v3

--- a/solution.py
+++ b/solution.py
@@ -161,15 +161,28 @@
         x_zero[at(i), at(j)] = value
         if i != j:
             x_zero[at(j), at(i)] = value.T
-    for i in range(KB):
-        square = jnp.dot(x_zero[at(i), :], x_zero[...], preferred_element_type=jnp.float32)
-        for j in range(KB):
-            part = -0.5 * square[:, j * width : (j + 1) * width]
-            t_one[at(i), at(j)] = (1.5 * unit + part if i == j else part).astype(jnp.bfloat16)
-    for i in range(KB):
-        x_one[at(i), :] = jnp.dot(
-            x_zero[at(i), :], t_one[...], preferred_element_type=jnp.float32
+    for i in range(0, KB, 2):
+        pair = pl.ds(i * width, 2 * width)
+        right = pl.ds(i * width, order - i * width)
+        square = jnp.dot(x_zero[pair, :], x_zero[:, right], preferred_element_type=jnp.float32)
+        for k in (i, i + 1):
+            for j in range(i, KB):
+                rows, cols = (k - i) * width, (j - i) * width
+                part = -0.5 * square[rows : rows + width, cols : cols + width]
+                value = (1.5 * unit + part if k == j else part).astype(jnp.bfloat16)
+                t_one[at(k), at(j)] = value
+                if j > i + 1:
+                    t_one[at(j), at(k)] = value.T
+    for i in range(0, KB, 2):
+        pair = pl.ds(i * width, 2 * width)
+        right = pl.ds(i * width, order - i * width)
+        value = jnp.dot(
+            x_zero[pair, :], t_one[:, right], preferred_element_type=jnp.float32
         ).astype(jnp.bfloat16)
+        x_one[pair, right] = value
+        if i + 2 < KB:
+            below = pl.ds((i + 2) * width, order - (i + 2) * width)
+            x_one[below, pair] = value[:, 2 * width :].T
     square = jnp.dot(x_one[...], x_one[:, at(0)], preferred_element_type=jnp.float32)
     parts = []
     for i in range(KB):
@@ -228,7 +241,18 @@
     total_ref[...] = pair_density(slots, total, full, table_ref, groups)
 
 
-def far_kernel(
+def mid_density_kernel(capacity, full, steps, row_ref, table_ref, near_ref, *rest):
+    groups = dict(zip(steps, rest))
+    slots = tile_slots(row_ref[...], steps, capacity)
+    rest[-1][...] = pair_density(slots, near_ref[...], full, table_ref, groups)
+
+
+def mid_partials_kernel(capacity, steps, row_ref, table_ref, weight_ref, found_ref, *rest):
+    slots = tile_slots(row_ref[...], steps, capacity)
+    pair_partials(slots, weight_ref[...] * found_ref[...], table_ref, dict(zip(steps, rest)))
+
+
+def last_kernel(
     capacity, full, steps, row_ref, table_ref, core_ref, weight_ref, near_ref, *rest
 ):
     groups = dict(zip(steps, rest[: len(steps)]))
@@ -345,56 +369,62 @@
     )(row, level, blocks)
     column = out[0]
     outgoing = dict(enumerate(out[1:]))
-    near, far = range(min(2, devices)), range(min(2, devices), devices)
+    near, mid, last = range(2), range(2, devices - 1), range(devices - 1, devices)
     incoming = exchange(outgoing, 1)
     tables = basis_values[0, 0]
     points = tables.shape[-1]
     full = devices * capacity == send_count
     line = jax.ShapeDtypeStruct((1, points), jnp.float32)
-
-    def cost(pairs):
-        return pl.CostEstimate(
-            flops=2 * pairs * block_width**2 * points,
-            bytes_accessed=4 * pairs * block_width * points,
-            transcendentals=0,
-        )
-
-    limit = pltpu.CompilerParams(vmem_limit_bytes=16 << 20)
-    total, density = pl.pallas_call(
+    lines = jax.ShapeDtypeStruct((8, points), jnp.float32)
+
+    def step_call(kernel, steps, out_shape, operands):
+        pairs = len(steps) * capacity
+        return pl.pallas_call(
+            kernel,
+            in_specs=[VMEM] * len(operands),
+            out_shape=out_shape,
+            out_specs=[VMEM] * len(out_shape),
+            compiler_params=pltpu.CompilerParams(vmem_limit_bytes=16 << 20),
+            cost_estimate=pl.CostEstimate(
+                flops=2 * pairs * block_width**2 * points,
+                bytes_accessed=4 * pairs * block_width * points,
+                transcendentals=0,
+            ),
+        )(*operands)
+
+    total, density = step_call(
         functools.partial(near_density_kernel, capacity, full, near),
-        name="near_density",
-        in_specs=[VMEM] * (3 + len(near)),
-        out_shape=[jax.ShapeDtypeStruct((8, points), jnp.float32), column],
-        out_specs=[VMEM] * 2,
-        compiler_params=limit,
-        cost_estimate=cost(len(near) * capacity),
-    )(row, tables, column, *[incoming[k] for k in near])
-    found, *sent = pl.pallas_call(
-        functools.partial(far_kernel, capacity, full, far),
-        name="far",
-        in_specs=[VMEM] * (5 + len(far)),
-        out_shape=[line] + [group] * len(far),
-        out_specs=[VMEM] * (1 + len(far)),
-        compiler_params=limit,
-        cost_estimate=cost(2 * len(far) * capacity),
-    )(
-        row,
-        tables,
-        core_density[0],
-        point_weights[0],
-        total,
-        *[incoming[k] for k in far],
-    )
-    partials = dict(zip(far, sent))
-    *sent, potential = pl.pallas_call(
+        near,
+        [lines, column],
+        [row, tables, column, *[incoming[k] for k in near]],
+    )
+    (total,) = step_call(
+        functools.partial(mid_density_kernel, capacity, full, mid),
+        mid,
+        [lines],
+        [row, tables, total, *[incoming[k] for k in mid]],
+    )
+    weight = point_weights[0]
+    found, *sent = step_call(
+        functools.partial(last_kernel, capacity, full, last),
+        last,
+        [line] + [group] * len(last),
+        [row, tables, core_density[0], weight, total, *[incoming[k] for k in last]],
+    )
+    partials = dict(zip(last, sent))
+    sent = step_call(
+        functools.partial(mid_partials_kernel, capacity, mid),
+        mid,
+        [group] * len(mid),
+        [row, tables, weight, found],
+    )
+    partials.update(zip(mid, sent))
+    *sent, potential = step_call(
         functools.partial(near_partials_kernel, capacity, near),
-        name="near_partials",
-        in_specs=[VMEM] * 4,
-        out_shape=[group] * len(near) + [line],
-        out_specs=[VMEM] * (len(near) + 1),
-        compiler_params=limit,
-        cost_estimate=cost(len(near) * capacity),
-    )(row, tables, point_weights[0], found)
+        near,
+        [group] * len(near) + [line],
+        [row, tables, weight, found],
+    )
     partials.update(zip(near, sent))
     returned = exchange(partials, -1)
     kohn = pl.pallas_call(

time: 45.9 us -> 45.5 us (level)
  waiting for transfers between devices: 17.2 us -> 16.7 us
    pallas_call x3 -> x5, Pallas kernels: 3.78 us -> 4.43 us  [step_call(): pl.pallas_call(kernel, in_specs=[VMEM] * len(operands), out_shape=out_sha...]
    pallas_call x1, Pallas kernels: 4.13 us -> 3.5 us  [per_device(): pl.pallas_call(functools.partial(sign_kernel, devices, capacity), name='s...]
    ppermute x6, waiting for transfers between devices: 8.67 us -> 8.19 us  [exchange(): lax.ppermute(groups[step], 'space', pairs)]
  transfers between devices with their start and end apart: 13 -> 13, of which waited for: 7 -> 7; matrix products, arithmetic and copies ran while one was open for 6% -> 6% of each run, Pallas kernels for 4% -> 5%
where the time goes in v4:
time: 45.5 us; the launch traced here: 45.3 us
  waiting for transfers between devices  16.7 us (37%)
  starting transfers between devices  15.1 us (33%)
  Pallas kernels  9.44 us (21%)
  local copies, waits for them, and re-layouts  1.86 us (4%)
  between operations  1.42 us (3%)
  other arithmetic  0.75 us (2%)
    ppermute x7, starting transfers between devices, gathered_blocks(): parts[offset] = lax.ppermute(parts[offset ^ step], 'atoms', pairs)  11.3 us
    ppermute x7, waiting for transfers between devices, gathered_blocks(): parts[offset] = lax.ppermute(parts[offset ^ step], 'atoms', pairs)  8.54 us
    ppermute x6, waiting for transfers between devices, exchange(): lax.ppermute(groups[step], 'space', pairs)  8.19 us
    pallas_call x5, Pallas kernels, step_call(): pl.pallas_call(kernel, in_specs=[VMEM] * len(operands), out_shape=out_sha...  4.43 us
    ppermute x6, starting transfers between devices, exchange(): lax.ppermute(groups[step], 'space', pairs)  3.84 us
    pallas_call x1, Pallas kernels, per_device(): pl.pallas_call(functools.partial(sign_kernel, devices, capacity), name='s...  3.5 us
    unnamed x13, local copies, waits for them, and re-layouts  1.08 us
  transfers between devices with their start and end apart: 13, of which 7 were waited for; matrix products, arithmetic and copies ran while one was open for 6% of the time, Pallas kernels for 5%

profile of v4, /device:TPU:0, one launch (start us, length us, event | category | flops | bytes accessed | tf_op | source)
XLA Modules:
  0.0 45.3 jit_solution(9273942916407956991)
XLA Ops:
  0.6 3.1 %collective-permute-start = (bf16[4,128,128]{2,1,0:T(8,128)(2,1)}, bf16[4,128,128]{2,1,0:T(8,128)(2,1)S(1)}, u32[]{:S(2)}, u32[]{:S(2)}) collective-permute-start(bf16[4,128,128]{2,1,0:T(8,128)(2,1)} %bitcast.24), channel_id=1, source_target_pairs={{0,4},{4,0},{8,12},{12,8},{16,20},{20,16},{24,28},{28,24},{1,5},{5... | collective-permute-start | bytes 393224 | tf_op jit(solution)/shard_map/ppermute | solution.py:60
  3.7 1.6 %collective-permute-start.1 = (bf16[4,128,128]{2,1,0:T(8,128)(2,1)}, bf16[4,128,128]{2,1,0:T(8,128)(2,1)S(1)}, u32[]{:S(2)}, u32[]{:S(2)}) collective-permute-start(bf16[4,128,128]{2,1,0:T(8,128)(2,1)} %bitcast.25), channel_id=1, source_target_pairs={{0,8},{4,12},{8,0},{12,4},{16,24},{20,28},{24,16},{28,20},{1,9},{5... | collective-permute-start | bytes 393224 | tf_op jit(solution)/shard_map/ppermute | solution.py:60
  5.3 2.6 %collective-permute-start.3 = (bf16[4,128,128]{2,1,0:T(8,128)(2,1)}, bf16[4,128,128]{2,1,0:T(8,128)(2,1)S(1)}, u32[]{:S(2)}, u32[]{:S(2)}) collective-permute-start(bf16[4,128,128]{2,1,0:T(8,128)(2,1)} %bitcast.26), channel_id=1, source_target_pairs={{0,16},{4,20},{8,24},{12,28},{16,0},{20,4},{24,8},{28,12},{1,17},{... | collective-permute-start | bytes 393224 | tf_op jit(solution)/shard_map/ppermute | solution.py:60
  7.9 0.9 %constant_dynamic-update-slice_fusion.7 = bf16[32,128,128]{2,1,0:T(8,128)(2,1)S(1)} fusion(bf16[1,4,128,128]{3,2,1,0:T(8,128)(2,1)} %param.8), kind=kLoop, calls=%fused_computation.7 | loop fusion | bytes 262144
  8.8 0.8 %reshape_squeeze.3 = s32[24]{0:T(128)S(1)} reshape(s32[1,1,2,12]{3,2,1,0:T(2,128)} %param.15) | data formatting | bytes 192 | tf_op jit(solution)/shard_map/reshape;squeeze | solution.py:325
  9.6 0.7 %pad_add_fusion = s32[72]{0:T(128)S(1)} fusion(s32[24]{0:T(128)S(1)} %reshape_squeeze.3, s32[12]{0:T(128)} %bitcast.27, s32[36]{0:T(128)} %bitcast.28), kind=kLoop, calls=%fused_computation.8 | loop fusion | flops 144 | bytes 576 | tf_op jit(solution)/shard_map/concatenate | solution.py:325
  11.0 0.6 %index.1 = (s32[1,128]{1,0:T(1,128)S(1)}, f32[1,128]{1,0:T(1,128)S(1)}) custom-call(s32[1,128]{1,0:T(1,128)S(1)} %pad_bitcast_fusion.table_ref, s32[1]{0:T(128)} %bitcast.3.atom_ref, s32[1]{0:T(128)} %bitcast.4.me_ref, f32[1]{0:T(128)S(6)} %copy.18.chem_ref), custom_call_target="tpu_custom_call" | custom-call | flops 2000 | bytes 2000 | tf_op jit(solution)/shard_map/index/pallas_call | solution.py:327
  11.6 2.3 %collective-permute-done.3 = bf16[4,128,128]{2,1,0:T(8,128)(2,1)S(1)} collective-permute-done((bf16[4,128,128]{2,1,0:T(8,128)(2,1)}, bf16[4,128,128]{2,1,0:T(8,128)(2,1)S(1)}, u32[]{:S(2)}, u32[]{:S(2)}) %collective-permute-start.3) | collective-permute-done | bytes 131104 | tf_op jit(solution)/shard_map/ppermute | solution.py:60
  13.9 0.5 %collective-permute-start.4 = (bf16[4,128,128]{2,1,0:T(8,128)(2,1)S(1)}, bf16[4,128,128]{2,1,0:T(8,128)(2,1)S(1)}, u32[]{:S(2)}, u32[]{:S(2)}) collective-permute-start(bf16[4,128,128]{2,1,0:T(8,128)(2,1)S(1)} %collective-permute-done.3), channel_id=1, source_target_pairs={{0,4},{4,0},{8,12},{12,8},{16,20},{20,16},{24,28},{28,24},{1,5},{5... | collective-permute-start | bytes 393224 | tf_op jit(solution)/shard_map/ppermute | solution.py:60
  14.4 0.3 collective-permute-start.5
  14.8 1.7 %collective-permute-start.2 = (bf16[4,128,128]{2,1,0:T(8,128)(2,1)S(1)}, bf16[4,128,128]{2,1,0:T(8,128)(2,1)S(1)}, u32[]{:S(2)}, u32[]{:S(2)}) collective-permute-start(bf16[4,128,128]{2,1,0:T(8,128)(2,1)S(1)} %collective-permute-done), channel_id=1, source_target_pairs={{0,8},{4,12},{8,0},{12,4},{16,24},{20,28},{24,16},{28,20},{1,9},{5... | collective-permute-start | bytes 393224 | tf_op jit(solution)/shard_map/ppermute | solution.py:60
  16.5 2.9 %collective-permute-done.5 = bf16[4,128,128]{2,1,0:T(8,128)(2,1)S(1)} collective-permute-done((bf16[4,128,128]{2,1,0:T(8,128)(2,1)S(1)}, bf16[4,128,128]{2,1,0:T(8,128)(2,1)S(1)}, u32[]{:S(2)}, u32[]{:S(2)}) %collective-permute-start.5) | collective-permute-done | bytes 131104 | tf_op jit(solution)/shard_map/ppermute | solution.py:60
  19.4 1.5 %collective-permute-start.6 = (bf16[4,128,128]{2,1,0:T(8,128)(2,1)S(1)}, bf16[4,128,128]{2,1,0:T(8,128)(2,1)S(1)}, u32[]{:S(2)}, u32[]{:S(2)}) collective-permute-start(bf16[4,128,128]{2,1,0:T(8,128)(2,1)S(1)} %collective-permute-done.5), channel_id=1, source_target_pairs={{0,4},{4,0},{8,12},{12,8},{16,20},{20,16},{24,28},{28,24},{1,5},{5... | collective-permute-start | bytes 393224 | tf_op jit(solution)/shard_map/ppermute | solution.py:60
  21.1 3.3 %collective-permute-done.6 = bf16[4,128,128]{2,1,0:T(8,128)(2,1)S(1)} collective-permute-done((bf16[4,128,128]{2,1,0:T(8,128)(2,1)S(1)}, bf16[4,128,128]{2,1,0:T(8,128)(2,1)S(1)}, u32[]{:S(2)}, u32[]{:S(2)}) %collective-permute-start.6) | collective-permute-done | bytes 131104 | tf_op jit(solution)/shard_map/ppermute | solution.py:60
  24.4 0.0 copy-start
  24.4 3.5 %sign.1 = (bf16[768,128]{1,0:T(8,128)(2,1)S(1)}, bf16[3,128,128]{2,1,0:T(8,128)(2,1)S(1)}, bf16[3,128,128]{2,1,0:T(8,128)(2,1)S(1)}, bf16[3,128,128]{2,1,0:T(8,128)(2,1)S(1)}, bf16[3,128,128]{2,1,0:T(8,128)(2,1)S(1)}) custom-call(s32[1,128]{1,0:T(1,128)S(1)} %get-tuple-element.17.row_ref, f32[1,128]{1,0:T(1,128)S(1)} %get-tuple-element.18.level_ref, ...), custom_call_target="tpu_custom_call" | custom-call | flops 1811939328 | bytes 2359296 | tf_op jit(solution)/shard_map/sign/pallas_call | solution.py:352
  27.9 0.1 collective-permute-start.7
  28.0 1.6 %collective-permute-start.8 = (bf16[3,128,128]{2,1,0:T(8,128)(2,1)S(1)}, bf16[3,128,128]{2,1,0:T(8,128)(2,1)S(1)}, u32[]{:S(2)}, u32[]{:S(2)}) collective-permute-start(bf16[3,128,128]{2,1,0:T(8,128)(2,1)S(1)} %get-tuple-element.24), channel_id=1, source_target_pairs={{0,2},{1,3},{2,0},{3,1},{4,6},{5,7},{6,4},{7,5},{8,10},{9,11},{10,... | collective-permute-start | bytes 294920 | tf_op jit(solution)/shard_map/ppermute | solution.py:87
  29.5 0.3 collective-permute-start.9
  29.9 1.3 %shard_map.103 = (f32[8,1024]{1,0:T(8,128)S(1)}, bf16[768,128]{1,0:T(8,128)(2,1)}) custom-call(s32[1,128]{1,0:T(1,128)S(1)} %get-tuple-element.17.row_ref, bf16[8,128,1024]{2,1,0:T(8,128)(2,1)S(1)} %bitcast.14, bf16[768,128]{1,0:T(8,128)(2,1)S(1)} %get-tuple-element.19.column_ref, bf16[3,128,128]{2,1,0:T(8,128)(2,1)S(1)} %get-tuple-element.20.rest_0_, ...), custom_call_target="tpu_custom_call" | custom-call | flops 201326592 | bytes 3145728 | tf_op jit(solution)/shard_map/pallas_call | solution.py:382
  31.2 2.6 %collective-permute-done.8.rest_0_ = bf16[3,128,128]{2,1,0:T(8,128)(2,1)S(1)} collective-permute-done((bf16[3,128,128]{2,1,0:T(8,128)(2,1)S(1)}, bf16[3,128,128]{2,1,0:T(8,128)(2,1)S(1)}, u32[]{:S(2)}, u32[]{:S(2)}) %collective-permute-start.8) | collective-permute-done | bytes 98336 | tf_op jit(solution)/shard_map/ppermute | solution.py:87
  33.7 0.5 %shard_map.104.near_ref = f32[8,1024]{1,0:T(8,128)S(1)} custom-call(s32[1,128]{1,0:T(1,128)S(1)} %get-tuple-element.17.row_ref, bf16[8,128,1024]{2,1,0:T(8,128)(2,1)S(1)} %bitcast.15, f32[8,1024]{1,0:T(8,128)S(1)} %get-tuple-element.23.near_ref, bf16[3,128,128]{2,1,0:T(8,128)(2,1)S(1)} %collective-permute-done.8.rest_0_), custom_call_target="tpu_custom_call" | custom-call | flops 100663296 | bytes 1572864 | tf_op jit(solution)/shard_map/pallas_call | solution.py:382
  34.2 0.5 %collective-permute-done.9.rest_0_ = bf16[3,128,128]{2,1,0:T(8,128)(2,1)S(1)} collective-permute-done((bf16[3,128,128]{2,1,0:T(8,128)(2,1)S(1)}, bf16[3,128,128]{2,1,0:T(8,128)(2,1)S(1)}, u32[]{:S(2)}, u32[]{:S(2)}) %collective-permute-start.9) | collective-permute-done | bytes 98336 | tf_op jit(solution)/shard_map/ppermute | solution.py:87
  34.8 1.0 %shard_map.105 = (f32[1,1024]{1,0:T(1,128)S(1)}, bf16[3,128,128]{2,1,0:T(8,128)(2,1)S(1)}) custom-call(s32[1,128]{1,0:T(1,128)S(1)} %get-tuple-element.17.row_ref, bf16[8,128,1024]{2,1,0:T(8,128)(2,1)S(1)} %bitcast.16, f32[1,1024]{1,0:T(1,128)S(1)} %bitcast.22, f32[1,1024]{1,0:T(1,128)S(1)} %bitcast.19, f32[8,1024]{1,0:T(8,128)S(1)} %shard_map.104.near_ref, ...), custom_call_target="tpu_custom_call" | custom-call | flops 100663296 | bytes 1572864 | tf_op jit(solution)/shard_map/pallas_call | solution.py:382
  35.7 1.2 %shard_map.106 = (bf16[3,128,128]{2,1,0:T(8,128)(2,1)S(1)}, bf16[3,128,128]{2,1,0:T(8,128)(2,1)S(1)}, f32[1,1024]{1,0:T(1,128)}) custom-call(s32[1,128]{1,0:T(1,128)S(1)} %get-tuple-element.17.row_ref, bf16[8,128,1024]{2,1,0:T(8,128)(2,1)S(1)} %bitcast.17, f32[1,1024]{1,0:T(1,128)S(1)} %bitcast.20, f32[1,1024]{1,0:T(1,128)S(1)} %get-tuple-element.26.found_ref), custom_call_target="tpu_custom_call" | custom-call | flops 201326592 | bytes 3145728 | tf_op jit(solution)/shard_map/pallas_call | solution.py:382
  36.9 0.5 %shard_map.107 = bf16[3,128,128]{2,1,0:T(8,128)(2,1)S(1)} custom-call(s32[1,128]{1,0:T(1,128)S(1)} %get-tuple-element.17.row_ref, bf16[8,128,1024]{2,1,0:T(8,128)(2,1)S(1)} %bitcast.18, f32[1,1024]{1,0:T(1,128)S(1)} %bitcast.21, f32[1,1024]{1,0:T(1,128)S(1)} %get-tuple-element.26.found_ref), custom_call_target="tpu_custom_call" | custom-call | flops 100663296 | bytes 1572864 | tf_op jit(solution)/shard_map/pallas_call | solution.py:382
  37.4 0.4 collective-permute-start.10
  37.8 1.5 %collective-permute-start.11 = (bf16[3,128,128]{2,1,0:T(8,128)(2,1)S(1)}, bf16[3,128,128]{2,1,0:T(8,128)(2,1)S(1)}, u32[]{:S(2)}, u32[]{:S(2)}) collective-permute-start(bf16[3,128,128]{2,1,0:T(8,128)(2,1)S(1)} %shard_map.107), channel_id=1, source_target_pairs={{0,2},{1,3},{2,0},{3,1},{4,6},{5,7},{6,4},{7,5},{8,10},{9,11},{10,... | collective-permute-start | bytes 294920 | tf_op jit(solution)/shard_map/ppermute | solution.py:87
  39.3 0.0 collective-permute-start.12
  39.3 3.7 %collective-permute-done.11.rest_2_ = bf16[3,128,128]{2,1,0:T(8,128)(2,1)S(1)} collective-permute-done((bf16[3,128,128]{2,1,0:T(8,128)(2,1)S(1)}, bf16[3,128,128]{2,1,0:T(8,128)(2,1)S(1)}, u32[]{:S(2)}, u32[]{:S(2)}) %collective-permute-start.11) | collective-permute-done | bytes 98336 | tf_op jit(solution)/shard_map/ppermute | solution.py:87
  43.0 1.4 %collective-permute-done.12.rest_3_ = bf16[3,128,128]{2,1,0:T(8,128)(2,1)S(1)} collective-permute-done((bf16[3,128,128]{2,1,0:T(8,128)(2,1)S(1)}, bf16[3,128,128]{2,1,0:T(8,128)(2,1)S(1)}, u32[]{:S(2)}, u32[]{:S(2)}) %collective-permute-start.12) | collective-permute-done | bytes 98336 | tf_op jit(solution)/shard_map/ppermute | solution.py:87
  44.4 0.9 %sum.1 = f32[768,128]{1,0:T(8,128)} custom-call(s32[1,128]{1,0:T(1,128)S(1)} %get-tuple-element.17.row_ref, bf16[3,128,128]{2,1,0:T(8,128)(2,1)S(1)} %get-tuple-element.28.rest_0_, bf16[3,128,128]{2,1,0:T(8,128)(2,1)S(1)} %collective-permute-done.10.rest_1_, bf16[3,128,128]{2,1,0:T(8,128)(2,1)S(1)} %collective-permute-done.11.rest_2_, ...), custom_call_target="tpu_custom_call" | custom-call | tf_op jit(solution)/shard_map/sum/pallas_call | solution.py:430
  (19 shorter events, 0.2 us)
Async XLA Ops:
  0.6 14.1 %collective-permute-start = (bf16[4,128,128]{2,1,0:T(8,128)(2,1)}, bf16[4,128,128]{2,1,0:T(8,128)(2,1)S(1)}, u32[]{:S(2)}, u32[]{:S(2)}) collective-permute-start(bf16[4,128,128]{2,1,0:T(8,128)(2,1)} %bitcast.24), channel_id=1, source_target_pairs={{0,4},{4,0},{8,12},{12,8},{16,20},{20,16},{24,28},{28,24},{1,5},{5... | collective-permute-start | bytes 393224 | tf_op jit(solution)/shard_map/ppermute | solution.py:60
  3.7 12.8 %collective-permute-start.1 = (bf16[4,128,128]{2,1,0:T(8,128)(2,1)}, bf16[4,128,128]{2,1,0:T(8,128)(2,1)S(1)}, u32[]{:S(2)}, u32[]{:S(2)}) collective-permute-start(bf16[4,128,128]{2,1,0:T(8,128)(2,1)} %bitcast.25), channel_id=1, source_target_pairs={{0,8},{4,12},{8,0},{12,4},{16,24},{20,28},{24,16},{28,20},{1,9},{5... | collective-permute-start | bytes 393224 | tf_op jit(solution)/shard_map/ppermute | solution.py:60
  5.3 8.7 %collective-permute-start.3 = (bf16[4,128,128]{2,1,0:T(8,128)(2,1)}, bf16[4,128,128]{2,1,0:T(8,128)(2,1)S(1)}, u32[]{:S(2)}, u32[]{:S(2)}) collective-permute-start(bf16[4,128,128]{2,1,0:T(8,128)(2,1)} %bitcast.26), channel_id=1, source_target_pairs={{0,16},{4,20},{8,24},{12,28},{16,0},{20,4},{24,8},{28,12},{1,17},{... | collective-permute-start | bytes 393224 | tf_op jit(solution)/shard_map/ppermute | solution.py:60
  13.9 7.1 %collective-permute-start.4 = (bf16[4,128,128]{2,1,0:T(8,128)(2,1)S(1)}, bf16[4,128,128]{2,1,0:T(8,128)(2,1)S(1)}, u32[]{:S(2)}, u32[]{:S(2)}) collective-permute-start(bf16[4,128,128]{2,1,0:T(8,128)(2,1)S(1)} %collective-permute-done.3), channel_id=1, source_target_pairs={{0,4},{4,0},{8,12},{12,8},{16,20},{20,16},{24,28},{28,24},{1,5},{5... | collective-permute-start | bytes 393224 | tf_op jit(solution)/shard_map/ppermute | solution.py:60
  14.4 5.0 %collective-permute-start.5 = (bf16[4,128,128]{2,1,0:T(8,128)(2,1)S(1)}, bf16[4,128,128]{2,1,0:T(8,128)(2,1)S(1)}, u32[]{:S(2)}, u32[]{:S(2)}) collective-permute-start(bf16[4,128,128]{2,1,0:T(8,128)(2,1)S(1)} %collective-permute-done.3), channel_id=1, source_target_pairs={{0,8},{4,12},{8,0},{12,4},{16,24},{20,28},{24,16},{28,20},{1,9},{5... | collective-permute-start | bytes 393224 | tf_op jit(solution)/shard_map/ppermute | solution.py:60
  14.8 6.2 %collective-permute-start.2 = (bf16[4,128,128]{2,1,0:T(8,128)(2,1)S(1)}, bf16[4,128,128]{2,1,0:T(8,128)(2,1)S(1)}, u32[]{:S(2)}, u32[]{:S(2)}) collective-permute-start(bf16[4,128,128]{2,1,0:T(8,128)(2,1)S(1)} %collective-permute-done), channel_id=1, source_target_pairs={{0,8},{4,12},{8,0},{12,4},{16,24},{20,28},{24,16},{28,20},{1,9},{5... | collective-permute-start | bytes 393224 | tf_op jit(solution)/shard_map/ppermute | solution.py:60
  19.4 5.0 %collective-permute-start.6 = (bf16[4,128,128]{2,1,0:T(8,128)(2,1)S(1)}, bf16[4,128,128]{2,1,0:T(8,128)(2,1)S(1)}, u32[]{:S(2)}, u32[]{:S(2)}) collective-permute-start(bf16[4,128,128]{2,1,0:T(8,128)(2,1)S(1)} %collective-permute-done.5), channel_id=1, source_target_pairs={{0,4},{4,0},{8,12},{12,8},{16,20},{20,16},{24,28},{28,24},{1,5},{5... | collective-permute-start | bytes 393224 | tf_op jit(solution)/shard_map/ppermute | solution.py:60
  24.4 5.5 %copy-start = (bf16[1,1,8,128,1024]{4,3,2,1,0:T(8,128)(2,1)S(1)}, bf16[1,1,8,128,1024]{4,3,2,1,0:T(8,128)(2,1)}, u32[]{:S(2)}) copy-start(bf16[1,1,8,128,1024]{4,3,2,1,0:T(8,128)(2,1)} %param.11) | copy-start | bytes 6291460
  27.9 1.9 %collective-permute-start.7 = (bf16[3,128,128]{2,1,0:T(8,128)(2,1)S(1)}, bf16[3,128,128]{2,1,0:T(8,128)(2,1)S(1)}, u32[]{:S(2)}, u32[]{:S(2)}) collective-permute-start(bf16[3,128,128]{2,1,0:T(8,128)(2,1)S(1)} %get-tuple-element.21), channel_id=1, source_target_pairs={{0,1},{1,0},{2,3},{3,2},{4,5},{5,4},{6,7},{7,6},{8,9},{9,8},{10,11... | collective-permute-start | bytes 294920 | tf_op jit(solution)/shard_map/ppermute | solution.py:87
  28.0 5.7 %collective-permute-start.8 = (bf16[3,128,128]{2,1,0:T(8,128)(2,1)S(1)}, bf16[3,128,128]{2,1,0:T(8,128)(2,1)S(1)}, u32[]{:S(2)}, u32[]{:S(2)}) collective-permute-start(bf16[3,128,128]{2,1,0:T(8,128)(2,1)S(1)} %get-tuple-element.24), channel_id=1, source_target_pairs={{0,2},{1,3},{2,0},{3,1},{4,6},{5,7},{6,4},{7,5},{8,10},{9,11},{10,... | collective-permute-start | bytes 294920 | tf_op jit(solution)/shard_map/ppermute | solution.py:87
  29.5 5.2 %collective-permute-start.9 = (bf16[3,128,128]{2,1,0:T(8,128)(2,1)S(1)}, bf16[3,128,128]{2,1,0:T(8,128)(2,1)S(1)}, u32[]{:S(2)}, u32[]{:S(2)}) collective-permute-start(bf16[3,128,128]{2,1,0:T(8,128)(2,1)S(1)} %get-tuple-element.25), channel_id=1, source_target_pairs={{0,3},{1,2},{2,1},{3,0},{4,7},{5,6},{6,5},{7,4},{8,11},{9,10},{10,... | collective-permute-start | bytes 294920 | tf_op jit(solution)/shard_map/ppermute | solution.py:87
  29.8 4.9 %copy-start.1 = (f32[1,1,1024]{2,1,0:T(1,128)S(1)}, f32[1,1,1024]{2,1,0:T(1,128)}, u32[]{:S(2)}) copy-start(f32[1,1,1024]{2,1,0:T(1,128)} %param.13) | copy-start | bytes 12292
  29.8 4.9 %copy-start.2 = (f32[1,1,1024]{2,1,0:T(1,128)S(1)}, f32[1,1,1024]{2,1,0:T(1,128)}, u32[]{:S(2)}) copy-start(f32[1,1,1024]{2,1,0:T(1,128)} %param.12) | copy-start | bytes 12292
  37.4 1.9 %collective-permute-start.10 = (bf16[3,128,128]{2,1,0:T(8,128)(2,1)S(1)}, bf16[3,128,128]{2,1,0:T(8,128)(2,1)S(1)}, u32[]{:S(2)}, u32[]{:S(2)}) collective-permute-start(bf16[3,128,128]{2,1,0:T(8,128)(2,1)S(1)} %get-tuple-element.29), channel_id=1, source_target_pairs={{0,1},{1,0},{2,3},{3,2},{4,5},{5,4},{6,7},{7,6},{8,9},{9,8},{10,11... | collective-permute-start | bytes 294920 | tf_op jit(solution)/shard_map/ppermute | solution.py:87
  37.8 5.2 %collective-permute-start.11 = (bf16[3,128,128]{2,1,0:T(8,128)(2,1)S(1)}, bf16[3,128,128]{2,1,0:T(8,128)(2,1)S(1)}, u32[]{:S(2)}, u32[]{:S(2)}) collective-permute-start(bf16[3,128,128]{2,1,0:T(8,128)(2,1)S(1)} %shard_map.107), channel_id=1, source_target_pairs={{0,2},{1,3},{2,0},{3,1},{4,6},{5,7},{6,4},{7,5},{8,10},{9,11},{10,... | collective-permute-start | bytes 294920 | tf_op jit(solution)/shard_map/ppermute | solution.py:87
  39.3 5.1 %collective-permute-start.12 = (bf16[3,128,128]{2,1,0:T(8,128)(2,1)S(1)}, bf16[3,128,128]{2,1,0:T(8,128)(2,1)S(1)}, u32[]{:S(2)}, u32[]{:S(2)}) collective-permute-start(bf16[3,128,128]{2,1,0:T(8,128)(2,1)S(1)} %get-tuple-element.30), channel_id=1, source_target_pairs={{0,3},{1,2},{2,1},{3,0},{4,7},{5,6},{6,5},{7,4},{8,11},{9,10},{10,... | collective-permute-start | bytes 294920 | tf_op jit(solution)/shard_map/ppermute | solution.py:87

commit v5 on v4

--- a/solution.py
+++ b/solution.py
@@ -247,18 +247,19 @@
     rest[-1][...] = pair_density(slots, near_ref[...], full, table_ref, groups)
 
 
-def mid_partials_kernel(capacity, steps, row_ref, table_ref, weight_ref, found_ref, *rest):
+def partials_kernel(capacity, steps, row_ref, table_ref, weight_ref, found_ref, *rest):
     slots = tile_slots(row_ref[...], steps, capacity)
     pair_partials(slots, weight_ref[...] * found_ref[...], table_ref, dict(zip(steps, rest)))
 
 
 def last_kernel(
-    capacity, full, steps, row_ref, table_ref, core_ref, weight_ref, near_ref, *rest
+    capacity, full, steps, out_steps, row_ref, table_ref, core_ref, weight_ref, near_ref, *rest
 ):
     groups = dict(zip(steps, rest[: len(steps)]))
     potential_ref = rest[len(steps)]
-    out_groups = dict(zip(steps, rest[len(steps) + 1 :]))
+    out_groups = dict(zip(out_steps, rest[len(steps) + 1 :]))
     slots = tile_slots(row_ref[...], steps, capacity)
+    out_slots = tile_slots(row_ref[...], out_steps, capacity)
     total = pair_density(slots, near_ref[...], full, table_ref, groups)
     valence = jnp.sum(total, axis=0, keepdims=True)
     value = jnp.maximum(core_ref[...] + valence, density_floor)
@@ -266,7 +267,7 @@
     root = root - (root * root * root - value) / (3.0 * root * root)
     potential = -slater_factor * root
     potential_ref[...] = potential
-    pair_partials(slots, weight_ref[...] * potential, table_ref, out_groups)
+    pair_partials(out_slots, weight_ref[...] * potential, table_ref, out_groups)
 
 
 def near_partials_kernel(
@@ -406,19 +407,19 @@
     )
     weight = point_weights[0]
     found, *sent = step_call(
-        functools.partial(last_kernel, capacity, full, last),
+        functools.partial(last_kernel, capacity, full, last, mid),
         last,
-        [line] + [group] * len(last),
+        [line] + [group] * len(mid),
         [row, tables, core_density[0], weight, total, *[incoming[k] for k in last]],
     )
-    partials = dict(zip(last, sent))
+    partials = dict(zip(mid, sent))
     sent = step_call(
-        functools.partial(mid_partials_kernel, capacity, mid),
-        mid,
-        [group] * len(mid),
+        functools.partial(partials_kernel, capacity, last),
+        last,
+        [group] * len(last),
         [row, tables, weight, found],
     )
-    partials.update(zip(mid, sent))
+    partials.update(zip(last, sent))
     *sent, potential = step_call(
         functools.partial(near_partials_kernel, capacity, near),
         near,

time: 45.5 us -> 46.1 us (1.013)
  no operation moved by 1% of the time
where the time goes in v5:
time: 46.1 us; the launch traced here: 45.9 us
  waiting for transfers between devices  17.1 us (37%)
  starting transfers between devices  15.4 us (33%)
  Pallas kernels  9.45 us (20%)
  local copies, waits for them, and re-layouts  1.86 us (4%)
  between operations  1.42 us (3%)
  other arithmetic  0.75 us (2%)
    ppermute x7, starting transfers between devices, gathered_blocks(): parts[offset] = lax.ppermute(parts[offset ^ step], 'atoms', pairs)  11.3 us
    ppermute x7, waiting for transfers between devices, gathered_blocks(): parts[offset] = lax.ppermute(parts[offset ^ step], 'atoms', pairs)  8.54 us
    ppermute x6, waiting for transfers between devices, exchange(): lax.ppermute(groups[step], 'space', pairs)  8.52 us
    pallas_call x5, Pallas kernels, step_call(): pl.pallas_call(kernel, in_specs=[VMEM] * len(operands), out_shape=out_sha...  4.44 us
    ppermute x6, starting transfers between devices, exchange(): lax.ppermute(groups[step], 'space', pairs)  4.12 us
    pallas_call x1, Pallas kernels, per_device(): pl.pallas_call(functools.partial(sign_kernel, devices, capacity), name='s...  3.5 us
    unnamed x13, local copies, waits for them, and re-layouts  1.08 us
  transfers between devices with their start and end apart: 13, of which 7 were waited for; matrix products, arithmetic and copies ran while one was open for 6% of the time, Pallas kernels for 5%

profile of v5, /device:TPU:0, one launch (start us, length us, event | category | flops | bytes accessed | tf_op | source)
XLA Modules:
  0.0 45.9 jit_solution(12576231914713240811)
XLA Ops:
  0.6 3.1 %collective-permute-start = (bf16[4,128,128]{2,1,0:T(8,128)(2,1)}, bf16[4,128,128]{2,1,0:T(8,128)(2,1)S(1)}, u32[]{:S(2)}, u32[]{:S(2)}) collective-permute-start(bf16[4,128,128]{2,1,0:T(8,128)(2,1)} %bitcast.24), channel_id=1, source_target_pairs={{0,4},{4,0},{8,12},{12,8},{16,20},{20,16},{24,28},{28,24},{1,5},{5... | collective-permute-start | bytes 393224 | tf_op jit(solution)/shard_map/ppermute | solution.py:60
  3.7 1.6 %collective-permute-start.1 = (bf16[4,128,128]{2,1,0:T(8,128)(2,1)}, bf16[4,128,128]{2,1,0:T(8,128)(2,1)S(1)}, u32[]{:S(2)}, u32[]{:S(2)}) collective-permute-start(bf16[4,128,128]{2,1,0:T(8,128)(2,1)} %bitcast.25), channel_id=1, source_target_pairs={{0,8},{4,12},{8,0},{12,4},{16,24},{20,28},{24,16},{28,20},{1,9},{5... | collective-permute-start | bytes 393224 | tf_op jit(solution)/shard_map/ppermute | solution.py:60
  5.3 2.6 %collective-permute-start.3 = (bf16[4,128,128]{2,1,0:T(8,128)(2,1)}, bf16[4,128,128]{2,1,0:T(8,128)(2,1)S(1)}, u32[]{:S(2)}, u32[]{:S(2)}) collective-permute-start(bf16[4,128,128]{2,1,0:T(8,128)(2,1)} %bitcast.26), channel_id=1, source_target_pairs={{0,16},{4,20},{8,24},{12,28},{16,0},{20,4},{24,8},{28,12},{1,17},{... | collective-permute-start | bytes 393224 | tf_op jit(solution)/shard_map/ppermute | solution.py:60
  7.9 0.9 %constant_dynamic-update-slice_fusion.7 = bf16[32,128,128]{2,1,0:T(8,128)(2,1)S(1)} fusion(bf16[1,4,128,128]{3,2,1,0:T(8,128)(2,1)} %param.8), kind=kLoop, calls=%fused_computation.7 | loop fusion | bytes 262144
  8.8 0.8 %reshape_squeeze.3 = s32[24]{0:T(128)S(1)} reshape(s32[1,1,2,12]{3,2,1,0:T(2,128)} %param.15) | data formatting | bytes 192 | tf_op jit(solution)/shard_map/reshape;squeeze | solution.py:326
  9.6 0.7 %pad_add_fusion = s32[72]{0:T(128)S(1)} fusion(s32[24]{0:T(128)S(1)} %reshape_squeeze.3, s32[12]{0:T(128)} %bitcast.27, s32[36]{0:T(128)} %bitcast.28), kind=kLoop, calls=%fused_computation.8 | loop fusion | flops 144 | bytes 576 | tf_op jit(solution)/shard_map/concatenate | solution.py:326
  11.0 0.6 %index.1 = (s32[1,128]{1,0:T(1,128)S(1)}, f32[1,128]{1,0:T(1,128)S(1)}) custom-call(s32[1,128]{1,0:T(1,128)S(1)} %pad_bitcast_fusion.table_ref, s32[1]{0:T(128)} %bitcast.3.atom_ref, s32[1]{0:T(128)} %bitcast.4.me_ref, f32[1]{0:T(128)S(6)} %copy.18.chem_ref), custom_call_target="tpu_custom_call" | custom-call | flops 2000 | bytes 2000 | tf_op jit(solution)/shard_map/index/pallas_call | solution.py:328
  11.6 2.3 %collective-permute-done.3 = bf16[4,128,128]{2,1,0:T(8,128)(2,1)S(1)} collective-permute-done((bf16[4,128,128]{2,1,0:T(8,128)(2,1)}, bf16[4,128,128]{2,1,0:T(8,128)(2,1)S(1)}, u32[]{:S(2)}, u32[]{:S(2)}) %collective-permute-start.3) | collective-permute-done | bytes 131104 | tf_op jit(solution)/shard_map/ppermute | solution.py:60
  13.9 0.5 %collective-permute-start.4 = (bf16[4,128,128]{2,1,0:T(8,128)(2,1)S(1)}, bf16[4,128,128]{2,1,0:T(8,128)(2,1)S(1)}, u32[]{:S(2)}, u32[]{:S(2)}) collective-permute-start(bf16[4,128,128]{2,1,0:T(8,128)(2,1)S(1)} %collective-permute-done.3), channel_id=1, source_target_pairs={{0,4},{4,0},{8,12},{12,8},{16,20},{20,16},{24,28},{28,24},{1,5},{5... | collective-permute-start | bytes 393224 | tf_op jit(solution)/shard_map/ppermute | solution.py:60
  14.4 0.3 collective-permute-start.5
  14.8 1.7 %collective-permute-start.2 = (bf16[4,128,128]{2,1,0:T(8,128)(2,1)S(1)}, bf16[4,128,128]{2,1,0:T(8,128)(2,1)S(1)}, u32[]{:S(2)}, u32[]{:S(2)}) collective-permute-start(bf16[4,128,128]{2,1,0:T(8,128)(2,1)S(1)} %collective-permute-done), channel_id=1, source_target_pairs={{0,8},{4,12},{8,0},{12,4},{16,24},{20,28},{24,16},{28,20},{1,9},{5... | collective-permute-start | bytes 393224 | tf_op jit(solution)/shard_map/ppermute | solution.py:60
  16.5 2.9 %collective-permute-done.5 = bf16[4,128,128]{2,1,0:T(8,128)(2,1)S(1)} collective-permute-done((bf16[4,128,128]{2,1,0:T(8,128)(2,1)S(1)}, bf16[4,128,128]{2,1,0:T(8,128)(2,1)S(1)}, u32[]{:S(2)}, u32[]{:S(2)}) %collective-permute-start.5) | collective-permute-done | bytes 131104 | tf_op jit(solution)/shard_map/ppermute | solution.py:60
  19.4 1.5 %collective-permute-start.6 = (bf16[4,128,128]{2,1,0:T(8,128)(2,1)S(1)}, bf16[4,128,128]{2,1,0:T(8,128)(2,1)S(1)}, u32[]{:S(2)}, u32[]{:S(2)}) collective-permute-start(bf16[4,128,128]{2,1,0:T(8,128)(2,1)S(1)} %collective-permute-done.5), channel_id=1, source_target_pairs={{0,4},{4,0},{8,12},{12,8},{16,20},{20,16},{24,28},{28,24},{1,5},{5... | collective-permute-start | bytes 393224 | tf_op jit(solution)/shard_map/ppermute | solution.py:60
  21.1 3.3 %collective-permute-done.6 = bf16[4,128,128]{2,1,0:T(8,128)(2,1)S(1)} collective-permute-done((bf16[4,128,128]{2,1,0:T(8,128)(2,1)S(1)}, bf16[4,128,128]{2,1,0:T(8,128)(2,1)S(1)}, u32[]{:S(2)}, u32[]{:S(2)}) %collective-permute-start.6) | collective-permute-done | bytes 131104 | tf_op jit(solution)/shard_map/ppermute | solution.py:60
  24.4 0.0 copy-start
  24.4 3.5 %sign.1 = (bf16[768,128]{1,0:T(8,128)(2,1)S(1)}, bf16[3,128,128]{2,1,0:T(8,128)(2,1)S(1)}, bf16[3,128,128]{2,1,0:T(8,128)(2,1)S(1)}, bf16[3,128,128]{2,1,0:T(8,128)(2,1)S(1)}, bf16[3,128,128]{2,1,0:T(8,128)(2,1)S(1)}) custom-call(s32[1,128]{1,0:T(1,128)S(1)} %get-tuple-element.17.row_ref, f32[1,128]{1,0:T(1,128)S(1)} %get-tuple-element.18.level_ref, ...), custom_call_target="tpu_custom_call" | custom-call | flops 1811939328 | bytes 2359296 | tf_op jit(solution)/shard_map/sign/pallas_call | solution.py:353
  27.9 0.1 collective-permute-start.7
  28.0 1.6 %collective-permute-start.8 = (bf16[3,128,128]{2,1,0:T(8,128)(2,1)S(1)}, bf16[3,128,128]{2,1,0:T(8,128)(2,1)S(1)}, u32[]{:S(2)}, u32[]{:S(2)}) collective-permute-start(bf16[3,128,128]{2,1,0:T(8,128)(2,1)S(1)} %get-tuple-element.24), channel_id=1, source_target_pairs={{0,2},{1,3},{2,0},{3,1},{4,6},{5,7},{6,4},{7,5},{8,10},{9,11},{10,... | collective-permute-start | bytes 294920 | tf_op jit(solution)/shard_map/ppermute | solution.py:87
  29.5 0.3 collective-permute-start.9
  29.9 1.3 %shard_map.103 = (f32[8,1024]{1,0:T(8,128)S(1)}, bf16[768,128]{1,0:T(8,128)(2,1)}) custom-call(s32[1,128]{1,0:T(1,128)S(1)} %get-tuple-element.17.row_ref, bf16[8,128,1024]{2,1,0:T(8,128)(2,1)S(1)} %bitcast.14, bf16[768,128]{1,0:T(8,128)(2,1)S(1)} %get-tuple-element.19.column_ref, bf16[3,128,128]{2,1,0:T(8,128)(2,1)S(1)} %get-tuple-element.20.rest_0_, ...), custom_call_target="tpu_custom_call" | custom-call | flops 201326592 | bytes 3145728 | tf_op jit(solution)/shard_map/pallas_call | solution.py:383
  31.2 2.6 %collective-permute-done.8.rest_0_ = bf16[3,128,128]{2,1,0:T(8,128)(2,1)S(1)} collective-permute-done((bf16[3,128,128]{2,1,0:T(8,128)(2,1)S(1)}, bf16[3,128,128]{2,1,0:T(8,128)(2,1)S(1)}, u32[]{:S(2)}, u32[]{:S(2)}) %collective-permute-start.8) | collective-permute-done | bytes 98336 | tf_op jit(solution)/shard_map/ppermute | solution.py:87
  33.7 0.5 %shard_map.104.near_ref = f32[8,1024]{1,0:T(8,128)S(1)} custom-call(s32[1,128]{1,0:T(1,128)S(1)} %get-tuple-element.17.row_ref, bf16[8,128,1024]{2,1,0:T(8,128)(2,1)S(1)} %bitcast.15, f32[8,1024]{1,0:T(8,128)S(1)} %get-tuple-element.23.near_ref, bf16[3,128,128]{2,1,0:T(8,128)(2,1)S(1)} %collective-permute-done.8.rest_0_), custom_call_target="tpu_custom_call" | custom-call | flops 100663296 | bytes 1572864 | tf_op jit(solution)/shard_map/pallas_call | solution.py:383
  34.2 0.5 %collective-permute-done.9.rest_0_ = bf16[3,128,128]{2,1,0:T(8,128)(2,1)S(1)} collective-permute-done((bf16[3,128,128]{2,1,0:T(8,128)(2,1)S(1)}, bf16[3,128,128]{2,1,0:T(8,128)(2,1)S(1)}, u32[]{:S(2)}, u32[]{:S(2)}) %collective-permute-start.9) | collective-permute-done | bytes 98336 | tf_op jit(solution)/shard_map/ppermute | solution.py:87
  34.8 1.0 %shard_map.105 = (f32[1,1024]{1,0:T(1,128)S(1)}, bf16[3,128,128]{2,1,0:T(8,128)(2,1)S(1)}) custom-call(s32[1,128]{1,0:T(1,128)S(1)} %get-tuple-element.17.row_ref, bf16[8,128,1024]{2,1,0:T(8,128)(2,1)S(1)} %bitcast.16, f32[1,1024]{1,0:T(1,128)S(1)} %bitcast.22, f32[1,1024]{1,0:T(1,128)S(1)} %bitcast.19, f32[8,1024]{1,0:T(8,128)S(1)} %shard_map.104.near_ref, ...), custom_call_target="tpu_custom_call" | custom-call | flops 100663296 | bytes 1572864 | tf_op jit(solution)/shard_map/pallas_call | solution.py:383
  35.8 1.2 %shard_map.106 = (bf16[3,128,128]{2,1,0:T(8,128)(2,1)S(1)}, bf16[3,128,128]{2,1,0:T(8,128)(2,1)S(1)}, f32[1,1024]{1,0:T(1,128)}) custom-call(s32[1,128]{1,0:T(1,128)S(1)} %get-tuple-element.17.row_ref, bf16[8,128,1024]{2,1,0:T(8,128)(2,1)S(1)} %bitcast.17, f32[1,1024]{1,0:T(1,128)S(1)} %bitcast.20, f32[1,1024]{1,0:T(1,128)S(1)} %get-tuple-element.26.found_ref), custom_call_target="tpu_custom_call" | custom-call | flops 201326592 | bytes 3145728 | tf_op jit(solution)/shard_map/pallas_call | solution.py:383
  36.9 0.5 %shard_map.107 = bf16[3,128,128]{2,1,0:T(8,128)(2,1)S(1)} custom-call(s32[1,128]{1,0:T(1,128)S(1)} %get-tuple-element.17.row_ref, bf16[8,128,1024]{2,1,0:T(8,128)(2,1)S(1)} %bitcast.18, f32[1,1024]{1,0:T(1,128)S(1)} %bitcast.21, f32[1,1024]{1,0:T(1,128)S(1)} %get-tuple-element.26.found_ref), custom_call_target="tpu_custom_call" | custom-call | flops 100663296 | bytes 1572864 | tf_op jit(solution)/shard_map/pallas_call | solution.py:383
  37.4 0.4 collective-permute-start.10
  37.8 1.2 %collective-permute-start.12 = (bf16[3,128,128]{2,1,0:T(8,128)(2,1)S(1)}, bf16[3,128,128]{2,1,0:T(8,128)(2,1)S(1)}, u32[]{:S(2)}, u32[]{:S(2)}) collective-permute-start(bf16[3,128,128]{2,1,0:T(8,128)(2,1)S(1)} %shard_map.107), channel_id=1, source_target_pairs={{0,3},{1,2},{2,1},{3,0},{4,7},{5,6},{6,5},{7,4},{8,11},{9,10},{10,... | collective-permute-start | bytes 294920 | tf_op jit(solution)/shard_map/ppermute | solution.py:87
  39.1 0.5 %collective-permute-start.11 = (bf16[3,128,128]{2,1,0:T(8,128)(2,1)S(1)}, bf16[3,128,128]{2,1,0:T(8,128)(2,1)S(1)}, u32[]{:S(2)}, u32[]{:S(2)}) collective-permute-start(bf16[3,128,128]{2,1,0:T(8,128)(2,1)S(1)} %get-tuple-element.30), channel_id=1, source_target_pairs={{0,2},{1,3},{2,0},{3,1},{4,6},{5,7},{6,4},{7,5},{8,10},{9,11},{10,... | collective-permute-start | bytes 294920 | tf_op jit(solution)/shard_map/ppermute | solution.py:87
  39.6 3.0 %collective-permute-done.12.rest_3_ = bf16[3,128,128]{2,1,0:T(8,128)(2,1)S(1)} collective-permute-done((bf16[3,128,128]{2,1,0:T(8,128)(2,1)S(1)}, bf16[3,128,128]{2,1,0:T(8,128)(2,1)S(1)}, u32[]{:S(2)}, u32[]{:S(2)}) %collective-permute-start.12) | collective-permute-done | bytes 98336 | tf_op jit(solution)/shard_map/ppermute | solution.py:87
  42.6 2.4 %collective-permute-done.11.rest_2_ = bf16[3,128,128]{2,1,0:T(8,128)(2,1)S(1)} collective-permute-done((bf16[3,128,128]{2,1,0:T(8,128)(2,1)S(1)}, bf16[3,128,128]{2,1,0:T(8,128)(2,1)S(1)}, u32[]{:S(2)}, u32[]{:S(2)}) %collective-permute-start.11) | collective-permute-done | bytes 98336 | tf_op jit(solution)/shard_map/ppermute | solution.py:87
  45.0 0.9 %sum.1 = f32[768,128]{1,0:T(8,128)} custom-call(s32[1,128]{1,0:T(1,128)S(1)} %get-tuple-element.17.row_ref, bf16[3,128,128]{2,1,0:T(8,128)(2,1)S(1)} %get-tuple-element.28.rest_0_, bf16[3,128,128]{2,1,0:T(8,128)(2,1)S(1)} %collective-permute-done.10.rest_1_, bf16[3,128,128]{2,1,0:T(8,128)(2,1)S(1)} %collective-permute-done.11.rest_2_, ...), custom_call_target="tpu_custom_call" | custom-call | tf_op jit(solution)/shard_map/sum/pallas_call | solution.py:431
  (19 shorter events, 0.2 us)
Async XLA Ops:
  0.6 14.1 %collective-permute-start = (bf16[4,128,128]{2,1,0:T(8,128)(2,1)}, bf16[4,128,128]{2,1,0:T(8,128)(2,1)S(1)}, u32[]{:S(2)}, u32[]{:S(2)}) collective-permute-start(bf16[4,128,128]{2,1,0:T(8,128)(2,1)} %bitcast.24), channel_id=1, source_target_pairs={{0,4},{4,0},{8,12},{12,8},{16,20},{20,16},{24,28},{28,24},{1,5},{5... | collective-permute-start | bytes 393224 | tf_op jit(solution)/shard_map/ppermute | solution.py:60
  3.7 12.8 %collective-permute-start.1 = (bf16[4,128,128]{2,1,0:T(8,128)(2,1)}, bf16[4,128,128]{2,1,0:T(8,128)(2,1)S(1)}, u32[]{:S(2)}, u32[]{:S(2)}) collective-permute-start(bf16[4,128,128]{2,1,0:T(8,128)(2,1)} %bitcast.25), channel_id=1, source_target_pairs={{0,8},{4,12},{8,0},{12,4},{16,24},{20,28},{24,16},{28,20},{1,9},{5... | collective-permute-start | bytes 393224 | tf_op jit(solution)/shard_map/ppermute | solution.py:60
  5.3 8.7 %collective-permute-start.3 = (bf16[4,128,128]{2,1,0:T(8,128)(2,1)}, bf16[4,128,128]{2,1,0:T(8,128)(2,1)S(1)}, u32[]{:S(2)}, u32[]{:S(2)}) collective-permute-start(bf16[4,128,128]{2,1,0:T(8,128)(2,1)} %bitcast.26), channel_id=1, source_target_pairs={{0,16},{4,20},{8,24},{12,28},{16,0},{20,4},{24,8},{28,12},{1,17},{... | collective-permute-start | bytes 393224 | tf_op jit(solution)/shard_map/ppermute | solution.py:60
  13.9 7.1 %collective-permute-start.4 = (bf16[4,128,128]{2,1,0:T(8,128)(2,1)S(1)}, bf16[4,128,128]{2,1,0:T(8,128)(2,1)S(1)}, u32[]{:S(2)}, u32[]{:S(2)}) collective-permute-start(bf16[4,128,128]{2,1,0:T(8,128)(2,1)S(1)} %collective-permute-done.3), channel_id=1, source_target_pairs={{0,4},{4,0},{8,12},{12,8},{16,20},{20,16},{24,28},{28,24},{1,5},{5... | collective-permute-start | bytes 393224 | tf_op jit(solution)/shard_map/ppermute | solution.py:60
  14.4 5.0 %collective-permute-start.5 = (bf16[4,128,128]{2,1,0:T(8,128)(2,1)S(1)}, bf16[4,128,128]{2,1,0:T(8,128)(2,1)S(1)}, u32[]{:S(2)}, u32[]{:S(2)}) collective-permute-start(bf16[4,128,128]{2,1,0:T(8,128)(2,1)S(1)} %collective-permute-done.3), channel_id=1, source_target_pairs={{0,8},{4,12},{8,0},{12,4},{16,24},{20,28},{24,16},{28,20},{1,9},{5... | collective-permute-start | bytes 393224 | tf_op jit(solution)/shard_map/ppermute | solution.py:60
  14.8 6.2 %collective-permute-start.2 = (bf16[4,128,128]{2,1,0:T(8,128)(2,1)S(1)}, bf16[4,128,128]{2,1,0:T(8,128)(2,1)S(1)}, u32[]{:S(2)}, u32[]{:S(2)}) collective-permute-start(bf16[4,128,128]{2,1,0:T(8,128)(2,1)S(1)} %collective-permute-done), channel_id=1, source_target_pairs={{0,8},{4,12},{8,0},{12,4},{16,24},{20,28},{24,16},{28,20},{1,9},{5... | collective-permute-start | bytes 393224 | tf_op jit(solution)/shard_map/ppermute | solution.py:60
  19.4 5.0 %collective-permute-start.6 = (bf16[4,128,128]{2,1,0:T(8,128)(2,1)S(1)}, bf16[4,128,128]{2,1,0:T(8,128)(2,1)S(1)}, u32[]{:S(2)}, u32[]{:S(2)}) collective-permute-start(bf16[4,128,128]{2,1,0:T(8,128)(2,1)S(1)} %collective-permute-done.5), channel_id=1, source_target_pairs={{0,4},{4,0},{8,12},{12,8},{16,20},{20,16},{24,28},{28,24},{1,5},{5... | collective-permute-start | bytes 393224 | tf_op jit(solution)/shard_map/ppermute | solution.py:60
  24.4 5.5 %copy-start = (bf16[1,1,8,128,1024]{4,3,2,1,0:T(8,128)(2,1)S(1)}, bf16[1,1,8,128,1024]{4,3,2,1,0:T(8,128)(2,1)}, u32[]{:S(2)}) copy-start(bf16[1,1,8,128,1024]{4,3,2,1,0:T(8,128)(2,1)} %param.11) | copy-start | bytes 6291460
  27.9 1.9 %collective-permute-start.7 = (bf16[3,128,128]{2,1,0:T(8,128)(2,1)S(1)}, bf16[3,128,128]{2,1,0:T(8,128)(2,1)S(1)}, u32[]{:S(2)}, u32[]{:S(2)}) collective-permute-start(bf16[3,128,128]{2,1,0:T(8,128)(2,1)S(1)} %get-tuple-element.21), channel_id=1, source_target_pairs={{0,1},{1,0},{2,3},{3,2},{4,5},{5,4},{6,7},{7,6},{8,9},{9,8},{10,11... | collective-permute-start | bytes 294920 | tf_op jit(solution)/shard_map/ppermute | solution.py:87
  28.0 5.7 %collective-permute-start.8 = (bf16[3,128,128]{2,1,0:T(8,128)(2,1)S(1)}, bf16[3,128,128]{2,1,0:T(8,128)(2,1)S(1)}, u32[]{:S(2)}, u32[]{:S(2)}) collective-permute-start(bf16[3,128,128]{2,1,0:T(8,128)(2,1)S(1)} %get-tuple-element.24), channel_id=1, source_target_pairs={{0,2},{1,3},{2,0},{3,1},{4,6},{5,7},{6,4},{7,5},{8,10},{9,11},{10,... | collective-permute-start | bytes 294920 | tf_op jit(solution)/shard_map/ppermute | solution.py:87
  29.5 5.2 %collective-permute-start.9 = (bf16[3,128,128]{2,1,0:T(8,128)(2,1)S(1)}, bf16[3,128,128]{2,1,0:T(8,128)(2,1)S(1)}, u32[]{:S(2)}, u32[]{:S(2)}) collective-permute-start(bf16[3,128,128]{2,1,0:T(8,128)(2,1)S(1)} %get-tuple-element.25), channel_id=1, source_target_pairs={{0,3},{1,2},{2,1},{3,0},{4,7},{5,6},{6,5},{7,4},{8,11},{9,10},{10,... | collective-permute-start | bytes 294920 | tf_op jit(solution)/shard_map/ppermute | solution.py:87
  29.8 4.9 %copy-start.1 = (f32[1,1,1024]{2,1,0:T(1,128)S(1)}, f32[1,1,1024]{2,1,0:T(1,128)}, u32[]{:S(2)}) copy-start(f32[1,1,1024]{2,1,0:T(1,128)} %param.13) | copy-start | bytes 12292
  29.8 4.9 %copy-start.2 = (f32[1,1,1024]{2,1,0:T(1,128)S(1)}, f32[1,1,1024]{2,1,0:T(1,128)}, u32[]{:S(2)}) copy-start(f32[1,1,1024]{2,1,0:T(1,128)} %param.12) | copy-start | bytes 12292
  37.4 2.2 %collective-permute-start.10 = (bf16[3,128,128]{2,1,0:T(8,128)(2,1)S(1)}, bf16[3,128,128]{2,1,0:T(8,128)(2,1)S(1)}, u32[]{:S(2)}, u32[]{:S(2)}) collective-permute-start(bf16[3,128,128]{2,1,0:T(8,128)(2,1)S(1)} %get-tuple-element.29), channel_id=1, source_target_pairs={{0,1},{1,0},{2,3},{3,2},{4,5},{5,4},{6,7},{7,6},{8,9},{9,8},{10,11... | collective-permute-start | bytes 294920 | tf_op jit(solution)/shard_map/ppermute | solution.py:87
  37.8 4.8 %collective-permute-start.12 = (bf16[3,128,128]{2,1,0:T(8,128)(2,1)S(1)}, bf16[3,128,128]{2,1,0:T(8,128)(2,1)S(1)}, u32[]{:S(2)}, u32[]{:S(2)}) collective-permute-start(bf16[3,128,128]{2,1,0:T(8,128)(2,1)S(1)} %shard_map.107), channel_id=1, source_target_pairs={{0,3},{1,2},{2,1},{3,0},{4,7},{5,6},{6,5},{7,4},{8,11},{9,10},{10,... | collective-permute-start | bytes 294920 | tf_op jit(solution)/shard_map/ppermute | solution.py:87
  39.1 6.0 %collective-permute-start.11 = (bf16[3,128,128]{2,1,0:T(8,128)(2,1)S(1)}, bf16[3,128,128]{2,1,0:T(8,128)(2,1)S(1)}, u32[]{:S(2)}, u32[]{:S(2)}) collective-permute-start(bf16[3,128,128]{2,1,0:T(8,128)(2,1)S(1)} %get-tuple-element.30), channel_id=1, source_target_pairs={{0,2},{1,3},{2,0},{3,1},{4,6},{5,7},{6,4},{7,5},{8,10},{9,11},{10,... | collective-permute-start | bytes 294920 | tf_op jit(solution)/shard_map/ppermute | solution.py:87

commit v6 on v5

--- a/solution.py
+++ b/solution.py
@@ -45,6 +45,9 @@
         tiled=True,
     )
     return arrived.reshape(atom_devices * capacity, block_width, block_width), slot_index
+
+
+upper_tiles = [(i, j) for i in range(KB) for j in range(i, KB)]
 
 
 def gather_order(devices):
@@ -126,17 +129,14 @@
     return [row[0, KB * KB + j] for j in range(sends)]
 
 
-def sign_kernel(
-    devices, capacity, row_ref, level_ref, block_ref, density_ref, *rest
-):
+def sign_kernel(devices, capacity, row_ref, level_ref, block_ref, density_ref, *rest):
     out_refs = rest[:devices]
-    shifted, x_zero, t_one, x_one, pairs = rest[devices:]
+    x_zero, t_one, x_one, pairs = rest[devices:]
     width = block_ref.shape[-1]
     order = KB * width
     rows = lax.broadcasted_iota(jnp.int32, (width, width), 0)
     cols = lax.broadcasted_iota(jnp.int32, (width, width), 1)
-    diagonal = rows == cols
-    unit = jnp.where(diagonal, 1.0, 0.0)
+    unit = jnp.where(rows == cols, 1.0, 0.0)
     level = level_ref[...] * unit
     row = row_ref[...]
 
@@ -144,23 +144,23 @@
         return pl.ds(i * width, width)
 
     total = jnp.zeros((8, width), jnp.float32)
-    tiles = [(i, j) for i in range(KB) for j in range(i, KB)]
-    for i, j in tiles:
+    shifted = []
+    for i, j in upper_tiles:
         upper = block_ref[row[0, i * KB + j]].astype(jnp.float32)
         lower = block_ref[row[0, j * KB + i]].astype(jnp.float32)
         value = 0.5 * (upper + lower.T)
         if i == j:
             value = value - level
-        shifted[at(i), at(j)] = value
         squares = (value * value).reshape(width // 8, 8, width).sum(axis=0)
         total = total + (squares if i == j else 2.0 * squares)
-    mean = jnp.sum(total, keepdims=True) / order
-    inverse = 1.0 / (2.0 * jnp.sqrt(mean + 1e-06))
-    for i, j in tiles:
-        value = (shifted[at(i), at(j)] * inverse).astype(jnp.bfloat16)
+        shifted.append((i, j, value.astype(jnp.bfloat16)))
+    for i, j, value in shifted:
         x_zero[at(i), at(j)] = value
         if i != j:
             x_zero[at(j), at(i)] = value.T
+    mean = jnp.sum(total, keepdims=True) / order + 1e-06
+    inverse = 1.0 / (2.0 * jnp.sqrt(mean))
+    weight = -0.5 / (4.0 * mean)
     for i in range(0, KB, 2):
         pair = pl.ds(i * width, 2 * width)
         right = pl.ds(i * width, order - i * width)
@@ -168,7 +168,7 @@
         for k in (i, i + 1):
             for j in range(i, KB):
                 rows, cols = (k - i) * width, (j - i) * width
-                part = -0.5 * square[rows : rows + width, cols : cols + width]
+                part = weight * square[rows : rows + width, cols : cols + width]
                 value = (1.5 * unit + part if k == j else part).astype(jnp.bfloat16)
                 t_one[at(k), at(j)] = value
                 if j > i + 1:
@@ -176,9 +176,8 @@
     for i in range(0, KB, 2):
         pair = pl.ds(i * width, 2 * width)
         right = pl.ds(i * width, order - i * width)
-        value = jnp.dot(
-            x_zero[pair, :], t_one[:, right], preferred_element_type=jnp.float32
-        ).astype(jnp.bfloat16)
+        value = jnp.dot(x_zero[pair, :], t_one[:, right], preferred_element_type=jnp.float32)
+        value = (inverse * value).astype(jnp.bfloat16)
         x_one[pair, right] = value
         if i + 2 < KB:
             below = pl.ds((i + 2) * width, order - (i + 2) * width)
@@ -190,12 +189,13 @@
         parts.append((1.5 * unit + part if i == 0 else part).astype(jnp.bfloat16))
     t_two = jnp.concatenate(parts, axis=0)
     final = jnp.dot(x_one[...], t_two, preferred_element_type=jnp.float32)
+    column = []
     for i in range(KB):
         part = final[i * width : (i + 1) * width]
-        density_ref[at(i), :] = (0.5 * (unit - part if i == 0 else -part)).astype(jnp.bfloat16)
-    places = pair_places(row, 2 * KB)
-    for j, place in enumerate(places):
-        pairs[place] = density_ref[at(j // 2), :]
+        column.append((0.5 * (unit - part if i == 0 else -part)).astype(jnp.bfloat16))
+    for j, place in enumerate(pair_places(row, 2 * KB)):
+        pairs[place] = column[j // 2]
+    density_ref[...] = jnp.concatenate(column, axis=0)
     for k in range(devices):
         out_refs[k][...] = pairs[k * capacity : (k + 1) * capacity]
 
@@ -357,7 +357,6 @@
         out_shape=[jax.ShapeDtypeStruct((order, block_width), jnp.bfloat16)] + [group] * devices,
         out_specs=[VMEM] * (1 + devices),
         scratch_shapes=[
-            pltpu.VMEM((order, order), jnp.float32),
             pltpu.VMEM((order, order), jnp.bfloat16),
             pltpu.VMEM((order, order), jnp.bfloat16),
             pltpu.VMEM((order, order), jnp.bfloat16),

time: 46.1 us -> 45.9 us (level)
  no operation moved by 1% of the time
where the time goes in v6:
time: 45.9 us; the launch traced here: 45.7 us
  waiting for transfers between devices  17.1 us (37%)
  starting transfers between devices  15.4 us (34%)
  Pallas kernels  9.21 us (20%)
  local copies, waits for them, and re-layouts  1.86 us (4%)
  between operations  1.41 us (3%)
  other arithmetic  0.75 us (2%)
    ppermute x7, starting transfers between devices, gathered_blocks(): parts[offset] = lax.ppermute(parts[offset ^ step], 'atoms', pairs)  11.3 us
    ppermute x6, waiting for transfers between devices, exchange(): lax.ppermute(groups[step], 'space', pairs)  8.54 us
    ppermute x7, waiting for transfers between devices, gathered_blocks(): parts[offset] = lax.ppermute(parts[offset ^ step], 'atoms', pairs)  8.54 us
    pallas_call x5, Pallas kernels, step_call(): pl.pallas_call(kernel, in_specs=[VMEM] * len(operands), out_shape=out_sha...  4.42 us
    ppermute x6, starting transfers between devices, exchange(): lax.ppermute(groups[step], 'space', pairs)  4.12 us
    pallas_call x1, Pallas kernels, per_device(): pl.pallas_call(functools.partial(sign_kernel, devices, capacity), name='s...  3.28 us
    unnamed x13, local copies, waits for them, and re-layouts  1.08 us
  transfers between devices with their start and end apart: 13, of which 7 were waited for; matrix products, arithmetic and copies ran while one was open for 6% of the time, Pallas kernels for 5%

profile of v6, /device:TPU:0, one launch (start us, length us, event | category | flops | bytes accessed | tf_op | source)
XLA Modules:
  0.0 45.7 jit_solution(13753763613784006980)
XLA Ops:
  0.6 3.1 %collective-permute-start = (bf16[4,128,128]{2,1,0:T(8,128)(2,1)}, bf16[4,128,128]{2,1,0:T(8,128)(2,1)S(1)}, u32[]{:S(2)}, u32[]{:S(2)}) collective-permute-start(bf16[4,128,128]{2,1,0:T(8,128)(2,1)} %bitcast.24), channel_id=1, source_target_pairs={{0,4},{4,0},{8,12},{12,8},{16,20},{20,16},{24,28},{28,24},{1,5},{5... | collective-permute-start | bytes 393224 | tf_op jit(solution)/shard_map/ppermute | solution.py:63
  3.7 1.6 %collective-permute-start.1 = (bf16[4,128,128]{2,1,0:T(8,128)(2,1)}, bf16[4,128,128]{2,1,0:T(8,128)(2,1)S(1)}, u32[]{:S(2)}, u32[]{:S(2)}) collective-permute-start(bf16[4,128,128]{2,1,0:T(8,128)(2,1)} %bitcast.25), channel_id=1, source_target_pairs={{0,8},{4,12},{8,0},{12,4},{16,24},{20,28},{24,16},{28,20},{1,9},{5... | collective-permute-start | bytes 393224 | tf_op jit(solution)/shard_map/ppermute | solution.py:63
  5.3 2.6 %collective-permute-start.3 = (bf16[4,128,128]{2,1,0:T(8,128)(2,1)}, bf16[4,128,128]{2,1,0:T(8,128)(2,1)S(1)}, u32[]{:S(2)}, u32[]{:S(2)}) collective-permute-start(bf16[4,128,128]{2,1,0:T(8,128)(2,1)} %bitcast.26), channel_id=1, source_target_pairs={{0,16},{4,20},{8,24},{12,28},{16,0},{20,4},{24,8},{28,12},{1,17},{... | collective-permute-start | bytes 393224 | tf_op jit(solution)/shard_map/ppermute | solution.py:63
  7.9 0.9 %constant_dynamic-update-slice_fusion.7 = bf16[32,128,128]{2,1,0:T(8,128)(2,1)S(1)} fusion(bf16[1,4,128,128]{3,2,1,0:T(8,128)(2,1)} %param.8), kind=kLoop, calls=%fused_computation.7 | loop fusion | bytes 262144
  8.8 0.8 %reshape_squeeze.3 = s32[24]{0:T(128)S(1)} reshape(s32[1,1,2,12]{3,2,1,0:T(2,128)} %param.15) | data formatting | bytes 192 | tf_op jit(solution)/shard_map/reshape;squeeze | solution.py:326
  9.6 0.7 %pad_add_fusion = s32[72]{0:T(128)S(1)} fusion(s32[24]{0:T(128)S(1)} %reshape_squeeze.3, s32[12]{0:T(128)} %bitcast.27, s32[36]{0:T(128)} %bitcast.28), kind=kLoop, calls=%fused_computation.8 | loop fusion | flops 144 | bytes 576 | tf_op jit(solution)/shard_map/concatenate | solution.py:326
  11.0 0.6 %index.1 = (s32[1,128]{1,0:T(1,128)S(1)}, f32[1,128]{1,0:T(1,128)S(1)}) custom-call(s32[1,128]{1,0:T(1,128)S(1)} %pad_bitcast_fusion.table_ref, s32[1]{0:T(128)} %bitcast.3.atom_ref, s32[1]{0:T(128)} %bitcast.4.me_ref, f32[1]{0:T(128)S(6)} %copy.18.chem_ref), custom_call_target="tpu_custom_call" | custom-call | flops 2000 | bytes 2000 | tf_op jit(solution)/shard_map/index/pallas_call | solution.py:328
  11.6 2.3 %collective-permute-done.3 = bf16[4,128,128]{2,1,0:T(8,128)(2,1)S(1)} collective-permute-done((bf16[4,128,128]{2,1,0:T(8,128)(2,1)}, bf16[4,128,128]{2,1,0:T(8,128)(2,1)S(1)}, u32[]{:S(2)}, u32[]{:S(2)}) %collective-permute-start.3) | collective-permute-done | bytes 131104 | tf_op jit(solution)/shard_map/ppermute | solution.py:63
  13.9 0.5 %collective-permute-start.4 = (bf16[4,128,128]{2,1,0:T(8,128)(2,1)S(1)}, bf16[4,128,128]{2,1,0:T(8,128)(2,1)S(1)}, u32[]{:S(2)}, u32[]{:S(2)}) collective-permute-start(bf16[4,128,128]{2,1,0:T(8,128)(2,1)S(1)} %collective-permute-done.3), channel_id=1, source_target_pairs={{0,4},{4,0},{8,12},{12,8},{16,20},{20,16},{24,28},{28,24},{1,5},{5... | collective-permute-start | bytes 393224 | tf_op jit(solution)/shard_map/ppermute | solution.py:63
  14.4 0.3 collective-permute-start.5
  14.8 1.7 %collective-permute-start.2 = (bf16[4,128,128]{2,1,0:T(8,128)(2,1)S(1)}, bf16[4,128,128]{2,1,0:T(8,128)(2,1)S(1)}, u32[]{:S(2)}, u32[]{:S(2)}) collective-permute-start(bf16[4,128,128]{2,1,0:T(8,128)(2,1)S(1)} %collective-permute-done), channel_id=1, source_target_pairs={{0,8},{4,12},{8,0},{12,4},{16,24},{20,28},{24,16},{28,20},{1,9},{5... | collective-permute-start | bytes 393224 | tf_op jit(solution)/shard_map/ppermute | solution.py:63
  16.5 2.9 %collective-permute-done.5 = bf16[4,128,128]{2,1,0:T(8,128)(2,1)S(1)} collective-permute-done((bf16[4,128,128]{2,1,0:T(8,128)(2,1)S(1)}, bf16[4,128,128]{2,1,0:T(8,128)(2,1)S(1)}, u32[]{:S(2)}, u32[]{:S(2)}) %collective-permute-start.5) | collective-permute-done | bytes 131104 | tf_op jit(solution)/shard_map/ppermute | solution.py:63
  19.4 1.5 %collective-permute-start.6 = (bf16[4,128,128]{2,1,0:T(8,128)(2,1)S(1)}, bf16[4,128,128]{2,1,0:T(8,128)(2,1)S(1)}, u32[]{:S(2)}, u32[]{:S(2)}) collective-permute-start(bf16[4,128,128]{2,1,0:T(8,128)(2,1)S(1)} %collective-permute-done.5), channel_id=1, source_target_pairs={{0,4},{4,0},{8,12},{12,8},{16,20},{20,16},{24,28},{28,24},{1,5},{5... | collective-permute-start | bytes 393224 | tf_op jit(solution)/shard_map/ppermute | solution.py:63
  21.1 3.3 %collective-permute-done.6 = bf16[4,128,128]{2,1,0:T(8,128)(2,1)S(1)} collective-permute-done((bf16[4,128,128]{2,1,0:T(8,128)(2,1)S(1)}, bf16[4,128,128]{2,1,0:T(8,128)(2,1)S(1)}, u32[]{:S(2)}, u32[]{:S(2)}) %collective-permute-start.6) | collective-permute-done | bytes 131104 | tf_op jit(solution)/shard_map/ppermute | solution.py:63
  24.4 0.0 copy-start
  24.4 3.3 %sign.1 = (bf16[768,128]{1,0:T(8,128)(2,1)S(1)}, bf16[3,128,128]{2,1,0:T(8,128)(2,1)S(1)}, bf16[3,128,128]{2,1,0:T(8,128)(2,1)S(1)}, bf16[3,128,128]{2,1,0:T(8,128)(2,1)S(1)}, bf16[3,128,128]{2,1,0:T(8,128)(2,1)S(1)}) custom-call(s32[1,128]{1,0:T(1,128)S(1)} %get-tuple-element.17.row_ref, f32[1,128]{1,0:T(1,128)S(1)} %get-tuple-element.18.level_ref, ...), custom_call_target="tpu_custom_call" | custom-call | flops 1811939328 | bytes 2359296 | tf_op jit(solution)/shard_map/sign/pallas_call | solution.py:353
  27.7 0.1 collective-permute-start.7
  27.8 1.6 %collective-permute-start.8 = (bf16[3,128,128]{2,1,0:T(8,128)(2,1)S(1)}, bf16[3,128,128]{2,1,0:T(8,128)(2,1)S(1)}, u32[]{:S(2)}, u32[]{:S(2)}) collective-permute-start(bf16[3,128,128]{2,1,0:T(8,128)(2,1)S(1)} %get-tuple-element.24), channel_id=1, source_target_pairs={{0,2},{1,3},{2,0},{3,1},{4,6},{5,7},{6,4},{7,5},{8,10},{9,11},{10,... | collective-permute-start | bytes 294920 | tf_op jit(solution)/shard_map/ppermute | solution.py:90
  29.3 0.3 collective-permute-start.9
  29.6 1.3 %shard_map.103 = (f32[8,1024]{1,0:T(8,128)S(1)}, bf16[768,128]{1,0:T(8,128)(2,1)}) custom-call(s32[1,128]{1,0:T(1,128)S(1)} %get-tuple-element.17.row_ref, bf16[8,128,1024]{2,1,0:T(8,128)(2,1)S(1)} %bitcast.14, bf16[768,128]{1,0:T(8,128)(2,1)S(1)} %get-tuple-element.19.column_ref, bf16[3,128,128]{2,1,0:T(8,128)(2,1)S(1)} %get-tuple-element.20.rest_0_, ...), custom_call_target="tpu_custom_call" | custom-call | flops 201326592 | bytes 3145728 | tf_op jit(solution)/shard_map/pallas_call | solution.py:382
  30.9 2.6 %collective-permute-done.8.rest_0_ = bf16[3,128,128]{2,1,0:T(8,128)(2,1)S(1)} collective-permute-done((bf16[3,128,128]{2,1,0:T(8,128)(2,1)S(1)}, bf16[3,128,128]{2,1,0:T(8,128)(2,1)S(1)}, u32[]{:S(2)}, u32[]{:S(2)}) %collective-permute-start.8) | collective-permute-done | bytes 98336 | tf_op jit(solution)/shard_map/ppermute | solution.py:90
  33.5 0.5 %shard_map.104.near_ref = f32[8,1024]{1,0:T(8,128)S(1)} custom-call(s32[1,128]{1,0:T(1,128)S(1)} %get-tuple-element.17.row_ref, bf16[8,128,1024]{2,1,0:T(8,128)(2,1)S(1)} %bitcast.15, f32[8,1024]{1,0:T(8,128)S(1)} %get-tuple-element.23.near_ref, bf16[3,128,128]{2,1,0:T(8,128)(2,1)S(1)} %collective-permute-done.8.rest_0_), custom_call_target="tpu_custom_call" | custom-call | flops 100663296 | bytes 1572864 | tf_op jit(solution)/shard_map/pallas_call | solution.py:382
  34.0 0.6 %collective-permute-done.9.rest_0_ = bf16[3,128,128]{2,1,0:T(8,128)(2,1)S(1)} collective-permute-done((bf16[3,128,128]{2,1,0:T(8,128)(2,1)S(1)}, bf16[3,128,128]{2,1,0:T(8,128)(2,1)S(1)}, u32[]{:S(2)}, u32[]{:S(2)}) %collective-permute-start.9) | collective-permute-done | bytes 98336 | tf_op jit(solution)/shard_map/ppermute | solution.py:90
  34.5 1.0 %shard_map.105 = (f32[1,1024]{1,0:T(1,128)S(1)}, bf16[3,128,128]{2,1,0:T(8,128)(2,1)S(1)}) custom-call(s32[1,128]{1,0:T(1,128)S(1)} %get-tuple-element.17.row_ref, bf16[8,128,1024]{2,1,0:T(8,128)(2,1)S(1)} %bitcast.16, f32[1,1024]{1,0:T(1,128)S(1)} %bitcast.22, f32[1,1024]{1,0:T(1,128)S(1)} %bitcast.19, f32[8,1024]{1,0:T(8,128)S(1)} %shard_map.104.near_ref, ...), custom_call_target="tpu_custom_call" | custom-call | flops 100663296 | bytes 1572864 | tf_op jit(solution)/shard_map/pallas_call | solution.py:382
  35.5 1.2 %shard_map.106 = (bf16[3,128,128]{2,1,0:T(8,128)(2,1)S(1)}, bf16[3,128,128]{2,1,0:T(8,128)(2,1)S(1)}, f32[1,1024]{1,0:T(1,128)}) custom-call(s32[1,128]{1,0:T(1,128)S(1)} %get-tuple-element.17.row_ref, bf16[8,128,1024]{2,1,0:T(8,128)(2,1)S(1)} %bitcast.17, f32[1,1024]{1,0:T(1,128)S(1)} %bitcast.20, f32[1,1024]{1,0:T(1,128)S(1)} %get-tuple-element.26.found_ref), custom_call_target="tpu_custom_call" | custom-call | flops 201326592 | bytes 3145728 | tf_op jit(solution)/shard_map/pallas_call | solution.py:382
  36.7 0.5 %shard_map.107 = bf16[3,128,128]{2,1,0:T(8,128)(2,1)S(1)} custom-call(s32[1,128]{1,0:T(1,128)S(1)} %get-tuple-element.17.row_ref, bf16[8,128,1024]{2,1,0:T(8,128)(2,1)S(1)} %bitcast.18, f32[1,1024]{1,0:T(1,128)S(1)} %bitcast.21, f32[1,1024]{1,0:T(1,128)S(1)} %get-tuple-element.26.found_ref), custom_call_target="tpu_custom_call" | custom-call | flops 100663296 | bytes 1572864 | tf_op jit(solution)/shard_map/pallas_call | solution.py:382
  37.2 0.4 collective-permute-start.10
  37.6 1.2 %collective-permute-start.12 = (bf16[3,128,128]{2,1,0:T(8,128)(2,1)S(1)}, bf16[3,128,128]{2,1,0:T(8,128)(2,1)S(1)}, u32[]{:S(2)}, u32[]{:S(2)}) collective-permute-start(bf16[3,128,128]{2,1,0:T(8,128)(2,1)S(1)} %shard_map.107), channel_id=1, source_target_pairs={{0,3},{1,2},{2,1},{3,0},{4,7},{5,6},{6,5},{7,4},{8,11},{9,10},{10,... | collective-permute-start | bytes 294920 | tf_op jit(solution)/shard_map/ppermute | solution.py:90
  38.9 0.5 %collective-permute-start.11 = (bf16[3,128,128]{2,1,0:T(8,128)(2,1)S(1)}, bf16[3,128,128]{2,1,0:T(8,128)(2,1)S(1)}, u32[]{:S(2)}, u32[]{:S(2)}) collective-permute-start(bf16[3,128,128]{2,1,0:T(8,128)(2,1)S(1)} %get-tuple-element.30), channel_id=1, source_target_pairs={{0,2},{1,3},{2,0},{3,1},{4,6},{5,7},{6,4},{7,5},{8,10},{9,11},{10,... | collective-permute-start | bytes 294920 | tf_op jit(solution)/shard_map/ppermute | solution.py:90
  39.4 3.0 %collective-permute-done.12.rest_3_ = bf16[3,128,128]{2,1,0:T(8,128)(2,1)S(1)} collective-permute-done((bf16[3,128,128]{2,1,0:T(8,128)(2,1)S(1)}, bf16[3,128,128]{2,1,0:T(8,128)(2,1)S(1)}, u32[]{:S(2)}, u32[]{:S(2)}) %collective-permute-start.12) | collective-permute-done | bytes 98336 | tf_op jit(solution)/shard_map/ppermute | solution.py:90
  42.4 2.4 %collective-permute-done.11.rest_2_ = bf16[3,128,128]{2,1,0:T(8,128)(2,1)S(1)} collective-permute-done((bf16[3,128,128]{2,1,0:T(8,128)(2,1)S(1)}, bf16[3,128,128]{2,1,0:T(8,128)(2,1)S(1)}, u32[]{:S(2)}, u32[]{:S(2)}) %collective-permute-start.11) | collective-permute-done | bytes 98336 | tf_op jit(solution)/shard_map/ppermute | solution.py:90
  44.8 0.9 %sum.1 = f32[768,128]{1,0:T(8,128)} custom-call(s32[1,128]{1,0:T(1,128)S(1)} %get-tuple-element.17.row_ref, bf16[3,128,128]{2,1,0:T(8,128)(2,1)S(1)} %get-tuple-element.28.rest_0_, bf16[3,128,128]{2,1,0:T(8,128)(2,1)S(1)} %collective-permute-done.10.rest_1_, bf16[3,128,128]{2,1,0:T(8,128)(2,1)S(1)} %collective-permute-done.11.rest_2_, ...), custom_call_target="tpu_custom_call" | custom-call | tf_op jit(solution)/shard_map/sum/pallas_call | solution.py:430
  (19 shorter events, 0.2 us)
Async XLA Ops:
  0.6 14.1 %collective-permute-start = (bf16[4,128,128]{2,1,0:T(8,128)(2,1)}, bf16[4,128,128]{2,1,0:T(8,128)(2,1)S(1)}, u32[]{:S(2)}, u32[]{:S(2)}) collective-permute-start(bf16[4,128,128]{2,1,0:T(8,128)(2,1)} %bitcast.24), channel_id=1, source_target_pairs={{0,4},{4,0},{8,12},{12,8},{16,20},{20,16},{24,28},{28,24},{1,5},{5... | collective-permute-start | bytes 393224 | tf_op jit(solution)/shard_map/ppermute | solution.py:63
  3.7 12.8 %collective-permute-start.1 = (bf16[4,128,128]{2,1,0:T(8,128)(2,1)}, bf16[4,128,128]{2,1,0:T(8,128)(2,1)S(1)}, u32[]{:S(2)}, u32[]{:S(2)}) collective-permute-start(bf16[4,128,128]{2,1,0:T(8,128)(2,1)} %bitcast.25), channel_id=1, source_target_pairs={{0,8},{4,12},{8,0},{12,4},{16,24},{20,28},{24,16},{28,20},{1,9},{5... | collective-permute-start | bytes 393224 | tf_op jit(solution)/shard_map/ppermute | solution.py:63
  5.3 8.7 %collective-permute-start.3 = (bf16[4,128,128]{2,1,0:T(8,128)(2,1)}, bf16[4,128,128]{2,1,0:T(8,128)(2,1)S(1)}, u32[]{:S(2)}, u32[]{:S(2)}) collective-permute-start(bf16[4,128,128]{2,1,0:T(8,128)(2,1)} %bitcast.26), channel_id=1, source_target_pairs={{0,16},{4,20},{8,24},{12,28},{16,0},{20,4},{24,8},{28,12},{1,17},{... | collective-permute-start | bytes 393224 | tf_op jit(solution)/shard_map/ppermute | solution.py:63
  13.9 7.1 %collective-permute-start.4 = (bf16[4,128,128]{2,1,0:T(8,128)(2,1)S(1)}, bf16[4,128,128]{2,1,0:T(8,128)(2,1)S(1)}, u32[]{:S(2)}, u32[]{:S(2)}) collective-permute-start(bf16[4,128,128]{2,1,0:T(8,128)(2,1)S(1)} %collective-permute-done.3), channel_id=1, source_target_pairs={{0,4},{4,0},{8,12},{12,8},{16,20},{20,16},{24,28},{28,24},{1,5},{5... | collective-permute-start | bytes 393224 | tf_op jit(solution)/shard_map/ppermute | solution.py:63
  14.4 5.0 %collective-permute-start.5 = (bf16[4,128,128]{2,1,0:T(8,128)(2,1)S(1)}, bf16[4,128,128]{2,1,0:T(8,128)(2,1)S(1)}, u32[]{:S(2)}, u32[]{:S(2)}) collective-permute-start(bf16[4,128,128]{2,1,0:T(8,128)(2,1)S(1)} %collective-permute-done.3), channel_id=1, source_target_pairs={{0,8},{4,12},{8,0},{12,4},{16,24},{20,28},{24,16},{28,20},{1,9},{5... | collective-permute-start | bytes 393224 | tf_op jit(solution)/shard_map/ppermute | solution.py:63
  14.8 6.2 %collective-permute-start.2 = (bf16[4,128,128]{2,1,0:T(8,128)(2,1)S(1)}, bf16[4,128,128]{2,1,0:T(8,128)(2,1)S(1)}, u32[]{:S(2)}, u32[]{:S(2)}) collective-permute-start(bf16[4,128,128]{2,1,0:T(8,128)(2,1)S(1)} %collective-permute-done), channel_id=1, source_target_pairs={{0,8},{4,12},{8,0},{12,4},{16,24},{20,28},{24,16},{28,20},{1,9},{5... | collective-permute-start | bytes 393224 | tf_op jit(solution)/shard_map/ppermute | solution.py:63
  19.4 5.0 %collective-permute-start.6 = (bf16[4,128,128]{2,1,0:T(8,128)(2,1)S(1)}, bf16[4,128,128]{2,1,0:T(8,128)(2,1)S(1)}, u32[]{:S(2)}, u32[]{:S(2)}) collective-permute-start(bf16[4,128,128]{2,1,0:T(8,128)(2,1)S(1)} %collective-permute-done.5), channel_id=1, source_target_pairs={{0,4},{4,0},{8,12},{12,8},{16,20},{20,16},{24,28},{28,24},{1,5},{5... | collective-permute-start | bytes 393224 | tf_op jit(solution)/shard_map/ppermute | solution.py:63
  24.4 5.2 %copy-start = (bf16[1,1,8,128,1024]{4,3,2,1,0:T(8,128)(2,1)S(1)}, bf16[1,1,8,128,1024]{4,3,2,1,0:T(8,128)(2,1)}, u32[]{:S(2)}) copy-start(bf16[1,1,8,128,1024]{4,3,2,1,0:T(8,128)(2,1)} %param.11) | copy-start | bytes 6291460
  27.7 1.9 %collective-permute-start.7 = (bf16[3,128,128]{2,1,0:T(8,128)(2,1)S(1)}, bf16[3,128,128]{2,1,0:T(8,128)(2,1)S(1)}, u32[]{:S(2)}, u32[]{:S(2)}) collective-permute-start(bf16[3,128,128]{2,1,0:T(8,128)(2,1)S(1)} %get-tuple-element.21), channel_id=1, source_target_pairs={{0,1},{1,0},{2,3},{3,2},{4,5},{5,4},{6,7},{7,6},{8,9},{9,8},{10,11... | collective-permute-start | bytes 294920 | tf_op jit(solution)/shard_map/ppermute | solution.py:90
  27.8 5.7 %collective-permute-start.8 = (bf16[3,128,128]{2,1,0:T(8,128)(2,1)S(1)}, bf16[3,128,128]{2,1,0:T(8,128)(2,1)S(1)}, u32[]{:S(2)}, u32[]{:S(2)}) collective-permute-start(bf16[3,128,128]{2,1,0:T(8,128)(2,1)S(1)} %get-tuple-element.24), channel_id=1, source_target_pairs={{0,2},{1,3},{2,0},{3,1},{4,6},{5,7},{6,4},{7,5},{8,10},{9,11},{10,... | collective-permute-start | bytes 294920 | tf_op jit(solution)/shard_map/ppermute | solution.py:90
  29.3 5.2 %collective-permute-start.9 = (bf16[3,128,128]{2,1,0:T(8,128)(2,1)S(1)}, bf16[3,128,128]{2,1,0:T(8,128)(2,1)S(1)}, u32[]{:S(2)}, u32[]{:S(2)}) collective-permute-start(bf16[3,128,128]{2,1,0:T(8,128)(2,1)S(1)} %get-tuple-element.25), channel_id=1, source_target_pairs={{0,3},{1,2},{2,1},{3,0},{4,7},{5,6},{6,5},{7,4},{8,11},{9,10},{10,... | collective-permute-start | bytes 294920 | tf_op jit(solution)/shard_map/ppermute | solution.py:90
  29.6 4.9 %copy-start.1 = (f32[1,1,1024]{2,1,0:T(1,128)S(1)}, f32[1,1,1024]{2,1,0:T(1,128)}, u32[]{:S(2)}) copy-start(f32[1,1,1024]{2,1,0:T(1,128)} %param.13) | copy-start | bytes 12292
  29.6 4.9 %copy-start.2 = (f32[1,1,1024]{2,1,0:T(1,128)S(1)}, f32[1,1,1024]{2,1,0:T(1,128)}, u32[]{:S(2)}) copy-start(f32[1,1,1024]{2,1,0:T(1,128)} %param.12) | copy-start | bytes 12292
  37.2 2.2 %collective-permute-start.10 = (bf16[3,128,128]{2,1,0:T(8,128)(2,1)S(1)}, bf16[3,128,128]{2,1,0:T(8,128)(2,1)S(1)}, u32[]{:S(2)}, u32[]{:S(2)}) collective-permute-start(bf16[3,128,128]{2,1,0:T(8,128)(2,1)S(1)} %get-tuple-element.29), channel_id=1, source_target_pairs={{0,1},{1,0},{2,3},{3,2},{4,5},{5,4},{6,7},{7,6},{8,9},{9,8},{10,11... | collective-permute-start | bytes 294920 | tf_op jit(solution)/shard_map/ppermute | solution.py:90
  37.6 4.8 %collective-permute-start.12 = (bf16[3,128,128]{2,1,0:T(8,128)(2,1)S(1)}, bf16[3,128,128]{2,1,0:T(8,128)(2,1)S(1)}, u32[]{:S(2)}, u32[]{:S(2)}) collective-permute-start(bf16[3,128,128]{2,1,0:T(8,128)(2,1)S(1)} %shard_map.107), channel_id=1, source_target_pairs={{0,3},{1,2},{2,1},{3,0},{4,7},{5,6},{6,5},{7,4},{8,11},{9,10},{10,... | collective-permute-start | bytes 294920 | tf_op jit(solution)/shard_map/ppermute | solution.py:90
  38.9 6.0 %collective-permute-start.11 = (bf16[3,128,128]{2,1,0:T(8,128)(2,1)S(1)}, bf16[3,128,128]{2,1,0:T(8,128)(2,1)S(1)}, u32[]{:S(2)}, u32[]{:S(2)}) collective-permute-start(bf16[3,128,128]{2,1,0:T(8,128)(2,1)S(1)} %get-tuple-element.30), channel_id=1, source_target_pairs={{0,2},{1,3},{2,0},{3,1},{4,6},{5,7},{6,4},{7,5},{8,10},{9,11},{10,... | collective-permute-start | bytes 294920 | tf_op jit(solution)/shard_map/ppermute | solution.py:90

commit v7 on v6

--- a/solution.py
+++ b/solution.py
@@ -153,14 +153,14 @@
             value = value - level
         squares = (value * value).reshape(width // 8, 8, width).sum(axis=0)
         total = total + (squares if i == j else 2.0 * squares)
-        shifted.append((i, j, value.astype(jnp.bfloat16)))
+        shifted.append((i, j, value))
+    mean = jnp.sum(total, keepdims=True) / order + 1e-06
+    inverse = 1.0 / (2.0 * jnp.sqrt(mean))
     for i, j, value in shifted:
+        value = (value * inverse).astype(jnp.bfloat16)
         x_zero[at(i), at(j)] = value
         if i != j:
             x_zero[at(j), at(i)] = value.T
-    mean = jnp.sum(total, keepdims=True) / order + 1e-06
-    inverse = 1.0 / (2.0 * jnp.sqrt(mean))
-    weight = -0.5 / (4.0 * mean)
     for i in range(0, KB, 2):
         pair = pl.ds(i * width, 2 * width)
         right = pl.ds(i * width, order - i * width)
@@ -168,7 +168,7 @@
         for k in (i, i + 1):
             for j in range(i, KB):
                 rows, cols = (k - i) * width, (j - i) * width
-                part = weight * square[rows : rows + width, cols : cols + width]
+                part = -0.5 * square[rows : rows + width, cols : cols + width]
                 value = (1.5 * unit + part if k == j else part).astype(jnp.bfloat16)
                 t_one[at(k), at(j)] = value
                 if j > i + 1:
@@ -177,22 +177,22 @@
         pair = pl.ds(i * width, 2 * width)
         right = pl.ds(i * width, order - i * width)
         value = jnp.dot(x_zero[pair, :], t_one[:, right], preferred_element_type=jnp.float32)
-        value = (inverse * value).astype(jnp.bfloat16)
+        value = value.astype(jnp.bfloat16)
         x_one[pair, right] = value
         if i + 2 < KB:
             below = pl.ds((i + 2) * width, order - (i + 2) * width)
             x_one[below, pair] = value[:, 2 * width :].T
-    square = jnp.dot(x_one[...], x_one[:, at(0)], preferred_element_type=jnp.float32)
+    square = jnp.dot(x_one[at(0), :], x_one[...], preferred_element_type=jnp.float32)
     parts = []
     for i in range(KB):
-        part = -0.5 * square[i * width : (i + 1) * width]
+        part = -0.5 * square[:, i * width : (i + 1) * width]
         parts.append((1.5 * unit + part if i == 0 else part).astype(jnp.bfloat16))
-    t_two = jnp.concatenate(parts, axis=0)
-    final = jnp.dot(x_one[...], t_two, preferred_element_type=jnp.float32)
+    t_two = jnp.concatenate(parts, axis=1)
+    final = jnp.dot(t_two, x_one[...], preferred_element_type=jnp.float32)
     column = []
     for i in range(KB):
-        part = final[i * width : (i + 1) * width]
-        column.append((0.5 * (unit - part if i == 0 else -part)).astype(jnp.bfloat16))
+        part = final[:, i * width : (i + 1) * width]
+        column.append((0.5 * (unit - part if i == 0 else -part)).astype(jnp.bfloat16).T)
     for j, place in enumerate(pair_places(row, 2 * KB)):
         pairs[place] = column[j // 2]
     density_ref[...] = jnp.concatenate(column, axis=0)
@@ -245,11 +245,6 @@
     groups = dict(zip(steps, rest))
     slots = tile_slots(row_ref[...], steps, capacity)
     rest[-1][...] = pair_density(slots, near_ref[...], full, table_ref, groups)
-
-
-def partials_kernel(capacity, steps, row_ref, table_ref, weight_ref, found_ref, *rest):
-    slots = tile_slots(row_ref[...], steps, capacity)
-    pair_partials(slots, weight_ref[...] * found_ref[...], table_ref, dict(zip(steps, rest)))
 
 
 def last_kernel(
@@ -406,19 +401,12 @@
     )
     weight = point_weights[0]
     found, *sent = step_call(
-        functools.partial(last_kernel, capacity, full, last, mid),
+        functools.partial(last_kernel, capacity, full, last, [*mid, *last]),
         last,
-        [line] + [group] * len(mid),
+        [line] + [group] * (devices - 2),
         [row, tables, core_density[0], weight, total, *[incoming[k] for k in last]],
     )
-    partials = dict(zip(mid, sent))
-    sent = step_call(
-        functools.partial(partials_kernel, capacity, last),
-        last,
-        [group] * len(last),
-        [row, tables, weight, found],
-    )
-    partials.update(zip(last, sent))
+    partials = dict(zip([*mid, *last], sent))
     *sent, potential = step_call(
         functools.partial(near_partials_kernel, capacity, near),
         near,

time: 45.9 us -> 44.4 us (0.967)
  Pallas kernels: 9.21 us -> 8.37 us
    pallas_call x5 -> x4, Pallas kernels: 4.42 us -> 4.02 us  [step_call(): pl.pallas_call(kernel, in_specs=[VMEM] * len(operands), out_shape=out_sha...]
where the time goes in v7:
time: 44.4 us; the launch traced here: 44.2 us
  waiting for transfers between devices  16.7 us (38%)
  starting transfers between devices  15.1 us (34%)
  Pallas kernels  8.37 us (19%)
  local copies, waits for them, and re-layouts  1.86 us (4%)
  between operations  1.41 us (3%)
  other arithmetic  0.75 us (2%)
    ppermute x7, starting transfers between devices, gathered_blocks(): parts[offset] = lax.ppermute(parts[offset ^ step], 'atoms', pairs)  11.3 us
    ppermute x7, waiting for transfers between devices, gathered_blocks(): parts[offset] = lax.ppermute(parts[offset ^ step], 'atoms', pairs)  8.54 us
    ppermute x6, waiting for transfers between devices, exchange(): lax.ppermute(groups[step], 'space', pairs)  8.2 us
    pallas_call x4, Pallas kernels, step_call(): pl.pallas_call(kernel, in_specs=[VMEM] * len(operands), out_shape=out_sha...  4.02 us
    ppermute x6, starting transfers between devices, exchange(): lax.ppermute(groups[step], 'space', pairs)  3.78 us
    pallas_call x1, Pallas kernels, per_device(): pl.pallas_call(functools.partial(sign_kernel, devices, capacity), name='s...  2.84 us
    unnamed x13, local copies, waits for them, and re-layouts  1.08 us
    pallas_call x1, Pallas kernels, per_device(): pl.pallas_call(functools.partial(sum_kernel, devices, capacity), name='su...  0.89 us
  transfers between devices with their start and end apart: 13, of which 7 were waited for; matrix products, arithmetic and copies ran while one was open for 6% of the time, Pallas kernels for 5%

profile of v7, /device:TPU:0, one launch (start us, length us, event | category | flops | bytes accessed | tf_op | source)
XLA Modules:
  0.0 44.2 jit_solution(7451724728175924958)
XLA Ops:
  0.6 3.1 %collective-permute-start = (bf16[4,128,128]{2,1,0:T(8,128)(2,1)}, bf16[4,128,128]{2,1,0:T(8,128)(2,1)S(1)}, u32[]{:S(2)}, u32[]{:S(2)}) collective-permute-start(bf16[4,128,128]{2,1,0:T(8,128)(2,1)} %bitcast.22), channel_id=1, source_target_pairs={{0,4},{4,0},{8,12},{12,8},{16,20},{20,16},{24,28},{28,24},{1,5},{5... | collective-permute-start | bytes 393224 | tf_op jit(solution)/shard_map/ppermute | solution.py:63
  3.7 1.6 %collective-permute-start.1 = (bf16[4,128,128]{2,1,0:T(8,128)(2,1)}, bf16[4,128,128]{2,1,0:T(8,128)(2,1)S(1)}, u32[]{:S(2)}, u32[]{:S(2)}) collective-permute-start(bf16[4,128,128]{2,1,0:T(8,128)(2,1)} %bitcast.23), channel_id=1, source_target_pairs={{0,8},{4,12},{8,0},{12,4},{16,24},{20,28},{24,16},{28,20},{1,9},{5... | collective-permute-start | bytes 393224 | tf_op jit(solution)/shard_map/ppermute | solution.py:63
  5.3 2.6 %collective-permute-start.3 = (bf16[4,128,128]{2,1,0:T(8,128)(2,1)}, bf16[4,128,128]{2,1,0:T(8,128)(2,1)S(1)}, u32[]{:S(2)}, u32[]{:S(2)}) collective-permute-start(bf16[4,128,128]{2,1,0:T(8,128)(2,1)} %bitcast.24), channel_id=1, source_target_pairs={{0,16},{4,20},{8,24},{12,28},{16,0},{20,4},{24,8},{28,12},{1,17},{... | collective-permute-start | bytes 393224 | tf_op jit(solution)/shard_map/ppermute | solution.py:63
  7.9 0.9 %constant_dynamic-update-slice_fusion.7 = bf16[32,128,128]{2,1,0:T(8,128)(2,1)S(1)} fusion(bf16[1,4,128,128]{3,2,1,0:T(8,128)(2,1)} %param.8), kind=kLoop, calls=%fused_computation.7 | loop fusion | bytes 262144
  8.8 0.8 %reshape_squeeze.3 = s32[24]{0:T(128)S(1)} reshape(s32[1,1,2,12]{3,2,1,0:T(2,128)} %param.15) | data formatting | bytes 192 | tf_op jit(solution)/shard_map/reshape;squeeze | solution.py:321
  9.6 0.7 %pad_add_fusion = s32[72]{0:T(128)S(1)} fusion(s32[24]{0:T(128)S(1)} %reshape_squeeze.3, s32[12]{0:T(128)} %bitcast.25, s32[36]{0:T(128)} %bitcast.26), kind=kLoop, calls=%fused_computation.8 | loop fusion | flops 144 | bytes 576 | tf_op jit(solution)/shard_map/concatenate | solution.py:321
  11.0 0.6 %index.1 = (s32[1,128]{1,0:T(1,128)S(1)}, f32[1,128]{1,0:T(1,128)S(1)}) custom-call(s32[1,128]{1,0:T(1,128)S(1)} %pad_bitcast_fusion.table_ref, s32[1]{0:T(128)} %bitcast.3.atom_ref, s32[1]{0:T(128)} %bitcast.4.me_ref, f32[1]{0:T(128)S(6)} %copy.18.chem_ref), custom_call_target="tpu_custom_call" | custom-call | flops 2000 | bytes 2000 | tf_op jit(solution)/shard_map/index/pallas_call | solution.py:323
  11.6 2.3 %collective-permute-done.3 = bf16[4,128,128]{2,1,0:T(8,128)(2,1)S(1)} collective-permute-done((bf16[4,128,128]{2,1,0:T(8,128)(2,1)}, bf16[4,128,128]{2,1,0:T(8,128)(2,1)S(1)}, u32[]{:S(2)}, u32[]{:S(2)}) %collective-permute-start.3) | collective-permute-done | bytes 131104 | tf_op jit(solution)/shard_map/ppermute | solution.py:63
  13.9 0.5 %collective-permute-start.4 = (bf16[4,128,128]{2,1,0:T(8,128)(2,1)S(1)}, bf16[4,128,128]{2,1,0:T(8,128)(2,1)S(1)}, u32[]{:S(2)}, u32[]{:S(2)}) collective-permute-start(bf16[4,128,128]{2,1,0:T(8,128)(2,1)S(1)} %collective-permute-done.3), channel_id=1, source_target_pairs={{0,4},{4,0},{8,12},{12,8},{16,20},{20,16},{24,28},{28,24},{1,5},{5... | collective-permute-start | bytes 393224 | tf_op jit(solution)/shard_map/ppermute | solution.py:63
  14.4 0.3 collective-permute-start.5
  14.8 0.0 collective-permute-done
  14.8 1.7 %collective-permute-start.2 = (bf16[4,128,128]{2,1,0:T(8,128)(2,1)S(1)}, bf16[4,128,128]{2,1,0:T(8,128)(2,1)S(1)}, u32[]{:S(2)}, u32[]{:S(2)}) collective-permute-start(bf16[4,128,128]{2,1,0:T(8,128)(2,1)S(1)} %collective-permute-done), channel_id=1, source_target_pairs={{0,8},{4,12},{8,0},{12,4},{16,24},{20,28},{24,16},{28,20},{1,9},{5... | collective-permute-start | bytes 393224 | tf_op jit(solution)/shard_map/ppermute | solution.py:63
  16.5 0.0 collective-permute-done.1
  16.5 2.9 %collective-permute-done.5 = bf16[4,128,128]{2,1,0:T(8,128)(2,1)S(1)} collective-permute-done((bf16[4,128,128]{2,1,0:T(8,128)(2,1)S(1)}, bf16[4,128,128]{2,1,0:T(8,128)(2,1)S(1)}, u32[]{:S(2)}, u32[]{:S(2)}) %collective-permute-start.5) | collective-permute-done | bytes 131104 | tf_op jit(solution)/shard_map/ppermute | solution.py:63
  19.4 1.5 %collective-permute-start.6 = (bf16[4,128,128]{2,1,0:T(8,128)(2,1)S(1)}, bf16[4,128,128]{2,1,0:T(8,128)(2,1)S(1)}, u32[]{:S(2)}, u32[]{:S(2)}) collective-permute-start(bf16[4,128,128]{2,1,0:T(8,128)(2,1)S(1)} %collective-permute-done.5), channel_id=1, source_target_pairs={{0,4},{4,0},{8,12},{12,8},{16,20},{20,16},{24,28},{28,24},{1,5},{5... | collective-permute-start | bytes 393224 | tf_op jit(solution)/shard_map/ppermute | solution.py:63
  21.1 3.3 %collective-permute-done.6 = bf16[4,128,128]{2,1,0:T(8,128)(2,1)S(1)} collective-permute-done((bf16[4,128,128]{2,1,0:T(8,128)(2,1)S(1)}, bf16[4,128,128]{2,1,0:T(8,128)(2,1)S(1)}, u32[]{:S(2)}, u32[]{:S(2)}) %collective-permute-start.6) | collective-permute-done | bytes 131104 | tf_op jit(solution)/shard_map/ppermute | solution.py:63
  24.4 0.0 copy-start
  24.4 2.8 %sign.1 = (bf16[768,128]{1,0:T(8,128)(2,1)S(1)}, bf16[3,128,128]{2,1,0:T(8,128)(2,1)S(1)}, bf16[3,128,128]{2,1,0:T(8,128)(2,1)S(1)}, bf16[3,128,128]{2,1,0:T(8,128)(2,1)S(1)}, bf16[3,128,128]{2,1,0:T(8,128)(2,1)S(1)}) custom-call(s32[1,128]{1,0:T(1,128)S(1)} %get-tuple-element.18.row_ref, f32[1,128]{1,0:T(1,128)S(1)} %get-tuple-element.19.level_ref, ...), custom_call_target="tpu_custom_call" | custom-call | flops 1811939328 | bytes 2359296 | tf_op jit(solution)/shard_map/sign/pallas_call | solution.py:348
  27.2 0.1 collective-permute-start.7
  27.3 1.6 %collective-permute-start.8 = (bf16[3,128,128]{2,1,0:T(8,128)(2,1)S(1)}, bf16[3,128,128]{2,1,0:T(8,128)(2,1)S(1)}, u32[]{:S(2)}, u32[]{:S(2)}) collective-permute-start(bf16[3,128,128]{2,1,0:T(8,128)(2,1)S(1)} %get-tuple-element.25), channel_id=1, source_target_pairs={{0,2},{1,3},{2,0},{3,1},{4,6},{5,7},{6,4},{7,5},{8,10},{9,11},{10,... | collective-permute-start | bytes 294920 | tf_op jit(solution)/shard_map/ppermute | solution.py:90
  28.9 0.3 collective-permute-start.9
  29.2 1.3 %shard_map.103 = (f32[8,1024]{1,0:T(8,128)S(1)}, bf16[768,128]{1,0:T(8,128)(2,1)}) custom-call(s32[1,128]{1,0:T(1,128)S(1)} %get-tuple-element.18.row_ref, bf16[8,128,1024]{2,1,0:T(8,128)(2,1)S(1)} %bitcast.14, bf16[768,128]{1,0:T(8,128)(2,1)S(1)} %get-tuple-element.20.column_ref, bf16[3,128,128]{2,1,0:T(8,128)(2,1)S(1)} %get-tuple-element.21.rest_0_, ...), custom_call_target="tpu_custom_call" | custom-call | flops 201326592 | bytes 3145728 | tf_op jit(solution)/shard_map/pallas_call | solution.py:377
  30.5 2.6 %collective-permute-done.8.rest_0_ = bf16[3,128,128]{2,1,0:T(8,128)(2,1)S(1)} collective-permute-done((bf16[3,128,128]{2,1,0:T(8,128)(2,1)S(1)}, bf16[3,128,128]{2,1,0:T(8,128)(2,1)S(1)}, u32[]{:S(2)}, u32[]{:S(2)}) %collective-permute-start.8) | collective-permute-done | bytes 98336 | tf_op jit(solution)/shard_map/ppermute | solution.py:90
  33.1 0.5 %shard_map.104.near_ref = f32[8,1024]{1,0:T(8,128)S(1)} custom-call(s32[1,128]{1,0:T(1,128)S(1)} %get-tuple-element.18.row_ref, bf16[8,128,1024]{2,1,0:T(8,128)(2,1)S(1)} %bitcast.15, f32[8,1024]{1,0:T(8,128)S(1)} %get-tuple-element.24.near_ref, bf16[3,128,128]{2,1,0:T(8,128)(2,1)S(1)} %collective-permute-done.8.rest_0_), custom_call_target="tpu_custom_call" | custom-call | flops 100663296 | bytes 1572864 | tf_op jit(solution)/shard_map/pallas_call | solution.py:377
  33.5 0.6 %collective-permute-done.9.rest_0_ = bf16[3,128,128]{2,1,0:T(8,128)(2,1)S(1)} collective-permute-done((bf16[3,128,128]{2,1,0:T(8,128)(2,1)S(1)}, bf16[3,128,128]{2,1,0:T(8,128)(2,1)S(1)}, u32[]{:S(2)}, u32[]{:S(2)}) %collective-permute-start.9) | collective-permute-done | bytes 98336 | tf_op jit(solution)/shard_map/ppermute | solution.py:90
  34.1 1.1 %shard_map.105 = (f32[1,1024]{1,0:T(1,128)S(1)}, bf16[3,128,128]{2,1,0:T(8,128)(2,1)S(1)}, bf16[3,128,128]{2,1,0:T(8,128)(2,1)S(1)}) custom-call(s32[1,128]{1,0:T(1,128)S(1)} %get-tuple-element.18.row_ref, bf16[8,128,1024]{2,1,0:T(8,128)(2,1)S(1)} %bitcast.16, f32[1,1024]{1,0:T(1,128)S(1)} %bitcast.20, f32[1,1024]{1,0:T(1,128)S(1)} %bitcast.18, ...), custom_call_target="tpu_custom_call" | custom-call | flops 100663296 | bytes 1572864 | tf_op jit(solution)/shard_map/pallas_call | solution.py:377
  35.2 1.2 %shard_map.106 = (bf16[3,128,128]{2,1,0:T(8,128)(2,1)S(1)}, bf16[3,128,128]{2,1,0:T(8,128)(2,1)S(1)}, f32[1,1024]{1,0:T(1,128)}) custom-call(s32[1,128]{1,0:T(1,128)S(1)} %get-tuple-element.18.row_ref, bf16[8,128,1024]{2,1,0:T(8,128)(2,1)S(1)} %bitcast.17, f32[1,1024]{1,0:T(1,128)S(1)} %bitcast.19, f32[1,1024]{1,0:T(1,128)S(1)} %get-tuple-element.27.found_ref), custom_call_target="tpu_custom_call" | custom-call | flops 201326592 | bytes 3145728 | tf_op jit(solution)/shard_map/pallas_call | solution.py:377
  36.3 0.4 collective-permute-start.10
  36.7 1.5 %collective-permute-start.11 = (bf16[3,128,128]{2,1,0:T(8,128)(2,1)S(1)}, bf16[3,128,128]{2,1,0:T(8,128)(2,1)S(1)}, u32[]{:S(2)}, u32[]{:S(2)}) collective-permute-start(bf16[3,128,128]{2,1,0:T(8,128)(2,1)S(1)} %get-tuple-element.31), channel_id=1, source_target_pairs={{0,2},{1,3},{2,0},{3,1},{4,6},{5,7},{6,4},{7,5},{8,10},{9,11},{10,... | collective-permute-start | bytes 294920 | tf_op jit(solution)/shard_map/ppermute | solution.py:90
  38.2 3.7 %collective-permute-done.11.rest_2_ = bf16[3,128,128]{2,1,0:T(8,128)(2,1)S(1)} collective-permute-done((bf16[3,128,128]{2,1,0:T(8,128)(2,1)S(1)}, bf16[3,128,128]{2,1,0:T(8,128)(2,1)S(1)}, u32[]{:S(2)}, u32[]{:S(2)}) %collective-permute-start.11) | collective-permute-done | bytes 98336 | tf_op jit(solution)/shard_map/ppermute | solution.py:90
  41.9 1.4 %collective-permute-done.12.rest_3_ = bf16[3,128,128]{2,1,0:T(8,128)(2,1)S(1)} collective-permute-done((bf16[3,128,128]{2,1,0:T(8,128)(2,1)S(1)}, bf16[3,128,128]{2,1,0:T(8,128)(2,1)S(1)}, u32[]{:S(2)}, u32[]{:S(2)}) %collective-permute-start.12) | collective-permute-done | bytes 98336 | tf_op jit(solution)/shard_map/ppermute | solution.py:90
  43.3 0.9 %sum.1 = f32[768,128]{1,0:T(8,128)} custom-call(s32[1,128]{1,0:T(1,128)S(1)} %get-tuple-element.18.row_ref, bf16[3,128,128]{2,1,0:T(8,128)(2,1)S(1)} %get-tuple-element.29.rest_0_, bf16[3,128,128]{2,1,0:T(8,128)(2,1)S(1)} %collective-permute-done.10.rest_1_, bf16[3,128,128]{2,1,0:T(8,128)(2,1)S(1)} %collective-permute-done.11.rest_2_, ...), custom_call_target="tpu_custom_call" | custom-call | tf_op jit(solution)/shard_map/sum/pallas_call | solution.py:418
  (18 shorter events, 0.2 us)
Async XLA Ops:
  0.6 14.1 %collective-permute-start = (bf16[4,128,128]{2,1,0:T(8,128)(2,1)}, bf16[4,128,128]{2,1,0:T(8,128)(2,1)S(1)}, u32[]{:S(2)}, u32[]{:S(2)}) collective-permute-start(bf16[4,128,128]{2,1,0:T(8,128)(2,1)} %bitcast.22), channel_id=1, source_target_pairs={{0,4},{4,0},{8,12},{12,8},{16,20},{20,16},{24,28},{28,24},{1,5},{5... | collective-permute-start | bytes 393224 | tf_op jit(solution)/shard_map/ppermute | solution.py:63
  3.7 12.8 %collective-permute-start.1 = (bf16[4,128,128]{2,1,0:T(8,128)(2,1)}, bf16[4,128,128]{2,1,0:T(8,128)(2,1)S(1)}, u32[]{:S(2)}, u32[]{:S(2)}) collective-permute-start(bf16[4,128,128]{2,1,0:T(8,128)(2,1)} %bitcast.23), channel_id=1, source_target_pairs={{0,8},{4,12},{8,0},{12,4},{16,24},{20,28},{24,16},{28,20},{1,9},{5... | collective-permute-start | bytes 393224 | tf_op jit(solution)/shard_map/ppermute | solution.py:63
  5.3 8.7 %collective-permute-start.3 = (bf16[4,128,128]{2,1,0:T(8,128)(2,1)}, bf16[4,128,128]{2,1,0:T(8,128)(2,1)S(1)}, u32[]{:S(2)}, u32[]{:S(2)}) collective-permute-start(bf16[4,128,128]{2,1,0:T(8,128)(2,1)} %bitcast.24), channel_id=1, source_target_pairs={{0,16},{4,20},{8,24},{12,28},{16,0},{20,4},{24,8},{28,12},{1,17},{... | collective-permute-start | bytes 393224 | tf_op jit(solution)/shard_map/ppermute | solution.py:63
  13.9 7.1 %collective-permute-start.4 = (bf16[4,128,128]{2,1,0:T(8,128)(2,1)S(1)}, bf16[4,128,128]{2,1,0:T(8,128)(2,1)S(1)}, u32[]{:S(2)}, u32[]{:S(2)}) collective-permute-start(bf16[4,128,128]{2,1,0:T(8,128)(2,1)S(1)} %collective-permute-done.3), channel_id=1, source_target_pairs={{0,4},{4,0},{8,12},{12,8},{16,20},{20,16},{24,28},{28,24},{1,5},{5... | collective-permute-start | bytes 393224 | tf_op jit(solution)/shard_map/ppermute | solution.py:63
  14.4 5.0 %collective-permute-start.5 = (bf16[4,128,128]{2,1,0:T(8,128)(2,1)S(1)}, bf16[4,128,128]{2,1,0:T(8,128)(2,1)S(1)}, u32[]{:S(2)}, u32[]{:S(2)}) collective-permute-start(bf16[4,128,128]{2,1,0:T(8,128)(2,1)S(1)} %collective-permute-done.3), channel_id=1, source_target_pairs={{0,8},{4,12},{8,0},{12,4},{16,24},{20,28},{24,16},{28,20},{1,9},{5... | collective-permute-start | bytes 393224 | tf_op jit(solution)/shard_map/ppermute | solution.py:63
  14.8 6.2 %collective-permute-start.2 = (bf16[4,128,128]{2,1,0:T(8,128)(2,1)S(1)}, bf16[4,128,128]{2,1,0:T(8,128)(2,1)S(1)}, u32[]{:S(2)}, u32[]{:S(2)}) collective-permute-start(bf16[4,128,128]{2,1,0:T(8,128)(2,1)S(1)} %collective-permute-done), channel_id=1, source_target_pairs={{0,8},{4,12},{8,0},{12,4},{16,24},{20,28},{24,16},{28,20},{1,9},{5... | collective-permute-start | bytes 393224 | tf_op jit(solution)/shard_map/ppermute | solution.py:63
  19.4 5.0 %collective-permute-start.6 = (bf16[4,128,128]{2,1,0:T(8,128)(2,1)S(1)}, bf16[4,128,128]{2,1,0:T(8,128)(2,1)S(1)}, u32[]{:S(2)}, u32[]{:S(2)}) collective-permute-start(bf16[4,128,128]{2,1,0:T(8,128)(2,1)S(1)} %collective-permute-done.5), channel_id=1, source_target_pairs={{0,4},{4,0},{8,12},{12,8},{16,20},{20,16},{24,28},{28,24},{1,5},{5... | collective-permute-start | bytes 393224 | tf_op jit(solution)/shard_map/ppermute | solution.py:63
  24.4 4.8 %copy-start = (bf16[1,1,8,128,1024]{4,3,2,1,0:T(8,128)(2,1)S(1)}, bf16[1,1,8,128,1024]{4,3,2,1,0:T(8,128)(2,1)}, u32[]{:S(2)}) copy-start(bf16[1,1,8,128,1024]{4,3,2,1,0:T(8,128)(2,1)} %param.11) | copy-start | bytes 6291460
  27.2 1.9 %collective-permute-start.7 = (bf16[3,128,128]{2,1,0:T(8,128)(2,1)S(1)}, bf16[3,128,128]{2,1,0:T(8,128)(2,1)S(1)}, u32[]{:S(2)}, u32[]{:S(2)}) collective-permute-start(bf16[3,128,128]{2,1,0:T(8,128)(2,1)S(1)} %get-tuple-element.22), channel_id=1, source_target_pairs={{0,1},{1,0},{2,3},{3,2},{4,5},{5,4},{6,7},{7,6},{8,9},{9,8},{10,11... | collective-permute-start | bytes 294920 | tf_op jit(solution)/shard_map/ppermute | solution.py:90
  27.3 5.7 %collective-permute-start.8 = (bf16[3,128,128]{2,1,0:T(8,128)(2,1)S(1)}, bf16[3,128,128]{2,1,0:T(8,128)(2,1)S(1)}, u32[]{:S(2)}, u32[]{:S(2)}) collective-permute-start(bf16[3,128,128]{2,1,0:T(8,128)(2,1)S(1)} %get-tuple-element.25), channel_id=1, source_target_pairs={{0,2},{1,3},{2,0},{3,1},{4,6},{5,7},{6,4},{7,5},{8,10},{9,11},{10,... | collective-permute-start | bytes 294920 | tf_op jit(solution)/shard_map/ppermute | solution.py:90
  28.9 5.2 %collective-permute-start.9 = (bf16[3,128,128]{2,1,0:T(8,128)(2,1)S(1)}, bf16[3,128,128]{2,1,0:T(8,128)(2,1)S(1)}, u32[]{:S(2)}, u32[]{:S(2)}) collective-permute-start(bf16[3,128,128]{2,1,0:T(8,128)(2,1)S(1)} %get-tuple-element.26), channel_id=1, source_target_pairs={{0,3},{1,2},{2,1},{3,0},{4,7},{5,6},{6,5},{7,4},{8,11},{9,10},{10,... | collective-permute-start | bytes 294920 | tf_op jit(solution)/shard_map/ppermute | solution.py:90
  29.2 4.9 %copy-start.1 = (f32[1,1,1024]{2,1,0:T(1,128)S(1)}, f32[1,1,1024]{2,1,0:T(1,128)}, u32[]{:S(2)}) copy-start(f32[1,1,1024]{2,1,0:T(1,128)} %param.13) | copy-start | bytes 12292
  29.2 4.9 %copy-start.2 = (f32[1,1,1024]{2,1,0:T(1,128)S(1)}, f32[1,1,1024]{2,1,0:T(1,128)}, u32[]{:S(2)}) copy-start(f32[1,1,1024]{2,1,0:T(1,128)} %param.12) | copy-start | bytes 12292
  36.3 1.9 %collective-permute-start.10 = (bf16[3,128,128]{2,1,0:T(8,128)(2,1)S(1)}, bf16[3,128,128]{2,1,0:T(8,128)(2,1)S(1)}, u32[]{:S(2)}, u32[]{:S(2)}) collective-permute-start(bf16[3,128,128]{2,1,0:T(8,128)(2,1)S(1)} %get-tuple-element.30), channel_id=1, source_target_pairs={{0,1},{1,0},{2,3},{3,2},{4,5},{5,4},{6,7},{7,6},{8,9},{9,8},{10,11... | collective-permute-start | bytes 294920 | tf_op jit(solution)/shard_map/ppermute | solution.py:90
  36.7 5.2 %collective-permute-start.11 = (bf16[3,128,128]{2,1,0:T(8,128)(2,1)S(1)}, bf16[3,128,128]{2,1,0:T(8,128)(2,1)S(1)}, u32[]{:S(2)}, u32[]{:S(2)}) collective-permute-start(bf16[3,128,128]{2,1,0:T(8,128)(2,1)S(1)} %get-tuple-element.31), channel_id=1, source_target_pairs={{0,2},{1,3},{2,0},{3,1},{4,6},{5,7},{6,4},{7,5},{8,10},{9,11},{10,... | collective-permute-start | bytes 294920 | tf_op jit(solution)/shard_map/ppermute | solution.py:90
  38.2 5.1 %collective-permute-start.12 = (bf16[3,128,128]{2,1,0:T(8,128)(2,1)S(1)}, bf16[3,128,128]{2,1,0:T(8,128)(2,1)S(1)}, u32[]{:S(2)}, u32[]{:S(2)}) collective-permute-start(bf16[3,128,128]{2,1,0:T(8,128)(2,1)S(1)} %get-tuple-element.32), channel_id=1, source_target_pairs={{0,3},{1,2},{2,1},{3,0},{4,7},{5,6},{6,5},{7,4},{8,11},{9,10},{10,... | collective-permute-start | bytes 294920 | tf_op jit(solution)/shard_map/ppermute | solution.py:90
